TPU v7x, 128 devices: a whole 4x4x4 slice. The times are simulated.
128 devices in a mesh: groups: 4 (over x), shard: 32 (over y, z, core).
Axes of the slice: x: 4, y: 4, z: 4, core: 2. Of those that a mesh axis runs over, the one named last changes fastest.
Arguments:
- gradients: bfloat16 [4, 96, 1024, 1024], P('groups', None, 'shard'), may hold values from -200 to 200
- second_moment: bfloat16 [96, 1024, 1024], P('groups', 'shard'), may hold values from 0.25 to 4
- inverse_roots: bfloat16 [4, 32, 2, 2, 1024, 1024], P('groups', 'shard'), may hold values from -2 to 2
- owners: int32 [96], replicated, may hold values from 0 to 31, as said below
- weights: bfloat16 [96, 1024, 1024], P('groups', 'shard'), may hold values from -4 to 4
Outputs:
- new_weights: bfloat16 [96, 1024, 1024], P(None, 'shard')
Inputs may be any that keep to these rules, and one draw needn't show every extreme that they name: `owners`: blocks 24 * g to 24 * (g + 1) - 1 form group g. Within a group no owner is named by more than 2 blocks, and some owner is named by exactly 2.
All inputs are finite; a program needn't handle non-finite values.
Results may differ from a plain program's by a relative error of at most 0.0004.
The roundings to bfloat16 on the way count: a program that leaves them out, or rounds other values in their place, can miss the bound.
Values may be sent and summed in bfloat16 or wider, within the bound.
No kernel may reach another device: no remote copies, remote signals or barrier semaphores. Data moves between devices by JAX's collectives and lax.ppermute only.
A program may use at most 128 MiB of HBM per device.

v0:
```python
import functools

import jax
import jax.numpy as jnp
from jax import lax
from jax.experimental import pallas as pl
from jax.experimental.pallas import tpu as pltpu
from jax.sharding import PartitionSpec as P


LANES = 128
CHUNKS = 2
STEP = 8
TALL = 256
ANY = pl.BlockSpec(memory_space=pl.ANY)
SMEM = pl.BlockSpec(memory_space=pltpu.SMEM)


def two_parts(values):
    high = values.astype(jnp.bfloat16)
    low = (values - high.astype(jnp.float32)).astype(jnp.bfloat16)
    return high, low


def dot(a, b):
    return jnp.dot(a, b, preferred_element_type=jnp.float32)


def sum_kernel(width, last, meta, own, one, two, three, old, *refs):
    before = refs[0] if last else None
    outs = refs[1 if last else 0 : -2]
    norms = None if last else outs[-1]
    outs = outs if last else outs[:-1]
    codes, sems = refs[-2:]
    step = pl.program_id(0)

    def block(b, _):
        total = (own[0, b].astype(jnp.float32) + one[b].astype(jnp.float32)) + (
            two[b].astype(jnp.float32) + three[b].astype(jnp.float32)
        )
        moment = 0.95 * old[b].astype(jnp.float32) + 0.05 * total * total
        adam = total / (jnp.sqrt(moment) + 1e-08)
        adam = adam * adam
        parts = [total[:, j : j + LANES] for j in range(0, width, LANES)]
        top = functools.reduce(jnp.maximum, [jnp.abs(p) for p in parts])
        power = jnp.ceil(jnp.log2(jnp.maximum(top, 1e-30))) - 15.0
        grow = jnp.exp2(-power)
        at = step * STEP + b
        for j, p in enumerate(parts):
            code = jnp.clip(jnp.round(p * grow), -32767.0, 32767.0)
            codes[at, :, j * LANES : (j + 1) * LANES] = code.astype(jnp.int32).astype(jnp.int16)
        codes[at, :, width : width + LANES] = power.astype(jnp.int32).astype(jnp.int16)
        squares = functools.reduce(jnp.add, [adam[:, j : j + LANES] for j in range(0, width, LANES)])
        squares = jnp.sum(squares, axis=0, keepdims=True)
        if not last:
            norms[at] = squares
            return 0
        squares = squares + before[at]
        power = jnp.ceil(jnp.log2(jnp.maximum(squares, 1e-30)))
        scaled = squares * jnp.exp2(14.0 - power)
        high = jnp.floor(scaled)
        low = jnp.floor((scaled - high) * 16384.0)
        row = lax.broadcasted_iota(jnp.int32, (codes.shape[1], LANES), 0)
        full = jnp.where(row == 0, power, jnp.where(row == 1, high, low))
        codes[at, :, width + LANES :] = full.astype(jnp.int32).astype(jnp.int16)
        return 0

    lax.fori_loop(0, STEP, block, 0)

    @pl.when(step == pl.num_programs(0) - 1)
    def _():
        copies = []
        for out in outs:
            for n in range(out.shape[0]):
                k = len(copies)
                copies.append(pltpu.make_async_copy(codes.at[meta[1 + k]], out.at[n], sems.at[k]))
        for c in copies:
            c.start()
        for c in copies:
            c.wait()


def sum_replicas(gradients, received, old, chunk, group, sources, before=None):
    nbg, per, width = received[0].shape
    steps = nbg // STEP
    last = before is not None
    columns = width + (2 if last else 1) * LANES
    count = sum(x.shape[0] for x in sources)
    part = pl.BlockSpec((STEP, per, width), lambda i, meta: (i, 0, 0))
    whole = pl.BlockSpec((nbg, 1, LANES), lambda i, meta: (0, 0, 0))
    shapes = [jax.ShapeDtypeStruct((x.shape[0], per, columns), jnp.int16) for x in sources]
    if not last:
        shapes.append(jax.ShapeDtypeStruct((nbg, 1, LANES), jnp.float32))
    return pl.pallas_call(
        functools.partial(sum_kernel, width, last),
        out_shape=shapes,
        grid_spec=pltpu.PrefetchScalarGridSpec(
            num_scalar_prefetch=1,
            grid=(steps,),
            in_specs=[
                pl.BlockSpec((1, STEP, per, width), lambda i, meta: (0, meta[0] * steps + i, chunk, 0)),
                part,
                part,
                part,
                pl.BlockSpec((STEP, per, width), lambda i, meta: (i, chunk, 0)),
            ]
            + ([whole] if last else []),
            out_specs=[ANY] * len(sources) + ([] if last else [whole]),
            scratch_shapes=[
                pltpu.VMEM((nbg, per, columns), jnp.int16),
                pltpu.SemaphoreType.DMA((count,)),
            ],
        ),
    )(
        jnp.concatenate([group[None].astype(jnp.int32), *sources]),
        gradients,
        *received,
        old,
        *([before] if last else []),
    )


def owner_kernel(width, roots, *refs):
    arrived, update, high, low, pre = refs[:-4], refs[-4], refs[-3], refs[-2], refs[-1]
    n_src = arrived[0].shape[0]
    per = arrived[0].shape[-2]
    rows = per * len(arrived)

    def unpack(n, graft):
        for c, code in enumerate(arrived):
            at = pl.ds(pl.multiple_of(n * rows + c * per, per), per)
            got = code[n, 0] if len(code.shape) == 4 else code[n]
            step = jnp.exp2(got[:, width : width + LANES].astype(jnp.int32).astype(jnp.float32))
            for j in range(0, width, LANES):
                value = got[:, j : j + LANES].astype(jnp.int32).astype(jnp.float32) * step
                high[at, j : j + LANES], low[at, j : j + LANES] = two_parts(value)
        norm = got[:, width + LANES :].astype(jnp.int32).astype(jnp.float32)
        return graft + jnp.exp2(norm[0:1] - 14.0) * (norm[1:2] + norm[2:3] * (1.0 / 16384.0))

    graft = lax.fori_loop(0, n_src, unpack, jnp.zeros((1, LANES), jnp.float32))
    graft = jnp.sum(graft, axis=1, keepdims=True)
    right = roots[0, 0, 0, 1]
    for m in range(0, width, TALL):
        at = pl.ds(m, TALL)
        high[at, :], low[at, :] = two_parts(dot(high[at, :], right) + dot(low[at, :], right))
    square = jnp.zeros((1, width), jnp.float32)
    for m in range(0, width, TALL):
        at = pl.ds(m, TALL)
        left = roots[0, 0, 0, 0, at, :]
        got = dot(left, high[...]) + dot(left, low[...])
        pre[at, :] = got
        square = square + jnp.sum(got * got, axis=0, keepdims=True)
    square = jnp.sum(square, axis=1, keepdims=True)
    scale = jnp.sqrt(graft) / jnp.sqrt(square + 1e-06)
    for m in range(0, width, TALL):
        at = pl.ds(m, TALL)
        update[at, :] = (scale * pre[at, :]).astype(jnp.bfloat16)


def owner_work(roots, arrived, slot):
    width = roots.shape[-1]
    specs = []
    for a in arrived:
        if a.ndim == 4:
            specs.append(pl.BlockSpec((a.shape[0], 1) + a.shape[2:], lambda i: (0, slot, 0, 0)))
        else:
            specs.append(pl.BlockSpec(a.shape, lambda i: (0, 0, 0)))
    return pl.pallas_call(
        functools.partial(owner_kernel, width),
        out_shape=jax.ShapeDtypeStruct((width, width), jnp.bfloat16),
        grid=(1,),
        in_specs=[pl.BlockSpec((1, 1, 1, 2, width, width), lambda i: (0, 0, slot, 0, 0, 0))] + specs,
        out_specs=pl.BlockSpec((width, width), lambda i: (0, 0)),
        scratch_shapes=[
            pltpu.VMEM((width, width), jnp.bfloat16),
            pltpu.VMEM((width, width), jnp.bfloat16),
            pltpu.VMEM((width, width), jnp.float32),
        ],
    )(roots, *arrived)


def renew_kernel(count, table, weights, *refs):
    backs, outs, held, grads, sems = refs[:-5], refs[-5:-3], refs[-3], refs[-2], refs[-1]

    def fetch(j):
        return pltpu.make_async_copy(weights.at[table[j]], held.at[j], sems.at[0, j])

    def pull(j, k):
        return pltpu.make_async_copy(backs[k].at[table[count + j]], grads.at[j], sems.at[1, j])

    for j in range(count):
        fetch(j).start()
        if len(backs) == 1:
            pull(j, 0).start()
        else:
            for k in range(len(backs)):

                @pl.when(table[2 * count + j] == k)
                def _():
                    pull(j, k).start()

    half = count // 2
    for j in range(count):
        fetch(j).wait()
        pull(j, 0).wait()
        stepped = held[j].astype(jnp.float32) - 0.5 * grads[j].astype(jnp.float32)
        scale = lax.rsqrt(jnp.mean(stepped * stepped, axis=1, keepdims=True) + 1e-06)
        outs[j // half][j % half] = (stepped * scale).astype(jnp.bfloat16)


def renew(table, weights, backs):
    count = table.shape[0] // 3
    rows, width = weights.shape[1:]
    half = jax.ShapeDtypeStruct((count // 2, rows, width), jnp.bfloat16)
    return pl.pallas_call(
        functools.partial(renew_kernel, count),
        out_shape=(half, half),
        in_specs=[SMEM] + [ANY] * (1 + len(backs)),
        scratch_shapes=[
            pltpu.VMEM((count, rows, width), jnp.bfloat16),
            pltpu.VMEM((count, rows, width), jnp.bfloat16),
            pltpu.SemaphoreType.DMA((2, count)),
        ],
    )(table, weights, *backs)


def pass_kernel(table, *refs):
    for j in range(table.shape[0]):
        refs[-1][j] = table[j]


def pass_table(table, *after):
    return pl.pallas_call(
        pass_kernel,
        out_shape=jax.ShapeDtypeStruct(table.shape, table.dtype),
        in_specs=[SMEM] + [ANY] * len(after),
        out_specs=SMEM,
    )(table, *after)


def scatter_kernel(place, *refs):
    pieces, out, sems = refs[:-2], refs[-2], refs[-1]
    copies = []
    for piece in pieces:
        for j in range(piece.shape[0]):
            n = len(copies)
            copies.append(pltpu.make_async_copy(piece.at[j], out.at[place[n]], sems.at[n]))
    for c in copies:
        c.start()
    for c in copies:
        c.wait()


def scatter_more_kernel(place, base, *refs):
    del base
    scatter_kernel(place, *refs)


def scatter_blocks(place, pieces, out_shape, base=None):
    count = sum(p.shape[0] for p in pieces)
    operands = list(pieces) if base is None else [base] + list(pieces)
    return pl.pallas_call(
        scatter_kernel if base is None else scatter_more_kernel,
        out_shape=out_shape,
        in_specs=[SMEM] + [ANY] * (len(operands) - len(pieces)) + [pl.BlockSpec(memory_space=pltpu.VMEM)] * len(pieces),
        out_specs=ANY,
        scratch_shapes=[pltpu.SemaphoreType.DMA((count,))],
        input_output_aliases={} if base is None else {1: 0},
    )(place, *operands)


def body(gradients, second_moment, inverse_roots, owners, weights):
    groups = lax.axis_size("groups")
    shards = lax.axis_size("shard")
    g = lax.axis_index("groups")
    total_blocks = owners.shape[0]
    nbg = total_blocks // groups
    slots = inverse_roots.shape[2]
    rows = gradients.shape[2]
    width = gradients.shape[3]
    half = nbg // 2

    def shift(n):
        return [(i, (i + n) % groups) for i in range(groups)]

    per = rows // CHUNKS
    received = []
    grads = gradients
    for c in range(CHUNKS):
        pieces = [
            lax.dynamic_slice(grads[0], (nbg * ((g + n) % groups), c * per, 0), (nbg, per, width)) for n in (1, 3, 2)
        ]
        grads, pieces = lax.optimization_barrier((grads, pieces))
        received.append([lax.ppermute(p, "groups", shift(n)) for p, n in zip(pieces, (1, 3, 2))])

    grouped = owners.reshape(groups, nbg)
    same = grouped[:, :, None] == grouped[:, None, :]
    ids = jnp.arange(nbg, dtype=jnp.int32)
    earlier = ids[None, :] < ids[:, None]
    rank = jnp.sum((same & earlier[None]).astype(jnp.int32), axis=2)
    firsts = rank == 0
    before = jnp.sum((firsts[:, None, :] & earlier[None]).astype(jnp.int32), axis=2)
    n_first = jnp.sum(firsts.astype(jnp.int32), axis=1, keepdims=True)
    spot = jnp.where(firsts, before, n_first + ids[None] - before)
    sits = spot[:, None, :] == ids[None, :, None]
    order = jnp.sum(jnp.where(sits, ids[None, None, :], 0), axis=2)
    by_order = [
        lax.dynamic_index_in_dim(jnp.sum(jnp.where(sits, t[:, None, :], 0), axis=2), g, 0, False)
        for t in (jnp.broadcast_to(ids[None], grouped.shape), grouped, rank)
    ]
    my_owner = lax.dynamic_index_in_dim(grouped, g, 0, False)
    my_rank = lax.dynamic_index_in_dim(rank, g, 0, False)
    dest = jnp.arange(shards, dtype=jnp.int32)
    match = [(my_owner[None, :] == dest[:, None]) & (my_rank[None, :] == k) for k in range(slots)]
    source = [jnp.sum(jnp.where(m, ids[None], 0), axis=1) for m in match]

    def exchange(x, after=None):
        if after is not None:
            x, after = lax.optimization_barrier((x, after))
        return lax.all_to_all(x, "shard", 0, 0, tiled=True)

    code, norm = sum_replicas(gradients, received[0], second_moment, 0, g, [jnp.stack(source, 1).reshape(-1)])
    codes = sum_replicas(gradients, received[1], second_moment, 1, g, source, norm)
    first = exchange(code.reshape(shards, slots, per, width + LANES))
    arrived = []
    for k in range(slots):
        arrived.append([first, exchange(codes[k], arrived[-1][-1] if k else first)])

    backs = []
    for k in range(slots):
        update = owner_work(inverse_roots, arrived[k], k)
        backs.append(exchange(update.reshape(shards, rows, width), backs[-1] if k else None))

    def to_all(new):
        a, b = new
        prev_a = lax.ppermute(a, "groups", shift(1))
        after_b = lax.ppermute(b, "groups", shift(3))
        prev_b = lax.ppermute(b, "groups", shift(1))
        after_a = lax.ppermute(a, "groups", shift(3))
        far_a = lax.ppermute(prev_a, "groups", shift(1))
        far_b = lax.ppermute(after_b, "groups", shift(3))
        return [a, b, prev_a, prev_b, after_a, after_b, far_a, far_b]

    def places(lo, hi):
        out = []
        for n in (0, 3, 1, 2):
            h = (g + n) % groups
            out.append(nbg * h + lax.dynamic_index_in_dim(order, h, 0, False)[lo:hi])
        return jnp.concatenate(out)

    def table(lo, hi):
        return jnp.concatenate([t[lo:hi] for t in by_order])

    out_shape = jax.ShapeDtypeStruct((total_blocks, rows, width), jnp.bfloat16)
    new = renew(table(0, half), weights, backs[:1])
    pieces0 = to_all(new)
    late = pass_table(table(half, nbg), pieces0[2], pieces0[5])
    new = renew(late, weights, backs)
    pieces1 = to_all(new)
    out = scatter_blocks(places(0, half), pieces0, out_shape)
    return scatter_blocks(places(half, nbg), pieces1, out_shape, base=out)


def solution(mesh):
    return jax.shard_map(
        body,
        mesh=mesh,
        in_specs=(
            P("groups", None, "shard", None),
            P("groups", "shard", None),
            P("groups", "shard", None, None, None, None),
            P(),
            P("groups", "shard", None),
        ),
        out_specs=P(None, "shard", None),
        check_vma=False,
    )
```

profile of v0, /device:TPU:1, one launch (start us, length us, event | category | flops | bytes accessed | tf_op | source)
XLA Modules:
  0.0 271.1 jit_solution(5037744018041775568)
XLA Ops:
  0.0 3.1 %dynamic-slice_bitcast_fusion.3 = (bf16[24,16,1024]{2,1,0:T(8,128)(2,1)S(1)}, bf16[24,16,1024]{2,1,0:T(8,128)(2,1)}, bf16[24,16,1024]{2,1,0:T(8,128)(2,1)}) fusion(bf16[1,96,32,1024]{3,2,1,0:T(8,128)(2,1)} %own.3, s32[]{:T(128)S(6)} %select_n.119, s32[]{:T(128)S(6)} %select_n.118, s32[]{:T(128)S(6)} %select_n.117), kind=kLoop, calls=%fused_computation.3 | loop fusion | bytes 4718604 | tf_op jit(solution)/shard_map/dynamic_slice | solution.py:291
  3.1 2.0 collective-permute-start
  9.4 14.1 %collective-permute-done.one = bf16[24,16,1024]{2,1,0:T(8,128)(2,1)S(1)} collective-permute-done((bf16[24,16,1024]{2,1,0:T(8,128)(2,1)}, bf16[24,16,1024]{2,1,0:T(8,128)(2,1)S(1)}, u32[]{:S(2)}, u32[]{:S(2)}) %collective-permute-start) | collective-permute-done | bytes 786464 | tf_op jit(solution)/shard_map/ppermute | solution.py:294
  23.5 18.1 %collective-permute-done.2.three = bf16[24,16,1024]{2,1,0:T(8,128)(2,1)S(1)} collective-permute-done((bf16[24,16,1024]{2,1,0:T(8,128)(2,1)S(1)}, bf16[24,16,1024]{2,1,0:T(8,128)(2,1)S(1)}, u32[]{:S(2)}, u32[]{:S(2)}) %collective-permute-start.2) | collective-permute-done | bytes 786464 | tf_op jit(solution)/shard_map/ppermute | solution.py:294
  42.5 7.0 %shard_map.55 = (s16[64,16,1152]{2,1,0:T(8,128)(2,1)}, f32[24,1,128]{2,1,0:T(1,128)}) custom-call(s32[65]{0:T(128)} %pad_add_fusion.4.meta, bf16[1,96,32,1024]{3,2,1,0:T(8,128)(2,1)} %own.3, bf16[24,16,1024]{2,1,0:T(8,128)(2,1)} %copy-done.5, bf16[24,16,1024]{2,1,0:T(8,128)(2,1)} %copy-done.6, bf16[24,16,1024]{2,1,0:T(8,128)(2,1)} %copy-done.7, ...), custom_call_target="tpu_custom_call" | custom-call | tf_op jit(solution)/shard_map/pallas_call | solution.py:94
  49.5 9.6 %all-to-all-start = ((s16[32,2,16,1152]{3,2,1,0:T(8,128)(2,1)}), s16[32,2,16,1152]{3,2,1,0:T(8,128)(2,1)S(1)}, u32[]{:S(2)}, u32[]{:S(2)}) async-start(s16[32,2,16,1152]{3,2,1,0:T(8,128)(2,1)} %bitcast.54), calls=%async_computation | async-start | bytes 4718592 | tf_op jit(solution)/shard_map/all_to_all | solution.py:320
  59.2 1.8 dynamic-slice_bitcast_fusion
  61.9 1.8 collective-permute-start.4
  65.4 15.7 %collective-permute-done.3.one = bf16[24,16,1024]{2,1,0:T(8,128)(2,1)S(1)} collective-permute-done((bf16[24,16,1024]{2,1,0:T(8,128)(2,1)S(1)}, bf16[24,16,1024]{2,1,0:T(8,128)(2,1)S(1)}, u32[]{:S(2)}, u32[]{:S(2)}) %collective-permute-start.3) | collective-permute-done | bytes 786464 | tf_op jit(solution)/shard_map/ppermute | solution.py:294
  81.2 17.9 %collective-permute-done.5.three = bf16[24,16,1024]{2,1,0:T(8,128)(2,1)S(1)} collective-permute-done((bf16[24,16,1024]{2,1,0:T(8,128)(2,1)S(1)}, bf16[24,16,1024]{2,1,0:T(8,128)(2,1)S(1)}, u32[]{:S(2)}, u32[]{:S(2)}) %collective-permute-start.5) | collective-permute-done | bytes 786464 | tf_op jit(solution)/shard_map/ppermute | solution.py:294
  100.0 6.8 %shard_map.56 = (s16[32,16,1280]{2,1,0:T(8,128)(2,1)}, s16[32,16,1280]{2,1,0:T(8,128)(2,1)}) custom-call(s32[65]{0:T(128)} %pad_add_fusion.5.meta, bf16[1,96,32,1024]{3,2,1,0:T(8,128)(2,1)} %own.3, bf16[24,16,1024]{2,1,0:T(8,128)(2,1)} %copy-done.8, bf16[24,16,1024]{2,1,0:T(8,128)(2,1)} %copy-done.9, bf16[24,16,1024]{2,1,0:T(8,128)(2,1)} %copy-done.10, ...), custom_call_target="tpu_custom_call" | custom-call | tf_op jit(solution)/shard_map/pallas_call | solution.py:94
  106.9 28.4 %all_to_all.25.refs_1_ = s16[32,16,1280]{2,1,0:T(8,128)(2,1)} all-to-all(s16[32,16,1280]{2,1,0:T(8,128)(2,1)} %get-tuple-element.33), channel_id=1, replica_groups=mesh['groups'=4,'shard'=32] {'shard'}, dimensions={0} | all-to-all | bytes 2621440 | tf_op jit(solution)/shard_map/all_to_all | solution.py:320
  135.3 4.6 %all-to-all-start.3 = ((s16[32,16,1280]{2,1,0:T(8,128)(2,1)}), s16[32,16,1280]{2,1,0:T(8,128)(2,1)}, u32[]{:S(2)}, u32[]{:S(2)}) async-start(s16[32,16,1280]{2,1,0:T(8,128)(2,1)} %get-tuple-element.37), calls=%async_computation.3 | async-start | bytes 2621440 | tf_op jit(solution)/shard_map/all_to_all | solution.py:320
  139.9 15.3 %shard_map.57 = bf16[1024,1024]{1,0:T(8,128)(2,1)} custom-call(bf16[1,1,2,2,1024,1024]{5,4,3,2,1,0:T(8,128)(2,1)} %roots.3, s16[32,2,16,1152]{3,2,1,0:T(8,128)(2,1)} %copy-done, s16[32,16,1280]{2,1,0:T(8,128)(2,1)} %all_to_all.25.refs_1_), custom_call_target="tpu_custom_call" | custom-call | tf_op jit(solution)/shard_map/pallas_call | solution.py:168
  155.2 4.5 %all-to-all-done.3.refs_1_ = s16[32,16,1280]{2,1,0:T(8,128)(2,1)} async-done(((s16[32,16,1280]{2,1,0:T(8,128)(2,1)}), s16[32,16,1280]{2,1,0:T(8,128)(2,1)}, u32[]{:S(2)}, u32[]{:S(2)}) %all-to-all-start.3) | async-done | bytes 1310752 | tf_op jit(solution)/shard_map/all_to_all | solution.py:320
  159.7 4.0 %all-to-all-start.2 = ((bf16[32,32,1024]{2,1,0:T(8,128)(2,1)}), bf16[32,32,1024]{2,1,0:T(8,128)(2,1)S(1)}, u32[]{:S(2)}, u32[]{:S(2)}) async-start(bf16[32,32,1024]{2,1,0:T(8,128)(2,1)} %bitcast.53), calls=%async_computation.2 | async-start | bytes 4194304 | tf_op jit(solution)/shard_map/all_to_all | solution.py:320
  163.8 15.2 %shard_map.61 = bf16[1024,1024]{1,0:T(8,128)(2,1)} custom-call(bf16[1,1,2,2,1024,1024]{5,4,3,2,1,0:T(8,128)(2,1)} %roots.3, s16[32,2,16,1152]{3,2,1,0:T(8,128)(2,1)} %copy-done, s16[32,16,1280]{2,1,0:T(8,128)(2,1)} %all-to-all-done.3.refs_1_), custom_call_target="tpu_custom_call" | custom-call | tf_op jit(solution)/shard_map/pallas_call | solution.py:168
  179.0 13.0 %all-to-all-done.2.refs_0_ = bf16[32,32,1024]{2,1,0:T(8,128)(2,1)S(1)} async-done(((bf16[32,32,1024]{2,1,0:T(8,128)(2,1)}), bf16[32,32,1024]{2,1,0:T(8,128)(2,1)S(1)}, u32[]{:S(2)}, u32[]{:S(2)}) %all-to-all-start.2) | async-done | bytes 2097184 | tf_op jit(solution)/shard_map/all_to_all | solution.py:320
  193.3 5.2 %all-to-all-start.4 = ((bf16[32,32,1024]{2,1,0:T(8,128)(2,1)}), bf16[32,32,1024]{2,1,0:T(8,128)(2,1)}, u32[]{:S(2)}, u32[]{:S(2)}) async-start(bf16[32,32,1024]{2,1,0:T(8,128)(2,1)} %bitcast.52), calls=%async_computation.4 | async-start | bytes 4194304 | tf_op jit(solution)/shard_map/all_to_all | solution.py:320
  200.0 4.0 %shard_map.58 = (bf16[6,32,1024]{2,1,0:T(8,128)(2,1)}, bf16[6,32,1024]{2,1,0:T(8,128)(2,1)}) custom-call(s32[36]{0:T(128)} %pad_add_fusion.3.table, bf16[24,32,1024]{2,1,0:T(8,128)(2,1)} %weights.3, bf16[32,32,1024]{2,1,0:T(8,128)(2,1)} %copy-done.1), custom_call_target="tpu_custom_call" | custom-call | tf_op jit(solution)/shard_map/pallas_call | solution.py:215
  204.9 1.8 collective-permute-start.9
  208.8 7.0 %collective-permute-done.6.refs_2_.refs_0_ = bf16[6,32,1024]{2,1,0:T(8,128)(2,1)S(1)} collective-permute-done((bf16[6,32,1024]{2,1,0:T(8,128)(2,1)}, bf16[6,32,1024]{2,1,0:T(8,128)(2,1)S(1)}, u32[]{:S(2)}, u32[]{:S(2)}) %collective-permute-start.6) | collective-permute-done | bytes 393248 | tf_op jit(solution)/shard_map/ppermute | solution.py:336
  218.5 8.4 %all-to-all-done.4.refs_1_ = bf16[32,32,1024]{2,1,0:T(8,128)(2,1)} async-done(((bf16[32,32,1024]{2,1,0:T(8,128)(2,1)}), bf16[32,32,1024]{2,1,0:T(8,128)(2,1)}, u32[]{:S(2)}, u32[]{:S(2)}) %all-to-all-start.4) | async-done | bytes 2097184 | tf_op jit(solution)/shard_map/all_to_all | solution.py:320
  227.0 4.0 %shard_map.62 = (bf16[6,32,1024]{2,1,0:T(8,128)(2,1)}, bf16[6,32,1024]{2,1,0:T(8,128)(2,1)}) custom-call(s32[36]{0:T(128)} %shard_map.60.table, bf16[24,32,1024]{2,1,0:T(8,128)(2,1)} %weights.3, bf16[32,32,1024]{2,1,0:T(8,128)(2,1)} %copy-done.1, bf16[32,32,1024]{2,1,0:T(8,128)(2,1)} %all-to-all-done.4.refs_1_), custom_call_target="tpu_custom_call" | custom-call | tf_op jit(solution)/shard_map/pallas_call | solution.py:215
  231.9 2.0 collective-permute-start.15
  237.2 5.0 %collective-permute-done.12.refs_2_ = bf16[6,32,1024]{2,1,0:T(8,128)(2,1)S(1)} collective-permute-done((bf16[6,32,1024]{2,1,0:T(8,128)(2,1)}, bf16[6,32,1024]{2,1,0:T(8,128)(2,1)S(1)}, u32[]{:S(2)}, u32[]{:S(2)}) %collective-permute-start.12) | collective-permute-done | bytes 393248 | tf_op jit(solution)/shard_map/ppermute | solution.py:336
  242.3 2.7 collective-permute-start.17
  247.1 3.0 %collective-permute-done.11.refs_7_ = bf16[6,32,1024]{2,1,0:T(8,128)(2,1)S(1)} collective-permute-done((bf16[6,32,1024]{2,1,0:T(8,128)(2,1)S(1)}, bf16[6,32,1024]{2,1,0:T(8,128)(2,1)S(1)}, u32[]{:S(2)}, u32[]{:S(2)}) %collective-permute-start.11) | collective-permute-done | bytes 393248 | tf_op jit(solution)/shard_map/ppermute | solution.py:341
  250.8 3.9 %shard_map.59.base = bf16[96,32,1024]{2,1,0:T(8,128)(2,1)} custom-call(s32[48]{0:T(128)} %get-tuple-element.76.place, bf16[6,32,1024]{2,1,0:T(8,128)(2,1)} %get-tuple-element.34.refs_0_, bf16[6,32,1024]{2,1,0:T(8,128)(2,1)} %get-tuple-element.35.refs_1_, bf16[6,32,1024]{2,1,0:T(8,128)(2,1)} %copy-done.2, bf16[6,32,1024]{2,1,0:T(8,128)(2,1)} %copy-done.12, ...), custom_call_target="tpu_custom_call" | custom-call | tf_op jit(solution)/shard_map/pallas_call | solution.py:262
  254.7 3.9 %collective-permute-done.14.refs_4_ = bf16[6,32,1024]{2,1,0:T(8,128)(2,1)S(1)} collective-permute-done((bf16[6,32,1024]{2,1,0:T(8,128)(2,1)}, bf16[6,32,1024]{2,1,0:T(8,128)(2,1)S(1)}, u32[]{:S(2)}, u32[]{:S(2)}) %collective-permute-start.14) | collective-permute-done | bytes 393248 | tf_op jit(solution)/shard_map/ppermute | solution.py:339
  259.2 7.8 %collective-permute-done.17.refs_7_ = bf16[6,32,1024]{2,1,0:T(8,128)(2,1)} collective-permute-done((bf16[6,32,1024]{2,1,0:T(8,128)(2,1)S(1)}, bf16[6,32,1024]{2,1,0:T(8,128)(2,1)}, u32[]{:S(2)}, u32[]{:S(2)}) %collective-permute-start.17) | collective-permute-done | bytes 393248 | tf_op jit(solution)/shard_map/ppermute | solution.py:341
  267.1 3.9 %shard_map.63 = bf16[96,32,1024]{2,1,0:T(8,128)(2,1)} custom-call(s32[48]{0:T(128)} %get-tuple-element.75.place, bf16[96,32,1024]{2,1,0:T(8,128)(2,1)} %shard_map.59.base, bf16[6,32,1024]{2,1,0:T(8,128)(2,1)} %get-tuple-element.39.refs_0_, bf16[6,32,1024]{2,1,0:T(8,128)(2,1)} %get-tuple-element.40.refs_1_, ...), custom_call_target="tpu_custom_call", output_to_operand_aliasing={{}: (1, {})} | custom-call | tf_op jit(solution)/shard_map/pallas_call | solution.py:262
  (91 shorter events, 25.0 us)
Async XLA Ops:
  3.1 20.4 %collective-permute-start = (bf16[24,16,1024]{2,1,0:T(8,128)(2,1)}, bf16[24,16,1024]{2,1,0:T(8,128)(2,1)S(1)}, u32[]{:S(2)}, u32[]{:S(2)}) collective-permute-start(bf16[24,16,1024]{2,1,0:T(8,128)(2,1)} %get-tuple-element.23), channel_id=1, source_target_pairs={{0,32},{32,64},{64,96},{96,0},{1,33},{33,65},{65,97},{97,1},{2,34}... | collective-permute-start | bytes 2359304 | tf_op jit(solution)/shard_map/ppermute | solution.py:294
  5.1 18.4 %collective-permute-start.1 = (bf16[24,16,1024]{2,1,0:T(8,128)(2,1)}, bf16[24,16,1024]{2,1,0:T(8,128)(2,1)S(1)}, u32[]{:S(2)}, u32[]{:S(2)}) collective-permute-start(bf16[24,16,1024]{2,1,0:T(8,128)(2,1)} %get-tuple-element.24), channel_id=1, source_target_pairs={{0,96},{32,0},{64,32},{96,64},{1,97},{33,1},{65,33},{97,65},{2,98}... | collective-permute-start | bytes 2359304 | tf_op jit(solution)/shard_map/ppermute | solution.py:294
  6.4 35.2 %collective-permute-start.2 = (bf16[24,16,1024]{2,1,0:T(8,128)(2,1)S(1)}, bf16[24,16,1024]{2,1,0:T(8,128)(2,1)S(1)}, u32[]{:S(2)}, u32[]{:S(2)}) collective-permute-start(bf16[24,16,1024]{2,1,0:T(8,128)(2,1)S(1)} %get-tuple-element.25), channel_id=1, source_target_pairs={{0,64},{32,96},{64,0},{96,32},{1,65},{33,97},{65,1},{97,33},{2,66}... | collective-permute-start | bytes 2359304 | tf_op jit(solution)/shard_map/ppermute | solution.py:294
  23.5 18.1 %copy-start.5 = (bf16[24,16,1024]{2,1,0:T(8,128)(2,1)}, bf16[24,16,1024]{2,1,0:T(8,128)(2,1)S(1)}, u32[]{:S(2)}) copy-start(bf16[24,16,1024]{2,1,0:T(8,128)(2,1)S(1)} %collective-permute-done.one) | copy-start | bytes 2359300
  23.5 18.1 %copy-start.6 = (bf16[24,16,1024]{2,1,0:T(8,128)(2,1)}, bf16[24,16,1024]{2,1,0:T(8,128)(2,1)S(1)}, u32[]{:S(2)}) copy-start(bf16[24,16,1024]{2,1,0:T(8,128)(2,1)S(1)} %collective-permute-done.1.two) | copy-start | bytes 2359300
  49.5 57.3 %all-to-all-start = ((s16[32,2,16,1152]{3,2,1,0:T(8,128)(2,1)}), s16[32,2,16,1152]{3,2,1,0:T(8,128)(2,1)S(1)}, u32[]{:S(2)}, u32[]{:S(2)}) async-start(s16[32,2,16,1152]{3,2,1,0:T(8,128)(2,1)} %bitcast.54), calls=%async_computation | async-start | bytes 4718592 | tf_op jit(solution)/shard_map/all_to_all | solution.py:320
  61.0 20.1 %collective-permute-start.3 = (bf16[24,16,1024]{2,1,0:T(8,128)(2,1)S(1)}, bf16[24,16,1024]{2,1,0:T(8,128)(2,1)S(1)}, u32[]{:S(2)}, u32[]{:S(2)}) collective-permute-start(bf16[24,16,1024]{2,1,0:T(8,128)(2,1)S(1)} %get-tuple-element.28), channel_id=1, source_target_pairs={{0,32},{32,64},{64,96},{96,0},{1,33},{33,65},{65,97},{97,1},{2,34}... | collective-permute-start | bytes 2359304 | tf_op jit(solution)/shard_map/ppermute | solution.py:294
  61.9 19.2 %collective-permute-start.4 = (bf16[24,16,1024]{2,1,0:T(8,128)(2,1)S(1)}, bf16[24,16,1024]{2,1,0:T(8,128)(2,1)S(1)}, u32[]{:S(2)}, u32[]{:S(2)}) collective-permute-start(bf16[24,16,1024]{2,1,0:T(8,128)(2,1)S(1)} %get-tuple-element.29), channel_id=1, source_target_pairs={{0,96},{32,0},{64,32},{96,64},{1,97},{33,1},{65,33},{97,65},{2,98}... | collective-permute-start | bytes 2359304 | tf_op jit(solution)/shard_map/ppermute | solution.py:294
  63.7 35.3 %collective-permute-start.5 = (bf16[24,16,1024]{2,1,0:T(8,128)(2,1)S(1)}, bf16[24,16,1024]{2,1,0:T(8,128)(2,1)S(1)}, u32[]{:S(2)}, u32[]{:S(2)}) collective-permute-start(bf16[24,16,1024]{2,1,0:T(8,128)(2,1)S(1)} %get-tuple-element.30), channel_id=1, source_target_pairs={{0,64},{32,96},{64,0},{96,32},{1,65},{33,97},{65,1},{97,33},{2,66}... | collective-permute-start | bytes 2359304 | tf_op jit(solution)/shard_map/ppermute | solution.py:294
  81.1 18.9 %copy-start.8 = (bf16[24,16,1024]{2,1,0:T(8,128)(2,1)}, bf16[24,16,1024]{2,1,0:T(8,128)(2,1)S(1)}, u32[]{:S(2)}) copy-start(bf16[24,16,1024]{2,1,0:T(8,128)(2,1)S(1)} %collective-permute-done.3.one) | copy-start | bytes 2359300
  81.1 17.9 %copy-start.9 = (bf16[24,16,1024]{2,1,0:T(8,128)(2,1)}, bf16[24,16,1024]{2,1,0:T(8,128)(2,1)S(1)}, u32[]{:S(2)}) copy-start(bf16[24,16,1024]{2,1,0:T(8,128)(2,1)S(1)} %collective-permute-done.4.two) | copy-start | bytes 2359300
  106.9 28.4 %copy-start = (s16[32,2,16,1152]{3,2,1,0:T(8,128)(2,1)}, s16[32,2,16,1152]{3,2,1,0:T(8,128)(2,1)S(1)}, u32[]{:S(2)}) copy-start(s16[32,2,16,1152]{3,2,1,0:T(8,128)(2,1)S(1)} %all-to-all-done.refs_0_) | copy-start | bytes 7077892
  135.3 24.4 %all-to-all-start.3 = ((s16[32,16,1280]{2,1,0:T(8,128)(2,1)}), s16[32,16,1280]{2,1,0:T(8,128)(2,1)}, u32[]{:S(2)}, u32[]{:S(2)}) async-start(s16[32,16,1280]{2,1,0:T(8,128)(2,1)} %get-tuple-element.37), calls=%async_computation.3 | async-start | bytes 2621440 | tf_op jit(solution)/shard_map/all_to_all | solution.py:320
  159.7 32.3 %all-to-all-start.2 = ((bf16[32,32,1024]{2,1,0:T(8,128)(2,1)}), bf16[32,32,1024]{2,1,0:T(8,128)(2,1)S(1)}, u32[]{:S(2)}, u32[]{:S(2)}) async-start(bf16[32,32,1024]{2,1,0:T(8,128)(2,1)} %bitcast.53), calls=%async_computation.2 | async-start | bytes 4194304 | tf_op jit(solution)/shard_map/all_to_all | solution.py:320
  193.3 33.6 %all-to-all-start.4 = ((bf16[32,32,1024]{2,1,0:T(8,128)(2,1)}), bf16[32,32,1024]{2,1,0:T(8,128)(2,1)}, u32[]{:S(2)}, u32[]{:S(2)}) async-start(bf16[32,32,1024]{2,1,0:T(8,128)(2,1)} %bitcast.52), calls=%async_computation.4 | async-start | bytes 4194304 | tf_op jit(solution)/shard_map/all_to_all | solution.py:320
  204.0 11.8 %collective-permute-start.6 = (bf16[6,32,1024]{2,1,0:T(8,128)(2,1)}, bf16[6,32,1024]{2,1,0:T(8,128)(2,1)S(1)}, u32[]{:S(2)}, u32[]{:S(2)}) collective-permute-start(bf16[6,32,1024]{2,1,0:T(8,128)(2,1)} %get-tuple-element.34.refs_0_), channel_id=1, source_target_pairs={{0,32},{32,64},{64,96},{96,0},{1,33},{33,65},{65,97},{97,1},{2,34}... | collective-permute-start | bytes 1179656 | tf_op jit(solution)/shard_map/ppermute | solution.py:336
  204.9 10.9 %collective-permute-start.9 = (bf16[6,32,1024]{2,1,0:T(8,128)(2,1)}, bf16[6,32,1024]{2,1,0:T(8,128)(2,1)S(1)}, u32[]{:S(2)}, u32[]{:S(2)}) collective-permute-start(bf16[6,32,1024]{2,1,0:T(8,128)(2,1)} %get-tuple-element.35.refs_1_), channel_id=1, source_target_pairs={{0,96},{32,0},{64,32},{96,64},{1,97},{33,1},{65,33},{97,65},{2,98}... | collective-permute-start | bytes 1179656 | tf_op jit(solution)/shard_map/ppermute | solution.py:337
  207.4 27.2 %collective-permute-start.8 = (bf16[6,32,1024]{2,1,0:T(8,128)(2,1)}, bf16[6,32,1024]{2,1,0:T(8,128)(2,1)S(1)}, u32[]{:S(2)}, u32[]{:S(2)}) collective-permute-start(bf16[6,32,1024]{2,1,0:T(8,128)(2,1)} %get-tuple-element.34.refs_0_), channel_id=1, source_target_pairs={{0,96},{32,0},{64,32},{96,64},{1,97},{33,1},{65,33},{97,65},{2,98}... | collective-permute-start | bytes 1179656 | tf_op jit(solution)/shard_map/ppermute | solution.py:339
  208.6 27.1 %collective-permute-start.7 = (bf16[6,32,1024]{2,1,0:T(8,128)(2,1)}, bf16[6,32,1024]{2,1,0:T(8,128)(2,1)S(1)}, u32[]{:S(2)}, u32[]{:S(2)}) collective-permute-start(bf16[6,32,1024]{2,1,0:T(8,128)(2,1)} %get-tuple-element.35.refs_1_), channel_id=1, source_target_pairs={{0,32},{32,64},{64,96},{96,0},{1,33},{33,65},{65,97},{97,1},{2,34}... | collective-permute-start | bytes 1179656 | tf_op jit(solution)/shard_map/ppermute | solution.py:338
  215.8 20.1 %collective-permute-start.10 = (bf16[6,32,1024]{2,1,0:T(8,128)(2,1)S(1)}, bf16[6,32,1024]{2,1,0:T(8,128)(2,1)S(1)}, u32[]{:S(2)}, u32[]{:S(2)}) collective-permute-start(bf16[6,32,1024]{2,1,0:T(8,128)(2,1)S(1)} %collective-permute-done.6.refs_2_.refs_0_), channel_id=1, source_target_pairs={{0,32},{32,64},{64,96},{96,0},{1,33},{33,65},{65,97},{97,1},{2,34}... | collective-permute-start | bytes 1179656 | tf_op jit(solution)/shard_map/ppermute | solution.py:340
  218.5 16.0 %copy-start.4 = (bf16[6,32,1024]{2,1,0:T(8,128)(2,1)S(1)}, bf16[6,32,1024]{2,1,0:T(8,128)(2,1)}, u32[]{:S(2)}) copy-start(bf16[6,32,1024]{2,1,0:T(8,128)(2,1)} %copy-done.3) | copy-start | bytes 1179652
  230.9 11.3 %collective-permute-start.12 = (bf16[6,32,1024]{2,1,0:T(8,128)(2,1)}, bf16[6,32,1024]{2,1,0:T(8,128)(2,1)S(1)}, u32[]{:S(2)}, u32[]{:S(2)}) collective-permute-start(bf16[6,32,1024]{2,1,0:T(8,128)(2,1)} %get-tuple-element.39.refs_0_), channel_id=1, source_target_pairs={{0,32},{32,64},{64,96},{96,0},{1,33},{33,65},{65,97},{97,1},{2,34}... | collective-permute-start | bytes 1179656 | tf_op jit(solution)/shard_map/ppermute | solution.py:336
  231.9 10.4 %collective-permute-start.15 = (bf16[6,32,1024]{2,1,0:T(8,128)(2,1)}, bf16[6,32,1024]{2,1,0:T(8,128)(2,1)S(1)}, u32[]{:S(2)}, u32[]{:S(2)}) collective-permute-start(bf16[6,32,1024]{2,1,0:T(8,128)(2,1)} %get-tuple-element.40.refs_1_), channel_id=1, source_target_pairs={{0,96},{32,0},{64,32},{96,64},{1,97},{33,1},{65,33},{97,65},{2,98}... | collective-permute-start | bytes 1179656 | tf_op jit(solution)/shard_map/ppermute | solution.py:337
  234.6 15.5 %copy-start.11 = (bf16[6,32,1024]{2,1,0:T(8,128)(2,1)}, bf16[6,32,1024]{2,1,0:T(8,128)(2,1)S(1)}, u32[]{:S(2)}) copy-start(bf16[6,32,1024]{2,1,0:T(8,128)(2,1)S(1)} %collective-permute-done.8.refs_4_) | copy-start | bytes 1179652
  234.6 15.5 %collective-permute-start.11 = (bf16[6,32,1024]{2,1,0:T(8,128)(2,1)S(1)}, bf16[6,32,1024]{2,1,0:T(8,128)(2,1)S(1)}, u32[]{:S(2)}, u32[]{:S(2)}) collective-permute-start(bf16[6,32,1024]{2,1,0:T(8,128)(2,1)S(1)} %copy-done.4), channel_id=1, source_target_pairs={{0,96},{32,0},{64,32},{96,64},{1,97},{33,1},{65,33},{97,65},{2,98}... | collective-permute-start | bytes 1179656 | tf_op jit(solution)/shard_map/ppermute | solution.py:341
  235.8 14.3 %copy-start.12 = (bf16[6,32,1024]{2,1,0:T(8,128)(2,1)}, bf16[6,32,1024]{2,1,0:T(8,128)(2,1)S(1)}, u32[]{:S(2)}) copy-start(bf16[6,32,1024]{2,1,0:T(8,128)(2,1)S(1)} %collective-permute-done.7.refs_3_) | copy-start | bytes 1179652
  235.8 22.8 %collective-permute-start.14 = (bf16[6,32,1024]{2,1,0:T(8,128)(2,1)}, bf16[6,32,1024]{2,1,0:T(8,128)(2,1)S(1)}, u32[]{:S(2)}, u32[]{:S(2)}) collective-permute-start(bf16[6,32,1024]{2,1,0:T(8,128)(2,1)} %get-tuple-element.39.refs_0_), channel_id=1, source_target_pairs={{0,96},{32,0},{64,32},{96,64},{1,97},{33,1},{65,33},{97,65},{2,98}... | collective-permute-start | bytes 1179656 | tf_op jit(solution)/shard_map/ppermute | solution.py:339
  235.9 22.7 %collective-permute-start.13 = (bf16[6,32,1024]{2,1,0:T(8,128)(2,1)}, bf16[6,32,1024]{2,1,0:T(8,128)(2,1)S(1)}, u32[]{:S(2)}, u32[]{:S(2)}) collective-permute-start(bf16[6,32,1024]{2,1,0:T(8,128)(2,1)} %get-tuple-element.40.refs_1_), channel_id=1, source_target_pairs={{0,32},{32,64},{64,96},{96,0},{1,33},{33,65},{65,97},{97,1},{2,34}... | collective-permute-start | bytes 1179656 | tf_op jit(solution)/shard_map/ppermute | solution.py:338
  242.3 24.8 %copy-start.15 = (bf16[6,32,1024]{2,1,0:T(8,128)(2,1)}, bf16[6,32,1024]{2,1,0:T(8,128)(2,1)S(1)}, u32[]{:S(2)}) copy-start(bf16[6,32,1024]{2,1,0:T(8,128)(2,1)S(1)} %collective-permute-done.12.refs_2_) | copy-start | bytes 1179652
  242.3 17.0 %collective-permute-start.16 = (bf16[6,32,1024]{2,1,0:T(8,128)(2,1)S(1)}, bf16[6,32,1024]{2,1,0:T(8,128)(2,1)}, u32[]{:S(2)}, u32[]{:S(2)}) collective-permute-start(bf16[6,32,1024]{2,1,0:T(8,128)(2,1)S(1)} %collective-permute-done.12.refs_2_), channel_id=1, source_target_pairs={{0,32},{32,64},{64,96},{96,0},{1,33},{33,65},{65,97},{97,1},{2,34}... | collective-permute-start | bytes 1179656 | tf_op jit(solution)/shard_map/ppermute | solution.py:340
  242.3 24.8 %copy-start.16 = (bf16[6,32,1024]{2,1,0:T(8,128)(2,1)}, bf16[6,32,1024]{2,1,0:T(8,128)(2,1)S(1)}, u32[]{:S(2)}) copy-start(bf16[6,32,1024]{2,1,0:T(8,128)(2,1)S(1)} %collective-permute-done.15.refs_5_) | copy-start | bytes 1179652
  242.3 24.7 %collective-permute-start.17 = (bf16[6,32,1024]{2,1,0:T(8,128)(2,1)S(1)}, bf16[6,32,1024]{2,1,0:T(8,128)(2,1)}, u32[]{:S(2)}, u32[]{:S(2)}) collective-permute-start(bf16[6,32,1024]{2,1,0:T(8,128)(2,1)S(1)} %collective-permute-done.15.refs_5_), channel_id=1, source_target_pairs={{0,96},{32,0},{64,32},{96,64},{1,97},{33,1},{65,33},{97,65},{2,98}... | collective-permute-start | bytes 1179656 | tf_op jit(solution)/shard_map/ppermute | solution.py:341
  (10 other events, 44.6 us)
where the time goes:
time: 273 us; the launch traced here: 271 us
  waiting for transfers between devices  119 us (44%)
  Pallas kernels  61.2 us (22%)
  starting transfers between devices  44.8 us (16%)
  blocking collectives  28.4 us (10%)
  local copies, waits for them, and re-layouts  10.9 us (4%)
  other arithmetic  6.25 us (2%)
    ppermute x6, waiting for transfers between devices, body(): lax.ppermute(p, 'groups', shift(n))  65.9 us
    pallas_call x2, Pallas kernels, owner_work(): pl.pallas_call(functools.partial(owner_kernel, width), out_shape=jax.Shap...  30.5 us
    all_to_all x1, blocking collectives, exchange(): return lax.all_to_all(x, 'shard', 0, 0, tiled=True)  28.4 us
    all_to_all x4, waiting for transfers between devices, exchange(): return lax.all_to_all(x, 'shard', 0, 0, tiled=True)  26 us
    all_to_all x4, starting transfers between devices, exchange(): return lax.all_to_all(x, 'shard', 0, 0, tiled=True)  23.5 us
    pallas_call x2, Pallas kernels, sum_replicas(): pl.pallas_call(functools.partial(sum_kernel, width, last), out_shape=shap...  13.8 us
    ppermute x2, waiting for transfers between devices, to_all(): prev_a = lax.ppermute(a, 'groups', shift(1))  12 us
    ppermute x2, waiting for transfers between devices, to_all(): far_b = lax.ppermute(after_b, 'groups', shift(3))  10.8 us
  transfers between devices with their start and end apart: 22, of which 13 were waited for; matrix products, arithmetic and copies ran while one was open for 3% of the time, Pallas kernels for 19%

commit v1 on v0

--- a/solution.py
+++ b/solution.py
@@ -9,7 +9,7 @@
 
 
 LANES = 128
-CHUNKS = 2
+CHUNKS = (8, 8, 16)
 STEP = 8
 TALL = 256
 ANY = pl.BlockSpec(memory_space=pl.ANY)
@@ -26,9 +26,9 @@
     return jnp.dot(a, b, preferred_element_type=jnp.float32)
 
 
-def sum_kernel(width, last, meta, own, one, two, three, old, *refs):
-    before = refs[0] if last else None
-    outs = refs[1 if last else 0 : -2]
+def sum_kernel(width, first, last, meta, own, one, two, three, old, *refs):
+    before = None if first else refs[0]
+    outs = refs[0 if first else 1 : -2]
     norms = None if last else outs[-1]
     outs = outs if last else outs[:-1]
     codes, sems = refs[-2:]
@@ -39,30 +39,35 @@
             two[b].astype(jnp.float32) + three[b].astype(jnp.float32)
         )
         moment = 0.95 * old[b].astype(jnp.float32) + 0.05 * total * total
-        adam = total / (jnp.sqrt(moment) + 1e-08)
+        adam = total / (moment * lax.rsqrt(moment) + 1e-08)
         adam = adam * adam
         parts = [total[:, j : j + LANES] for j in range(0, width, LANES)]
         top = functools.reduce(jnp.maximum, [jnp.abs(p) for p in parts])
-        power = jnp.ceil(jnp.log2(jnp.maximum(top, 1e-30))) - 15.0
+        if last:
+            top = jnp.maximum(top[:8], top[8:])
+        power = jnp.floor(jnp.log2(jnp.maximum(top, 1e-30)) + 1e-4) - 14.0
         grow = jnp.exp2(-power)
+        if last:
+            grow = jnp.concatenate([grow, grow], axis=0)
         at = step * STEP + b
         for j, p in enumerate(parts):
-            code = jnp.clip(jnp.round(p * grow), -32767.0, 32767.0)
-            codes[at, :, j * LANES : (j + 1) * LANES] = code.astype(jnp.int32).astype(jnp.int16)
-        codes[at, :, width : width + LANES] = power.astype(jnp.int32).astype(jnp.int16)
+            codes[at, :, j * LANES : (j + 1) * LANES] = jnp.round(p * grow).astype(jnp.int32).astype(jnp.int16)
         squares = functools.reduce(jnp.add, [adam[:, j : j + LANES] for j in range(0, width, LANES)])
         squares = jnp.sum(squares, axis=0, keepdims=True)
+        if not first:
+            squares = squares + before[at]
         if not last:
             norms[at] = squares
+            codes[at, :, width:] = power.astype(jnp.int32).astype(jnp.int16)
             return 0
-        squares = squares + before[at]
-        power = jnp.ceil(jnp.log2(jnp.maximum(squares, 1e-30)))
-        scaled = squares * jnp.exp2(14.0 - power)
+        scale = jnp.ceil(jnp.log2(jnp.maximum(squares, 1e-30)))
+        scaled = squares * jnp.exp2(14.0 - scale)
         high = jnp.floor(scaled)
         low = jnp.floor((scaled - high) * 16384.0)
-        row = lax.broadcasted_iota(jnp.int32, (codes.shape[1], LANES), 0)
-        full = jnp.where(row == 0, power, jnp.where(row == 1, high, low))
-        codes[at, :, width + LANES :] = full.astype(jnp.int32).astype(jnp.int16)
+        row = lax.broadcasted_iota(jnp.int32, (8, LANES), 0)
+        full = jnp.where(row == 0, scale, jnp.where(row == 1, high, low))
+        full = jnp.concatenate([power, full], axis=0)
+        codes[at, :, width:] = full.astype(jnp.int32).astype(jnp.int16)
         return 0
 
     lax.fori_loop(0, STEP, block, 0)
@@ -80,19 +85,20 @@
             c.wait()
 
 
-def sum_replicas(gradients, received, old, chunk, group, sources, before=None):
+def sum_replicas(gradients, received, old, start, group, sources, before, last):
     nbg, per, width = received[0].shape
     steps = nbg // STEP
-    last = before is not None
-    columns = width + (2 if last else 1) * LANES
+    chunk = start // per
+    columns = width + LANES
     count = sum(x.shape[0] for x in sources)
     part = pl.BlockSpec((STEP, per, width), lambda i, meta: (i, 0, 0))
     whole = pl.BlockSpec((nbg, 1, LANES), lambda i, meta: (0, 0, 0))
     shapes = [jax.ShapeDtypeStruct((x.shape[0], per, columns), jnp.int16) for x in sources]
     if not last:
         shapes.append(jax.ShapeDtypeStruct((nbg, 1, LANES), jnp.float32))
-    return pl.pallas_call(
-        functools.partial(sum_kernel, width, last),
+    carried = [] if before is None else [before]
+    return pl.pallas_call(
+        functools.partial(sum_kernel, width, before is None, last),
         out_shape=shapes,
         grid_spec=pltpu.PrefetchScalarGridSpec(
             num_scalar_prefetch=1,
@@ -104,38 +110,42 @@
                 part,
                 pl.BlockSpec((STEP, per, width), lambda i, meta: (i, chunk, 0)),
             ]
-            + ([whole] if last else []),
+            + [whole] * len(carried),
             out_specs=[ANY] * len(sources) + ([] if last else [whole]),
             scratch_shapes=[
                 pltpu.VMEM((nbg, per, columns), jnp.int16),
                 pltpu.SemaphoreType.DMA((count,)),
             ],
         ),
-    )(
-        jnp.concatenate([group[None].astype(jnp.int32), *sources]),
-        gradients,
-        *received,
-        old,
-        *([before] if last else []),
-    )
+    )(jnp.concatenate([group[None].astype(jnp.int32), *sources]), gradients, *received, old, *carried)
 
 
 def owner_kernel(width, roots, *refs):
     arrived, update, high, low, pre = refs[:-4], refs[-4], refs[-3], refs[-2], refs[-1]
     n_src = arrived[0].shape[0]
-    per = arrived[0].shape[-2]
-    rows = per * len(arrived)
+    early, final = arrived[:-1], arrived[-1]
+    top = sum(a.shape[-2] for a in early)
+    rows = top + final.shape[-2]
+
+    def step_of(powers):
+        return jnp.exp2(powers.astype(jnp.int32).astype(jnp.float32))
 
     def unpack(n, graft):
-        for c, code in enumerate(arrived):
-            at = pl.ds(pl.multiple_of(n * rows + c * per, per), per)
-            got = code[n, 0] if len(code.shape) == 4 else code[n]
-            step = jnp.exp2(got[:, width : width + LANES].astype(jnp.int32).astype(jnp.float32))
-            for j in range(0, width, LANES):
-                value = got[:, j : j + LANES].astype(jnp.int32).astype(jnp.float32) * step
-                high[at, j : j + LANES], low[at, j : j + LANES] = two_parts(value)
-        norm = got[:, width + LANES :].astype(jnp.int32).astype(jnp.float32)
-        return graft + jnp.exp2(norm[0:1] - 14.0) * (norm[1:2] + norm[2:3] * (1.0 / 16384.0))
+        at = pl.ds(pl.multiple_of(n * rows, rows), top)
+        got = [a[n, 0] for a in early]
+        steps = [step_of(x[:, width:]) for x in got]
+        for j in range(0, width, LANES):
+            value = [x[:, j : j + LANES].astype(jnp.int32).astype(jnp.float32) * t for x, t in zip(got, steps)]
+            high[at, j : j + LANES], low[at, j : j + LANES] = two_parts(jnp.concatenate(value, axis=0))
+        at = pl.ds(pl.multiple_of(n * rows + top, top), rows - top)
+        got = final[n]
+        tail = got[:, width:].astype(jnp.int32).astype(jnp.float32)
+        step = jnp.exp2(tail[:8])
+        step = jnp.concatenate([step, step], axis=0)
+        for j in range(0, width, LANES):
+            value = got[:, j : j + LANES].astype(jnp.int32).astype(jnp.float32) * step
+            high[at, j : j + LANES], low[at, j : j + LANES] = two_parts(value)
+        return graft + jnp.exp2(tail[8:9] - 14.0) * (tail[9:10] + tail[10:11] * (1.0 / 16384.0))
 
     graft = lax.fori_loop(0, n_src, unpack, jnp.zeros((1, LANES), jnp.float32))
     graft = jnp.sum(graft, axis=1, keepdims=True)
@@ -180,30 +190,17 @@
 
 
 def renew_kernel(count, table, weights, *refs):
-    backs, outs, held, grads, sems = refs[:-5], refs[-5:-3], refs[-3], refs[-2], refs[-1]
-
-    def fetch(j):
-        return pltpu.make_async_copy(weights.at[table[j]], held.at[j], sems.at[0, j])
-
-    def pull(j, k):
-        return pltpu.make_async_copy(backs[k].at[table[count + j]], grads.at[j], sems.at[1, j])
-
-    for j in range(count):
-        fetch(j).start()
-        if len(backs) == 1:
-            pull(j, 0).start()
-        else:
-            for k in range(len(backs)):
-
-                @pl.when(table[2 * count + j] == k)
-                def _():
-                    pull(j, k).start()
-
+    backs, outs, held, sems = refs[:-4], refs[-4:-2], refs[-2], refs[-1]
+    copies = [pltpu.make_async_copy(weights.at[table[j]], held.at[j], sems.at[j]) for j in range(count)]
+    for c in copies:
+        c.start()
     half = count // 2
     for j in range(count):
-        fetch(j).wait()
-        pull(j, 0).wait()
-        stepped = held[j].astype(jnp.float32) - 0.5 * grads[j].astype(jnp.float32)
+        grad = backs[0][table[count + j]].astype(jnp.float32)
+        for k in range(1, len(backs)):
+            grad = jnp.where(table[2 * count + j] == k, backs[k][table[count + j]].astype(jnp.float32), grad)
+        copies[j].wait()
+        stepped = held[j].astype(jnp.float32) - 0.5 * grad
         scale = lax.rsqrt(jnp.mean(stepped * stepped, axis=1, keepdims=True) + 1e-06)
         outs[j // half][j % half] = (stepped * scale).astype(jnp.bfloat16)
 
@@ -215,11 +212,10 @@
     return pl.pallas_call(
         functools.partial(renew_kernel, count),
         out_shape=(half, half),
-        in_specs=[SMEM] + [ANY] * (1 + len(backs)),
+        in_specs=[SMEM, ANY] + [pl.BlockSpec(memory_space=pltpu.VMEM)] * len(backs),
         scratch_shapes=[
             pltpu.VMEM((count, rows, width), jnp.bfloat16),
-            pltpu.VMEM((count, rows, width), jnp.bfloat16),
-            pltpu.SemaphoreType.DMA((2, count)),
+            pltpu.SemaphoreType.DMA((count,)),
         ],
     )(table, weights, *backs)
 
@@ -283,12 +279,12 @@
     def shift(n):
         return [(i, (i + n) % groups) for i in range(groups)]
 
-    per = rows // CHUNKS
+    starts = [sum(CHUNKS[:c]) for c in range(len(CHUNKS))]
     received = []
     grads = gradients
-    for c in range(CHUNKS):
+    for start, per in zip(starts, CHUNKS):
         pieces = [
-            lax.dynamic_slice(grads[0], (nbg * ((g + n) % groups), c * per, 0), (nbg, per, width)) for n in (1, 3, 2)
+            lax.dynamic_slice(grads[0], (nbg * ((g + n) % groups), start, 0), (nbg, per, width)) for n in (1, 3, 2)
         ]
         grads, pieces = lax.optimization_barrier((grads, pieces))
         received.append([lax.ppermute(p, "groups", shift(n)) for p, n in zip(pieces, (1, 3, 2))])
@@ -319,12 +315,21 @@
             x, after = lax.optimization_barrier((x, after))
         return lax.all_to_all(x, "shard", 0, 0, tiled=True)
 
-    code, norm = sum_replicas(gradients, received[0], second_moment, 0, g, [jnp.stack(source, 1).reshape(-1)])
-    codes = sum_replicas(gradients, received[1], second_moment, 1, g, source, norm)
-    first = exchange(code.reshape(shards, slots, per, width + LANES))
+    norm = None
+    coded = []
+    for c, start in enumerate(starts):
+        last = c == len(starts) - 1
+        wanted = source if last else [jnp.stack(source, 1).reshape(-1)]
+        code = sum_replicas(gradients, received[c], second_moment, start, g, wanted, norm, last)
+        coded.append(code)
+        norm = None if last else code[-1]
+    early = []
+    for c, code in enumerate(coded[:-1]):
+        packed = code[0].reshape(shards, slots, CHUNKS[c], width + LANES)
+        early.append(exchange(packed, early[-1] if early else None))
     arrived = []
     for k in range(slots):
-        arrived.append([first, exchange(codes[k], arrived[-1][-1] if k else first)])
+        arrived.append(early + [exchange(coded[-1][k], arrived[-1][-1] if k else early[-1])])
 
     backs = []
     for k in range(slots):
@@ -358,7 +363,10 @@
     new = renew(late, weights, backs)
     pieces1 = to_all(new)
     out = scatter_blocks(places(0, half), pieces0, out_shape)
-    return scatter_blocks(places(half, nbg), pieces1, out_shape, base=out)
+    where = places(half, nbg)
+    far = 3 * half
+    out = scatter_blocks(where[:far], pieces1[:6], out_shape, base=out)
+    return scatter_blocks(where[far:], pieces1[6:], out_shape, base=out)
 
 
 def solution(mesh):

time: 273 us -> 288 us (1.055)
  starting transfers between devices: 44.8 us -> 58.4 us
  Pallas kernels: 61.2 us -> 69.7 us
  waiting for transfers between devices: 119 us -> 112 us
    all_to_all x4 -> x5, starting transfers between devices: 23.5 us -> 31.1 us  [exchange(): return lax.all_to_all(x, 'shard', 0, 0, tiled=True)]
    pallas_call x2 -> x3, Pallas kernels: 13.8 us -> 18.5 us  [sum_replicas(): pl.pallas_call(functools.partial(sum_kernel, width, before is None, last)...]
    ppermute x2, starting transfers between devices: 1.36 us -> 5.01 us  [to_all(): after_a = lax.ppermute(a, 'groups', shift(3))]
    ppermute x6 -> x9, starting transfers between devices: 8.86 us -> 11.9 us  [body(): lax.ppermute(p, 'groups', shift(n))]
    all_to_all x4 -> x5, waiting for transfers between devices: 26 us -> 24 us  [exchange(): return lax.all_to_all(x, 'shard', 0, 0, tiled=True)]
    unnamed x40 -> x50, local copies, waits for them, and re-layouts: 5.41 us -> 7.07 us
    pallas_call x2 -> x3, Pallas kernels: 7.78 us -> 9.27 us  [scatter_blocks(): pl.pallas_call(scatter_kernel if base is None else scatter_more_kernel, o...]
    ppermute x6 -> x9, waiting for transfers between devices: 65.9 us -> 66.1 us  [body(): lax.ppermute(p, 'groups', shift(n))]
  transfers between devices with their start and end apart: 22 -> 26, of which waited for: 13 -> 14; matrix products, arithmetic and copies ran while one was open for 3% -> 3% of each run, Pallas kernels for 19% -> 22%
where the time goes in v1:
time: 288 us; the launch traced here: 285 us
  waiting for transfers between devices  112 us (39%)
  Pallas kernels  69.7 us (24%)
  starting transfers between devices  58.4 us (20%)
  blocking collectives  27.1 us (9%)
  local copies, waits for them, and re-layouts  12 us (4%)
  other arithmetic  5.5 us (2%)
    ppermute x9, waiting for transfers between devices, body(): lax.ppermute(p, 'groups', shift(n))  66.1 us
    all_to_all x5, starting transfers between devices, exchange(): return lax.all_to_all(x, 'shard', 0, 0, tiled=True)  31.1 us
    pallas_call x2, Pallas kernels, owner_work(): pl.pallas_call(functools.partial(owner_kernel, width), out_shape=jax.Shap...  30.4 us
    all_to_all x1, blocking collectives, exchange(): return lax.all_to_all(x, 'shard', 0, 0, tiled=True)  27.1 us
    all_to_all x5, waiting for transfers between devices, exchange(): return lax.all_to_all(x, 'shard', 0, 0, tiled=True)  24 us
    pallas_call x3, Pallas kernels, sum_replicas(): pl.pallas_call(functools.partial(sum_kernel, width, before is None, last)...  18.5 us
    ppermute x9, starting transfers between devices, body(): lax.ppermute(p, 'groups', shift(n))  11.9 us
    pallas_call x2, Pallas kernels, renew(): pl.pallas_call(functools.partial(renew_kernel, count), out_shape=(half, h...  10.3 us
  transfers between devices with their start and end apart: 26, of which 14 were waited for; matrix products, arithmetic and copies ran while one was open for 3% of the time, Pallas kernels for 22%

profile of v1, /device:TPU:1, one launch (start us, length us, event | category | flops | bytes accessed | tf_op | source)
XLA Modules:
  0.0 285.4 jit_solution(184700332259782911)
XLA Ops:
  7.7 5.4 %collective-permute-done.one = bf16[24,8,1024]{2,1,0:T(8,128)(2,1)S(1)} collective-permute-done((bf16[24,8,1024]{2,1,0:T(8,128)(2,1)S(1)}, bf16[24,8,1024]{2,1,0:T(8,128)(2,1)S(1)}, u32[]{:S(2)}, u32[]{:S(2)}) %collective-permute-start) | collective-permute-done | bytes 393248 | tf_op jit(solution)/shard_map/ppermute | solution.py:290
  13.2 9.7 %collective-permute-done.2.three = bf16[24,8,1024]{2,1,0:T(8,128)(2,1)S(1)} collective-permute-done((bf16[24,8,1024]{2,1,0:T(8,128)(2,1)S(1)}, bf16[24,8,1024]{2,1,0:T(8,128)(2,1)S(1)}, u32[]{:S(2)}, u32[]{:S(2)}) %collective-permute-start.2) | collective-permute-done | bytes 393248 | tf_op jit(solution)/shard_map/ppermute | solution.py:290
  23.6 5.9 %shard_map.55 = (s16[64,8,1152]{2,1,0:T(8,128)(2,1)}, f32[24,1,128]{2,1,0:T(1,128)}) custom-call(s32[65]{0:T(128)} %pad_add_fusion.4.meta, bf16[1,96,32,1024]{3,2,1,0:T(8,128)(2,1)} %own.5, bf16[24,8,1024]{2,1,0:T(8,128)(2,1)} %copy-done.14, bf16[24,8,1024]{2,1,0:T(8,128)(2,1)} %copy-done.15, bf16[24,8,1024]{2,1,0:T(8,128)(2,1)} %copy-done.16, ...), custom_call_target="tpu_custom_call" | custom-call | tf_op jit(solution)/shard_map/pallas_call | solution.py:100
  29.5 9.6 %all-to-all-start = ((s16[32,2,8,1152]{3,2,1,0:T(8,128)(2,1)}), s16[32,2,8,1152]{3,2,1,0:T(8,128)(2,1)S(1)}, u32[]{:S(2)}, u32[]{:S(2)}) async-start(s16[32,2,8,1152]{3,2,1,0:T(8,128)(2,1)} %bitcast.62), calls=%async_computation | async-start | bytes 2359296 | tf_op jit(solution)/shard_map/all_to_all | solution.py:316
  44.2 8.0 %collective-permute-done.3.one = bf16[24,8,1024]{2,1,0:T(8,128)(2,1)S(1)} collective-permute-done((bf16[24,8,1024]{2,1,0:T(8,128)(2,1)S(1)}, bf16[24,8,1024]{2,1,0:T(8,128)(2,1)S(1)}, u32[]{:S(2)}, u32[]{:S(2)}) %collective-permute-start.3) | collective-permute-done | bytes 393248 | tf_op jit(solution)/shard_map/ppermute | solution.py:290
  52.2 9.4 %collective-permute-done.5.three = bf16[24,8,1024]{2,1,0:T(8,128)(2,1)S(1)} collective-permute-done((bf16[24,8,1024]{2,1,0:T(8,128)(2,1)S(1)}, bf16[24,8,1024]{2,1,0:T(8,128)(2,1)S(1)}, u32[]{:S(2)}, u32[]{:S(2)}) %collective-permute-start.5) | collective-permute-done | bytes 393248 | tf_op jit(solution)/shard_map/ppermute | solution.py:290
  62.3 6.0 %shard_map.56 = (s16[64,8,1152]{2,1,0:T(8,128)(2,1)}, f32[24,1,128]{2,1,0:T(1,128)}) custom-call(s32[65]{0:T(128)} %pad_add_fusion.4.meta, bf16[1,96,32,1024]{3,2,1,0:T(8,128)(2,1)} %own.5, bf16[24,8,1024]{2,1,0:T(8,128)(2,1)} %copy-done.17, bf16[24,8,1024]{2,1,0:T(8,128)(2,1)} %copy-done.18, bf16[24,8,1024]{2,1,0:T(8,128)(2,1)} %copy-done.19, ...), custom_call_target="tpu_custom_call" | custom-call | tf_op jit(solution)/shard_map/pallas_call | solution.py:100
  68.4 8.1 %all-to-all-start.1 = ((s16[32,2,8,1152]{3,2,1,0:T(8,128)(2,1)}), s16[32,2,8,1152]{3,2,1,0:T(8,128)(2,1)S(1)}, u32[]{:S(2)}, u32[]{:S(2)}) async-start(s16[32,2,8,1152]{3,2,1,0:T(8,128)(2,1)} %bitcast.61), calls=%async_computation.1 | async-start | bytes 2359296 | tf_op jit(solution)/shard_map/all_to_all | solution.py:316
  82.0 16.4 %collective-permute-done.6.one = bf16[24,16,1024]{2,1,0:T(8,128)(2,1)S(1)} collective-permute-done((bf16[24,16,1024]{2,1,0:T(8,128)(2,1)S(1)}, bf16[24,16,1024]{2,1,0:T(8,128)(2,1)S(1)}, u32[]{:S(2)}, u32[]{:S(2)}) %collective-permute-start.6) | collective-permute-done | bytes 786464 | tf_op jit(solution)/shard_map/ppermute | solution.py:290
  98.5 17.2 %collective-permute-done.8.three = bf16[24,16,1024]{2,1,0:T(8,128)(2,1)S(1)} collective-permute-done((bf16[24,16,1024]{2,1,0:T(8,128)(2,1)S(1)}, bf16[24,16,1024]{2,1,0:T(8,128)(2,1)S(1)}, u32[]{:S(2)}, u32[]{:S(2)}) %collective-permute-start.8) | collective-permute-done | bytes 786464 | tf_op jit(solution)/shard_map/ppermute | solution.py:290
  116.6 6.7 %shard_map.57 = (s16[32,16,1152]{2,1,0:T(8,128)(2,1)}, s16[32,16,1152]{2,1,0:T(8,128)(2,1)}) custom-call(s32[65]{0:T(128)} %pad_add_fusion.5.meta, bf16[1,96,32,1024]{3,2,1,0:T(8,128)(2,1)} %own.5, bf16[24,16,1024]{2,1,0:T(8,128)(2,1)} %copy-done.7, bf16[24,16,1024]{2,1,0:T(8,128)(2,1)} %copy-done.8, bf16[24,16,1024]{2,1,0:T(8,128)(2,1)} %copy-done.9, ...), custom_call_target="tpu_custom_call" | custom-call | tf_op jit(solution)/shard_map/pallas_call | solution.py:100
  123.3 27.1 %all_to_all.30.refs_2_ = s16[32,16,1152]{2,1,0:T(8,128)(2,1)} all-to-all(s16[32,16,1152]{2,1,0:T(8,128)(2,1)} %get-tuple-element.47), channel_id=1, replica_groups=mesh['groups'=4,'shard'=32] {'shard'}, dimensions={0} | all-to-all | bytes 2359296 | tf_op jit(solution)/shard_map/all_to_all | solution.py:316
  150.4 4.0 %all-to-all-start.4 = ((s16[32,16,1152]{2,1,0:T(8,128)(2,1)}), s16[32,16,1152]{2,1,0:T(8,128)(2,1)S(1)}, u32[]{:S(2)}, u32[]{:S(2)}) async-start(s16[32,16,1152]{2,1,0:T(8,128)(2,1)} %get-tuple-element.51), calls=%async_computation.4 | async-start | bytes 2359296 | tf_op jit(solution)/shard_map/all_to_all | solution.py:316
  154.4 15.2 %shard_map.58 = bf16[1024,1024]{1,0:T(8,128)(2,1)} custom-call(bf16[1,1,2,2,1024,1024]{5,4,3,2,1,0:T(8,128)(2,1)} %roots.3, s16[32,2,8,1152]{3,2,1,0:T(8,128)(2,1)} %copy-done.1, s16[32,2,8,1152]{3,2,1,0:T(8,128)(2,1)} %copy-done.2, s16[32,16,1152]{2,1,0:T(8,128)(2,1)} %all_to_all.30.refs_2_), custom_call_target="tpu_custom_call" | custom-call | tf_op jit(solution)/shard_map/pallas_call | solution.py:178
  169.6 3.3 %all-to-all-done.4.refs_2_ = s16[32,16,1152]{2,1,0:T(8,128)(2,1)S(1)} async-done(((s16[32,16,1152]{2,1,0:T(8,128)(2,1)}), s16[32,16,1152]{2,1,0:T(8,128)(2,1)S(1)}, u32[]{:S(2)}, u32[]{:S(2)}) %all-to-all-start.4) | async-done | bytes 1179680 | tf_op jit(solution)/shard_map/all_to_all | solution.py:316
  173.8 4.2 %all-to-all-start.3 = ((bf16[32,32,1024]{2,1,0:T(8,128)(2,1)}), bf16[32,32,1024]{2,1,0:T(8,128)(2,1)S(1)}, u32[]{:S(2)}, u32[]{:S(2)}) async-start(bf16[32,32,1024]{2,1,0:T(8,128)(2,1)} %bitcast.60), calls=%async_computation.3 | async-start | bytes 4194304 | tf_op jit(solution)/shard_map/all_to_all | solution.py:316
  178.1 15.2 %shard_map.62 = bf16[1024,1024]{1,0:T(8,128)(2,1)} custom-call(bf16[1,1,2,2,1024,1024]{5,4,3,2,1,0:T(8,128)(2,1)} %roots.3, s16[32,2,8,1152]{3,2,1,0:T(8,128)(2,1)} %copy-done.1, s16[32,2,8,1152]{3,2,1,0:T(8,128)(2,1)} %copy-done.2, s16[32,16,1152]{2,1,0:T(8,128)(2,1)} %copy-done.3), custom_call_target="tpu_custom_call" | custom-call | tf_op jit(solution)/shard_map/pallas_call | solution.py:178
  193.3 13.1 %all-to-all-done.3.refs_0_ = bf16[32,32,1024]{2,1,0:T(8,128)(2,1)S(1)} async-done(((bf16[32,32,1024]{2,1,0:T(8,128)(2,1)}), bf16[32,32,1024]{2,1,0:T(8,128)(2,1)S(1)}, u32[]{:S(2)}, u32[]{:S(2)}) %all-to-all-start.3) | async-done | bytes 2097184 | tf_op jit(solution)/shard_map/all_to_all | solution.py:316
  207.7 5.2 %all-to-all-start.5 = ((bf16[32,32,1024]{2,1,0:T(8,128)(2,1)}), bf16[32,32,1024]{2,1,0:T(8,128)(2,1)}, u32[]{:S(2)}, u32[]{:S(2)}) async-start(bf16[32,32,1024]{2,1,0:T(8,128)(2,1)} %bitcast.59), calls=%async_computation.5 | async-start | bytes 4194304 | tf_op jit(solution)/shard_map/all_to_all | solution.py:316
  214.5 4.7 %shard_map.59 = (bf16[6,32,1024]{2,1,0:T(8,128)(2,1)}, bf16[6,32,1024]{2,1,0:T(8,128)(2,1)}) custom-call(s32[36]{0:T(128)} %pad_add_fusion.3.table, bf16[24,32,1024]{2,1,0:T(8,128)(2,1)} %weights.3, bf16[32,32,1024]{2,1,0:T(8,128)(2,1)} %copy-done), custom_call_target="tpu_custom_call" | custom-call | tf_op jit(solution)/shard_map/pallas_call | solution.py:212
  222.6 2.7 collective-permute-start.11
  225.3 5.8 %collective-permute-done.9.refs_2_.refs_0_ = bf16[6,32,1024]{2,1,0:T(8,128)(2,1)S(1)} collective-permute-done((bf16[6,32,1024]{2,1,0:T(8,128)(2,1)}, bf16[6,32,1024]{2,1,0:T(8,128)(2,1)S(1)}, u32[]{:S(2)}, u32[]{:S(2)}) %collective-permute-start.9) | collective-permute-done | bytes 393248 | tf_op jit(solution)/shard_map/ppermute | solution.py:341
  233.8 7.6 %all-to-all-done.5.refs_1_ = bf16[32,32,1024]{2,1,0:T(8,128)(2,1)} async-done(((bf16[32,32,1024]{2,1,0:T(8,128)(2,1)}), bf16[32,32,1024]{2,1,0:T(8,128)(2,1)}, u32[]{:S(2)}, u32[]{:S(2)}) %all-to-all-start.5) | async-done | bytes 2097184 | tf_op jit(solution)/shard_map/all_to_all | solution.py:316
  241.4 5.5 %shard_map.63 = (bf16[6,32,1024]{2,1,0:T(8,128)(2,1)}, bf16[6,32,1024]{2,1,0:T(8,128)(2,1)}) custom-call(s32[36]{0:T(128)} %shard_map.61.table, bf16[24,32,1024]{2,1,0:T(8,128)(2,1)} %weights.3, bf16[32,32,1024]{2,1,0:T(8,128)(2,1)} %copy-done, bf16[32,32,1024]{2,1,0:T(8,128)(2,1)} %all-to-all-done.5.refs_1_), custom_call_target="tpu_custom_call" | custom-call | tf_op jit(solution)/shard_map/pallas_call | solution.py:212
  251.6 2.3 collective-permute-start.17
  254.0 4.3 %collective-permute-done.15.refs_2_ = bf16[6,32,1024]{2,1,0:T(8,128)(2,1)S(1)} collective-permute-done((bf16[6,32,1024]{2,1,0:T(8,128)(2,1)}, bf16[6,32,1024]{2,1,0:T(8,128)(2,1)S(1)}, u32[]{:S(2)}, u32[]{:S(2)}) %collective-permute-start.15) | collective-permute-done | bytes 393248 | tf_op jit(solution)/shard_map/ppermute | solution.py:341
  258.3 3.0 %collective-permute-start.20 = (bf16[6,32,1024]{2,1,0:T(8,128)(2,1)S(1)}, bf16[6,32,1024]{2,1,0:T(8,128)(2,1)}, u32[]{:S(2)}, u32[]{:S(2)}) collective-permute-start(bf16[6,32,1024]{2,1,0:T(8,128)(2,1)S(1)} %collective-permute-done.18.refs_5_), channel_id=1, source_target_pairs={{0,96},{32,0},{64,32},{96,64},{1,97},{33,1},{65,33},{97,65},{2,98}... | collective-permute-start | bytes 1179656 | tf_op jit(solution)/shard_map/ppermute | solution.py:346
  263.1 3.2 %collective-permute-done.14.refs_7_ = bf16[6,32,1024]{2,1,0:T(8,128)(2,1)S(1)} collective-permute-done((bf16[6,32,1024]{2,1,0:T(8,128)(2,1)S(1)}, bf16[6,32,1024]{2,1,0:T(8,128)(2,1)S(1)}, u32[]{:S(2)}, u32[]{:S(2)}) %collective-permute-start.14) | collective-permute-done | bytes 393248 | tf_op jit(solution)/shard_map/ppermute | solution.py:346
  267.0 3.9 %shard_map.60.base = bf16[96,32,1024]{2,1,0:T(8,128)(2,1)} custom-call(s32[48]{0:T(128)} %pad_add_fusion.2.place, bf16[6,32,1024]{2,1,0:T(8,128)(2,1)} %get-tuple-element.48.refs_0_, bf16[6,32,1024]{2,1,0:T(8,128)(2,1)} %get-tuple-element.49.refs_1_, bf16[6,32,1024]{2,1,0:T(8,128)(2,1)} %copy-done.4, bf16[6,32,1024]{2,1,0:T(8,128)(2,1)} %copy-done.10, ...), custom_call_target="tpu_custom_call" | custom-call | tf_op jit(solution)/shard_map/pallas_call | solution.py:258
  271.0 3.9 %collective-permute-done.17.refs_4_ = bf16[6,32,1024]{2,1,0:T(8,128)(2,1)} collective-permute-done((bf16[6,32,1024]{2,1,0:T(8,128)(2,1)}, bf16[6,32,1024]{2,1,0:T(8,128)(2,1)}, u32[]{:S(2)}, u32[]{:S(2)}) %collective-permute-start.17) | collective-permute-done | bytes 393248 | tf_op jit(solution)/shard_map/ppermute | solution.py:344
  274.8 3.3 %shard_map.64.base = bf16[96,32,1024]{2,1,0:T(8,128)(2,1)} custom-call(s32[36]{0:T(128)} %pad_add_fusion.1.place, bf16[96,32,1024]{2,1,0:T(8,128)(2,1)} %shard_map.60.base, bf16[6,32,1024]{2,1,0:T(8,128)(2,1)} %get-tuple-element.53.refs_0_, bf16[6,32,1024]{2,1,0:T(8,128)(2,1)} %get-tuple-element.54.refs_1_, ...), custom_call_target="tpu_custom_call", output_to_operand_aliasing={{}: (1, {})} | custom-call | tf_op jit(solution)/shard_map/pallas_call | solution.py:258
  278.1 5.0 %collective-permute-done.20.refs_1_ = bf16[6,32,1024]{2,1,0:T(8,128)(2,1)} collective-permute-done((bf16[6,32,1024]{2,1,0:T(8,128)(2,1)S(1)}, bf16[6,32,1024]{2,1,0:T(8,128)(2,1)}, u32[]{:S(2)}, u32[]{:S(2)}) %collective-permute-start.20) | collective-permute-done | bytes 393248 | tf_op jit(solution)/shard_map/ppermute | solution.py:346
  (111 shorter events, 40.1 us)
Async XLA Ops:
  1.3 11.8 %collective-permute-start = (bf16[24,8,1024]{2,1,0:T(8,128)(2,1)S(1)}, bf16[24,8,1024]{2,1,0:T(8,128)(2,1)S(1)}, u32[]{:S(2)}, u32[]{:S(2)}) collective-permute-start(bf16[24,8,1024]{2,1,0:T(8,128)(2,1)S(1)} %get-tuple-element.30), channel_id=1, source_target_pairs={{0,32},{32,64},{64,96},{96,0},{1,33},{33,65},{65,97},{97,1},{2,34}... | collective-permute-start | bytes 1179656 | tf_op jit(solution)/shard_map/ppermute | solution.py:290
  3.4 9.7 %collective-permute-start.1 = (bf16[24,8,1024]{2,1,0:T(8,128)(2,1)S(1)}, bf16[24,8,1024]{2,1,0:T(8,128)(2,1)S(1)}, u32[]{:S(2)}, u32[]{:S(2)}) collective-permute-start(bf16[24,8,1024]{2,1,0:T(8,128)(2,1)S(1)} %get-tuple-element.31), channel_id=1, source_target_pairs={{0,96},{32,0},{64,32},{96,64},{1,97},{33,1},{65,33},{97,65},{2,98}... | collective-permute-start | bytes 1179656 | tf_op jit(solution)/shard_map/ppermute | solution.py:290
  4.8 18.1 %collective-permute-start.2 = (bf16[24,8,1024]{2,1,0:T(8,128)(2,1)S(1)}, bf16[24,8,1024]{2,1,0:T(8,128)(2,1)S(1)}, u32[]{:S(2)}, u32[]{:S(2)}) collective-permute-start(bf16[24,8,1024]{2,1,0:T(8,128)(2,1)S(1)} %get-tuple-element.32), channel_id=1, source_target_pairs={{0,64},{32,96},{64,0},{96,32},{1,65},{33,97},{65,1},{97,33},{2,66}... | collective-permute-start | bytes 1179656 | tf_op jit(solution)/shard_map/ppermute | solution.py:290
  29.5 38.9 %all-to-all-start = ((s16[32,2,8,1152]{3,2,1,0:T(8,128)(2,1)}), s16[32,2,8,1152]{3,2,1,0:T(8,128)(2,1)S(1)}, u32[]{:S(2)}, u32[]{:S(2)}) async-start(s16[32,2,8,1152]{3,2,1,0:T(8,128)(2,1)} %bitcast.62), calls=%async_computation | async-start | bytes 2359296 | tf_op jit(solution)/shard_map/all_to_all | solution.py:316
  40.5 11.7 %collective-permute-start.3 = (bf16[24,8,1024]{2,1,0:T(8,128)(2,1)S(1)}, bf16[24,8,1024]{2,1,0:T(8,128)(2,1)S(1)}, u32[]{:S(2)}, u32[]{:S(2)}) collective-permute-start(bf16[24,8,1024]{2,1,0:T(8,128)(2,1)S(1)} %get-tuple-element.35), channel_id=1, source_target_pairs={{0,32},{32,64},{64,96},{96,0},{1,33},{33,65},{65,97},{97,1},{2,34}... | collective-permute-start | bytes 1179656 | tf_op jit(solution)/shard_map/ppermute | solution.py:290
  41.4 10.8 %collective-permute-start.4 = (bf16[24,8,1024]{2,1,0:T(8,128)(2,1)S(1)}, bf16[24,8,1024]{2,1,0:T(8,128)(2,1)S(1)}, u32[]{:S(2)}, u32[]{:S(2)}) collective-permute-start(bf16[24,8,1024]{2,1,0:T(8,128)(2,1)S(1)} %get-tuple-element.36), channel_id=1, source_target_pairs={{0,96},{32,0},{64,32},{96,64},{1,97},{33,1},{65,33},{97,65},{2,98}... | collective-permute-start | bytes 1179656 | tf_op jit(solution)/shard_map/ppermute | solution.py:290
  43.2 18.4 %collective-permute-start.5 = (bf16[24,8,1024]{2,1,0:T(8,128)(2,1)S(1)}, bf16[24,8,1024]{2,1,0:T(8,128)(2,1)S(1)}, u32[]{:S(2)}, u32[]{:S(2)}) collective-permute-start(bf16[24,8,1024]{2,1,0:T(8,128)(2,1)S(1)} %get-tuple-element.37), channel_id=1, source_target_pairs={{0,64},{32,96},{64,0},{96,32},{1,65},{33,97},{65,1},{97,33},{2,66}... | collective-permute-start | bytes 1179656 | tf_op jit(solution)/shard_map/ppermute | solution.py:290
  68.4 54.9 %all-to-all-start.1 = ((s16[32,2,8,1152]{3,2,1,0:T(8,128)(2,1)}), s16[32,2,8,1152]{3,2,1,0:T(8,128)(2,1)S(1)}, u32[]{:S(2)}, u32[]{:S(2)}) async-start(s16[32,2,8,1152]{3,2,1,0:T(8,128)(2,1)} %bitcast.61), calls=%async_computation.1 | async-start | bytes 2359296 | tf_op jit(solution)/shard_map/all_to_all | solution.py:316
  78.3 20.1 %collective-permute-start.6 = (bf16[24,16,1024]{2,1,0:T(8,128)(2,1)S(1)}, bf16[24,16,1024]{2,1,0:T(8,128)(2,1)S(1)}, u32[]{:S(2)}, u32[]{:S(2)}) collective-permute-start(bf16[24,16,1024]{2,1,0:T(8,128)(2,1)S(1)} %get-tuple-element.42), channel_id=1, source_target_pairs={{0,32},{32,64},{64,96},{96,0},{1,33},{33,65},{65,97},{97,1},{2,34}... | collective-permute-start | bytes 2359304 | tf_op jit(solution)/shard_map/ppermute | solution.py:290
  79.3 19.2 %collective-permute-start.7 = (bf16[24,16,1024]{2,1,0:T(8,128)(2,1)S(1)}, bf16[24,16,1024]{2,1,0:T(8,128)(2,1)S(1)}, u32[]{:S(2)}, u32[]{:S(2)}) collective-permute-start(bf16[24,16,1024]{2,1,0:T(8,128)(2,1)S(1)} %get-tuple-element.43), channel_id=1, source_target_pairs={{0,96},{32,0},{64,32},{96,64},{1,97},{33,1},{65,33},{97,65},{2,98}... | collective-permute-start | bytes 2359304 | tf_op jit(solution)/shard_map/ppermute | solution.py:290
  81.1 34.6 %collective-permute-start.8 = (bf16[24,16,1024]{2,1,0:T(8,128)(2,1)S(1)}, bf16[24,16,1024]{2,1,0:T(8,128)(2,1)S(1)}, u32[]{:S(2)}, u32[]{:S(2)}) collective-permute-start(bf16[24,16,1024]{2,1,0:T(8,128)(2,1)S(1)} %get-tuple-element.44), channel_id=1, source_target_pairs={{0,64},{32,96},{64,0},{96,32},{1,65},{33,97},{65,1},{97,33},{2,66}... | collective-permute-start | bytes 2359304 | tf_op jit(solution)/shard_map/ppermute | solution.py:290
  98.5 18.1 %copy-start.7 = (bf16[24,16,1024]{2,1,0:T(8,128)(2,1)}, bf16[24,16,1024]{2,1,0:T(8,128)(2,1)S(1)}, u32[]{:S(2)}) copy-start(bf16[24,16,1024]{2,1,0:T(8,128)(2,1)S(1)} %collective-permute-done.6.one) | copy-start | bytes 2359300
  98.5 18.1 %copy-start.8 = (bf16[24,16,1024]{2,1,0:T(8,128)(2,1)}, bf16[24,16,1024]{2,1,0:T(8,128)(2,1)S(1)}, u32[]{:S(2)}) copy-start(bf16[24,16,1024]{2,1,0:T(8,128)(2,1)S(1)} %collective-permute-done.7.two) | copy-start | bytes 2359300
  123.2 27.1 %copy-start.2 = (s16[32,2,8,1152]{3,2,1,0:T(8,128)(2,1)}, s16[32,2,8,1152]{3,2,1,0:T(8,128)(2,1)S(1)}, u32[]{:S(2)}) copy-start(s16[32,2,8,1152]{3,2,1,0:T(8,128)(2,1)S(1)} %all-to-all-done.1.refs_1_) | copy-start | bytes 3538948
  150.4 22.4 %all-to-all-start.4 = ((s16[32,16,1152]{2,1,0:T(8,128)(2,1)}), s16[32,16,1152]{2,1,0:T(8,128)(2,1)S(1)}, u32[]{:S(2)}, u32[]{:S(2)}) async-start(s16[32,16,1152]{2,1,0:T(8,128)(2,1)} %get-tuple-element.51), calls=%async_computation.4 | async-start | bytes 2359296 | tf_op jit(solution)/shard_map/all_to_all | solution.py:316
  173.8 32.6 %all-to-all-start.3 = ((bf16[32,32,1024]{2,1,0:T(8,128)(2,1)}), bf16[32,32,1024]{2,1,0:T(8,128)(2,1)S(1)}, u32[]{:S(2)}, u32[]{:S(2)}) async-start(bf16[32,32,1024]{2,1,0:T(8,128)(2,1)} %bitcast.60), calls=%async_computation.3 | async-start | bytes 4194304 | tf_op jit(solution)/shard_map/all_to_all | solution.py:316
  207.7 33.6 %all-to-all-start.5 = ((bf16[32,32,1024]{2,1,0:T(8,128)(2,1)}), bf16[32,32,1024]{2,1,0:T(8,128)(2,1)}, u32[]{:S(2)}, u32[]{:S(2)}) async-start(bf16[32,32,1024]{2,1,0:T(8,128)(2,1)} %bitcast.59), calls=%async_computation.5 | async-start | bytes 4194304 | tf_op jit(solution)/shard_map/all_to_all | solution.py:316
  219.2 11.8 %collective-permute-start.9 = (bf16[6,32,1024]{2,1,0:T(8,128)(2,1)}, bf16[6,32,1024]{2,1,0:T(8,128)(2,1)S(1)}, u32[]{:S(2)}, u32[]{:S(2)}) collective-permute-start(bf16[6,32,1024]{2,1,0:T(8,128)(2,1)} %get-tuple-element.48.refs_0_), channel_id=1, source_target_pairs={{0,32},{32,64},{64,96},{96,0},{1,33},{33,65},{65,97},{97,1},{2,34}... | collective-permute-start | bytes 1179656 | tf_op jit(solution)/shard_map/ppermute | solution.py:341
  220.1 10.9 %collective-permute-start.12 = (bf16[6,32,1024]{2,1,0:T(8,128)(2,1)}, bf16[6,32,1024]{2,1,0:T(8,128)(2,1)S(1)}, u32[]{:S(2)}, u32[]{:S(2)}) collective-permute-start(bf16[6,32,1024]{2,1,0:T(8,128)(2,1)} %get-tuple-element.49.refs_1_), channel_id=1, source_target_pairs={{0,96},{32,0},{64,32},{96,64},{1,97},{33,1},{65,33},{97,65},{2,98}... | collective-permute-start | bytes 1179656 | tf_op jit(solution)/shard_map/ppermute | solution.py:342
  222.6 27.4 %collective-permute-start.10 = (bf16[6,32,1024]{2,1,0:T(8,128)(2,1)}, bf16[6,32,1024]{2,1,0:T(8,128)(2,1)S(1)}, u32[]{:S(2)}, u32[]{:S(2)}) collective-permute-start(bf16[6,32,1024]{2,1,0:T(8,128)(2,1)} %get-tuple-element.49.refs_1_), channel_id=1, source_target_pairs={{0,32},{32,64},{64,96},{96,0},{1,33},{33,65},{65,97},{97,1},{2,34}... | collective-permute-start | bytes 1179656 | tf_op jit(solution)/shard_map/ppermute | solution.py:343
  222.6 28.6 %collective-permute-start.11 = (bf16[6,32,1024]{2,1,0:T(8,128)(2,1)}, bf16[6,32,1024]{2,1,0:T(8,128)(2,1)S(1)}, u32[]{:S(2)}, u32[]{:S(2)}) collective-permute-start(bf16[6,32,1024]{2,1,0:T(8,128)(2,1)} %get-tuple-element.48.refs_0_), channel_id=1, source_target_pairs={{0,96},{32,0},{64,32},{96,64},{1,97},{33,1},{65,33},{97,65},{2,98}... | collective-permute-start | bytes 1179656 | tf_op jit(solution)/shard_map/ppermute | solution.py:344
  231.1 20.6 %collective-permute-start.13 = (bf16[6,32,1024]{2,1,0:T(8,128)(2,1)S(1)}, bf16[6,32,1024]{2,1,0:T(8,128)(2,1)S(1)}, u32[]{:S(2)}, u32[]{:S(2)}) collective-permute-start(bf16[6,32,1024]{2,1,0:T(8,128)(2,1)S(1)} %collective-permute-done.9.refs_2_.refs_0_), channel_id=1, source_target_pairs={{0,32},{32,64},{64,96},{96,0},{1,33},{33,65},{65,97},{97,1},{2,34}... | collective-permute-start | bytes 1179656 | tf_op jit(solution)/shard_map/ppermute | solution.py:345
  233.8 16.3 %copy-start.6 = (bf16[6,32,1024]{2,1,0:T(8,128)(2,1)S(1)}, bf16[6,32,1024]{2,1,0:T(8,128)(2,1)}, u32[]{:S(2)}) copy-start(bf16[6,32,1024]{2,1,0:T(8,128)(2,1)} %copy-done.5) | copy-start | bytes 1179652
  246.9 11.3 %collective-permute-start.15 = (bf16[6,32,1024]{2,1,0:T(8,128)(2,1)}, bf16[6,32,1024]{2,1,0:T(8,128)(2,1)S(1)}, u32[]{:S(2)}, u32[]{:S(2)}) collective-permute-start(bf16[6,32,1024]{2,1,0:T(8,128)(2,1)} %get-tuple-element.53.refs_0_), channel_id=1, source_target_pairs={{0,32},{32,64},{64,96},{96,0},{1,33},{33,65},{65,97},{97,1},{2,34}... | collective-permute-start | bytes 1179656 | tf_op jit(solution)/shard_map/ppermute | solution.py:341
  247.9 10.4 %collective-permute-start.18 = (bf16[6,32,1024]{2,1,0:T(8,128)(2,1)}, bf16[6,32,1024]{2,1,0:T(8,128)(2,1)S(1)}, u32[]{:S(2)}, u32[]{:S(2)}) collective-permute-start(bf16[6,32,1024]{2,1,0:T(8,128)(2,1)} %get-tuple-element.54.refs_1_), channel_id=1, source_target_pairs={{0,96},{32,0},{64,32},{96,64},{1,97},{33,1},{65,33},{97,65},{2,98}... | collective-permute-start | bytes 1179656 | tf_op jit(solution)/shard_map/ppermute | solution.py:342
  250.1 16.2 %collective-permute-start.14 = (bf16[6,32,1024]{2,1,0:T(8,128)(2,1)S(1)}, bf16[6,32,1024]{2,1,0:T(8,128)(2,1)S(1)}, u32[]{:S(2)}, u32[]{:S(2)}) collective-permute-start(bf16[6,32,1024]{2,1,0:T(8,128)(2,1)S(1)} %copy-done.6), channel_id=1, source_target_pairs={{0,96},{32,0},{64,32},{96,64},{1,97},{33,1},{65,33},{97,65},{2,98}... | collective-permute-start | bytes 1179656 | tf_op jit(solution)/shard_map/ppermute | solution.py:346
  251.3 19.7 %collective-permute-start.16 = (bf16[6,32,1024]{2,1,0:T(8,128)(2,1)}, bf16[6,32,1024]{2,1,0:T(8,128)(2,1)S(1)}, u32[]{:S(2)}, u32[]{:S(2)}) collective-permute-start(bf16[6,32,1024]{2,1,0:T(8,128)(2,1)} %get-tuple-element.54.refs_1_), channel_id=1, source_target_pairs={{0,32},{32,64},{64,96},{96,0},{1,33},{33,65},{65,97},{97,1},{2,34}... | collective-permute-start | bytes 1179656 | tf_op jit(solution)/shard_map/ppermute | solution.py:343
  251.6 23.2 %collective-permute-start.17 = (bf16[6,32,1024]{2,1,0:T(8,128)(2,1)}, bf16[6,32,1024]{2,1,0:T(8,128)(2,1)}, u32[]{:S(2)}, u32[]{:S(2)}) collective-permute-start(bf16[6,32,1024]{2,1,0:T(8,128)(2,1)} %get-tuple-element.53.refs_0_), channel_id=1, source_target_pairs={{0,96},{32,0},{64,32},{96,64},{1,97},{33,1},{65,33},{97,65},{2,98}... | collective-permute-start | bytes 1179656 | tf_op jit(solution)/shard_map/ppermute | solution.py:344
  258.3 16.5 %copy-start.20 = (bf16[6,32,1024]{2,1,0:T(8,128)(2,1)}, bf16[6,32,1024]{2,1,0:T(8,128)(2,1)S(1)}, u32[]{:S(2)}) copy-start(bf16[6,32,1024]{2,1,0:T(8,128)(2,1)S(1)} %collective-permute-done.15.refs_2_) | copy-start | bytes 1179652
  258.3 19.8 %collective-permute-start.19 = (bf16[6,32,1024]{2,1,0:T(8,128)(2,1)S(1)}, bf16[6,32,1024]{2,1,0:T(8,128)(2,1)S(1)}, u32[]{:S(2)}, u32[]{:S(2)}) collective-permute-start(bf16[6,32,1024]{2,1,0:T(8,128)(2,1)S(1)} %collective-permute-done.15.refs_2_), channel_id=1, source_target_pairs={{0,32},{32,64},{64,96},{96,0},{1,33},{33,65},{65,97},{97,1},{2,34}... | collective-permute-start | bytes 1179656 | tf_op jit(solution)/shard_map/ppermute | solution.py:345
  258.3 16.5 %copy-start.21 = (bf16[6,32,1024]{2,1,0:T(8,128)(2,1)}, bf16[6,32,1024]{2,1,0:T(8,128)(2,1)S(1)}, u32[]{:S(2)}) copy-start(bf16[6,32,1024]{2,1,0:T(8,128)(2,1)S(1)} %collective-permute-done.18.refs_5_) | copy-start | bytes 1179652
  258.3 24.8 %collective-permute-start.20 = (bf16[6,32,1024]{2,1,0:T(8,128)(2,1)S(1)}, bf16[6,32,1024]{2,1,0:T(8,128)(2,1)}, u32[]{:S(2)}, u32[]{:S(2)}) collective-permute-start(bf16[6,32,1024]{2,1,0:T(8,128)(2,1)S(1)} %collective-permute-done.18.refs_5_), channel_id=1, source_target_pairs={{0,96},{32,0},{64,32},{96,64},{1,97},{33,1},{65,33},{97,65},{2,98}... | collective-permute-start | bytes 1179656 | tf_op jit(solution)/shard_map/ppermute | solution.py:346
  (19 other events, 116.3 us)

commit v2 on v1

v2 whole, which is shorter than its diff:
```python
import functools

import jax
import jax.numpy as jnp
from jax import lax
from jax.experimental import pallas as pl
from jax.experimental.pallas import tpu as pltpu
from jax.sharding import PartitionSpec as P


LANES = 128
CHUNKS = (8, 8, 16)
TALL = 256
ANY = pl.BlockSpec(memory_space=pl.ANY)
SMEM = pl.BlockSpec(memory_space=pltpu.SMEM)
SMALL = pltpu.CompilerParams(vmem_limit_bytes=12 * 2**20)
LARGE = pltpu.CompilerParams(vmem_limit_bytes=20 * 2**20)
VMEM = pl.BlockSpec(memory_space=pltpu.VMEM)


def in_hbm(x):
    return pltpu.with_memory_space_constraint(x, pltpu.HBM)


def in_vmem(x):
    return pltpu.with_memory_space_constraint(x, pltpu.VMEM)


def two_parts(values):
    high = values.astype(jnp.bfloat16)
    low = (values - high.astype(jnp.float32)).astype(jnp.bfloat16)
    return high, low


def dot(a, b):
    return jnp.dot(a, b, preferred_element_type=jnp.float32)


def sum_kernel(start, first, last, meta, gradients, one, two, three, old_all, *refs):
    before = None if first else refs[0]
    outs = refs[0 if first else 1 : -5]
    norms = None if last else outs[-1]
    outs = outs if last else outs[:-1]
    own, old, codes, in_sems, sems = refs[-5:]
    nbg, per, width = one.shape
    rows = pl.ds(start, per)
    loads = [
        pltpu.make_async_copy(gradients.at[0, pl.ds(meta[0] * nbg, nbg), rows], own, in_sems.at[0]),
        pltpu.make_async_copy(old_all.at[:, rows], old, in_sems.at[1]),
    ]
    for x in loads:
        x.start()
    for x in loads:
        x.wait()

    def code_block(at):
        total = (own[at].astype(jnp.float32) + one[at].astype(jnp.float32)) + (
            two[at].astype(jnp.float32) + three[at].astype(jnp.float32)
        )
        moment = 0.95 * old[at].astype(jnp.float32) + 0.05 * total * total
        adam = total / (moment * lax.rsqrt(moment) + 1e-08)
        adam = adam * adam
        parts = [total[:, j : j + LANES] for j in range(0, width, LANES)]
        top = functools.reduce(jnp.maximum, [jnp.abs(p) for p in parts])
        if last:
            top = jnp.maximum(top[:8], top[8:])
        power = jnp.floor(jnp.log2(jnp.maximum(top, 1e-30)) + 1e-4) - 14.0
        grow = jnp.exp2(-power)
        if last:
            grow = jnp.concatenate([grow, grow], axis=0)
        for j, p in enumerate(parts):
            codes[at, :, j * LANES : (j + 1) * LANES] = jnp.round(p * grow).astype(jnp.int32).astype(jnp.int16)
        squares = functools.reduce(jnp.add, [adam[:, j : j + LANES] for j in range(0, width, LANES)])
        squares = jnp.sum(squares, axis=0, keepdims=True)
        if not first:
            squares = squares + before[at]
        if not last:
            norms[at] = squares
            codes[at, :, width:] = power.astype(jnp.int32).astype(jnp.int16)
            return
        scale = jnp.ceil(jnp.log2(jnp.maximum(squares, 1e-30)))
        scaled = squares * jnp.exp2(14.0 - scale)
        high = jnp.floor(scaled)
        low = jnp.floor((scaled - high) * 16384.0)
        row = lax.broadcasted_iota(jnp.int32, (8, LANES), 0)
        full = jnp.where(row == 0, scale, jnp.where(row == 1, high, low))
        full = jnp.concatenate([power, full], axis=0)
        codes[at, :, width:] = full.astype(jnp.int32).astype(jnp.int16)

    def block(at, _):
        code_block(at)
        owner, rank = meta[1 + at], meta[1 + nbg + at]
        if not last:
            slots = outs[0].shape[1]
            pltpu.make_async_copy(codes.at[at], outs[0].at[owner, jnp.minimum(rank, slots - 1)], sems.at[at]).start()
        else:
            for k, out in enumerate(outs):

                @pl.when(rank == k)
                def _():
                    pltpu.make_async_copy(codes.at[at], out.at[owner], sems.at[at]).start()

        return 0

    lax.fori_loop(0, nbg, block, 0)
    to = outs[0].at[0] if last else outs[0].at[0, 0]
    for n in range(nbg):
        pltpu.make_async_copy(codes.at[n], to, sems.at[n]).wait()


def sum_replicas(gradients, received, old, start, meta, before, shards, slots, last):
    nbg, per, width = received[0].shape
    columns = width + LANES
    if last:
        shapes = [jax.ShapeDtypeStruct((shards, per, columns), jnp.int16)] * slots
    else:
        shapes = [
            jax.ShapeDtypeStruct((shards, slots, per, columns), jnp.int16),
            jax.ShapeDtypeStruct((nbg, 1, LANES), jnp.float32),
        ]
    carried = [] if before is None else [before]
    return pl.pallas_call(
        functools.partial(sum_kernel, start, before is None, last),
        out_shape=shapes,
        in_specs=[SMEM, ANY, VMEM, VMEM, VMEM, ANY] + [VMEM] * len(carried),
        out_specs=[ANY] * slots if last else [ANY, VMEM],
        scratch_shapes=[
            pltpu.VMEM((nbg, per, width), jnp.bfloat16),
            pltpu.VMEM((nbg, per, width), jnp.bfloat16),
            pltpu.VMEM((nbg, per, columns), jnp.int16),
            pltpu.SemaphoreType.DMA((2,)),
            pltpu.SemaphoreType.DMA((nbg,)),
        ],
        compiler_params=SMALL,
    )(meta, in_hbm(gradients), *[in_vmem(r) for r in received], in_hbm(old), *carried)


def owner_kernel(slot, all_roots, *refs):
    arrived, update, high, low, pre, roots, sems = refs[:-6], *refs[-6:]
    width = update.shape[0]
    loads = [pltpu.make_async_copy(all_roots.at[0, 0, slot, k], roots.at[k], sems.at[k]) for k in (1, 0)]
    for x in loads:
        x.start()
    n_src = arrived[0].shape[0]
    early, final = arrived[:-1], arrived[-1]
    top = sum(a.shape[-2] for a in early)
    rows = top + final.shape[-2]

    def step_of(powers):
        return jnp.exp2(powers.astype(jnp.int32).astype(jnp.float32))

    def unpack(n, graft):
        at = pl.ds(pl.multiple_of(n * rows, rows), top)
        got = [a[n, slot] for a in early]
        steps = [step_of(x[:, width:]) for x in got]
        for j in range(0, width, LANES):
            value = [x[:, j : j + LANES].astype(jnp.int32).astype(jnp.float32) * t for x, t in zip(got, steps)]
            high[at, j : j + LANES], low[at, j : j + LANES] = two_parts(jnp.concatenate(value, axis=0))
        at = pl.ds(pl.multiple_of(n * rows + top, top), rows - top)
        got = final[n]
        tail = got[:, width:].astype(jnp.int32).astype(jnp.float32)
        step = jnp.exp2(tail[:8])
        step = jnp.concatenate([step, step], axis=0)
        for j in range(0, width, LANES):
            value = got[:, j : j + LANES].astype(jnp.int32).astype(jnp.float32) * step
            high[at, j : j + LANES], low[at, j : j + LANES] = two_parts(value)
        return graft + jnp.exp2(tail[8:9] - 14.0) * (tail[9:10] + tail[10:11] * (1.0 / 16384.0))

    graft = lax.fori_loop(0, n_src, unpack, jnp.zeros((1, LANES), jnp.float32))
    graft = jnp.sum(graft, axis=1, keepdims=True)
    loads[0].wait()
    right = roots[1]
    for m in range(0, width, TALL):
        at = pl.ds(m, TALL)
        high[at, :], low[at, :] = two_parts(dot(high[at, :], right) + dot(low[at, :], right))
    loads[1].wait()
    square = jnp.zeros((1, width), jnp.float32)
    for m in range(0, width, TALL):
        at = pl.ds(m, TALL)
        left = roots[0, at, :]
        got = dot(left, high[...]) + dot(left, low[...])
        pre[at, :] = got
        square = square + jnp.sum(got * got, axis=0, keepdims=True)
    square = jnp.sum(square, axis=1, keepdims=True)
    scale = jnp.sqrt(graft) / jnp.sqrt(square + 1e-06)
    for m in range(0, width, TALL):
        at = pl.ds(m, TALL)
        update[at, :] = (scale * pre[at, :]).astype(jnp.bfloat16)


def owner_work(roots, arrived, slot):
    width = roots.shape[-1]
    return pl.pallas_call(
        functools.partial(owner_kernel, slot),
        out_shape=jax.ShapeDtypeStruct((width, width), jnp.bfloat16),
        in_specs=[ANY] + [VMEM] * len(arrived),
        out_specs=VMEM,
        scratch_shapes=[
            pltpu.VMEM((width, width), jnp.bfloat16),
            pltpu.VMEM((width, width), jnp.bfloat16),
            pltpu.VMEM((width, width), jnp.float32),
            pltpu.VMEM((2, width, width), jnp.bfloat16),
            pltpu.SemaphoreType.DMA((2,)),
        ],
        compiler_params=LARGE,
    )(in_hbm(roots), *[in_vmem(a) for a in arrived])


def renew_kernel(count, table, weights, *refs):
    backs, outs, held, sems = refs[:-4], refs[-4:-2], refs[-2], refs[-1]
    copies = [pltpu.make_async_copy(weights.at[table[j]], held.at[j], sems.at[j]) for j in range(count)]
    for c in copies:
        c.start()
    half = count // 2

    def block(j, k):
        grad = backs[k][table[count + j]].astype(jnp.float32)
        stepped = held[j].astype(jnp.float32) - 0.5 * grad
        scale = lax.rsqrt(jnp.mean(stepped * stepped, axis=1, keepdims=True) + 1e-06)
        outs[j // half][j % half] = (stepped * scale).astype(jnp.bfloat16)

    for j in range(count):
        copies[j].wait()
        if len(backs) == 1:
            block(j, 0)
            continue
        for k in range(len(backs)):
            pl.when(table[2 * count + j] == k)(functools.partial(block, j, k))


def renew(table, weights, backs):
    count = table.shape[0] // 3
    rows, width = weights.shape[1:]
    half = jax.ShapeDtypeStruct((count // 2, rows, width), jnp.bfloat16)
    return pl.pallas_call(
        functools.partial(renew_kernel, count),
        out_shape=(half, half),
        in_specs=[SMEM, ANY] + [VMEM] * len(backs),
        scratch_shapes=[
            pltpu.VMEM((count, rows, width), jnp.bfloat16),
            pltpu.SemaphoreType.DMA((count,)),
        ],
        compiler_params=SMALL,
    )(table, in_hbm(weights), *[in_vmem(x) for x in backs])


def pass_kernel(count, *refs):
    for ref, out in zip(refs[:count], refs[-count:]):
        for j in range(ref.shape[0]):
            out[j] = ref[j]


def pass_tables(tables, after=()):
    return pl.pallas_call(
        functools.partial(pass_kernel, len(tables)),
        out_shape=[jax.ShapeDtypeStruct(t.shape, t.dtype) for t in tables],
        in_specs=[SMEM] * len(tables) + [VMEM] * len(after),
        out_specs=[SMEM] * len(tables),
        compiler_params=SMALL,
    )(*tables, *[in_vmem(a) for a in after])


def scatter_kernel(place, *refs):
    pieces, out, sems = refs[:-2], refs[-2], refs[-1]
    copies = []
    for piece in pieces:
        for j in range(piece.shape[0]):
            n = len(copies)
            copies.append(pltpu.make_async_copy(piece.at[j], out.at[place[n]], sems.at[n]))
    for c in copies:
        c.start()
    for c in copies:
        c.wait()


def scatter_more_kernel(place, base, *refs):
    del base
    scatter_kernel(place, *refs)


def scatter_blocks(place, pieces, out_shape, base=None):
    pieces = [in_vmem(p) for p in pieces]
    count = sum(p.shape[0] for p in pieces)
    operands = pieces if base is None else [in_hbm(base)] + pieces
    return pl.pallas_call(
        scatter_kernel if base is None else scatter_more_kernel,
        out_shape=out_shape,
        in_specs=[SMEM] + [ANY] * (len(operands) - len(pieces)) + [pl.BlockSpec(memory_space=pltpu.VMEM)] * len(pieces),
        out_specs=ANY,
        scratch_shapes=[pltpu.SemaphoreType.DMA((count,))],
        input_output_aliases={} if base is None else {1: 0},
        compiler_params=SMALL,
    )(place, *operands)


def body(gradients, second_moment, inverse_roots, owners, weights):
    groups = lax.axis_size("groups")
    shards = lax.axis_size("shard")
    g = lax.axis_index("groups")
    total_blocks = owners.shape[0]
    nbg = total_blocks // groups
    slots = inverse_roots.shape[2]
    rows = gradients.shape[2]
    width = gradients.shape[3]
    half = nbg // 2

    def shift(n):
        return [(i, (i + n) % groups) for i in range(groups)]

    starts = [sum(CHUNKS[:c]) for c in range(len(CHUNKS))]
    received = []
    grads = gradients
    for start, per in zip(starts, CHUNKS):
        pieces = [
            lax.dynamic_slice(grads[0], (nbg * ((g + n) % groups), start, 0), (nbg, per, width)) for n in (1, 3, 2)
        ]
        grads, pieces = lax.optimization_barrier((grads, pieces))
        received.append([lax.ppermute(p, "groups", shift(n)) for p, n in zip(pieces, (1, 3, 2))])

    ids = jnp.arange(nbg, dtype=jnp.int32)
    earlier = ids[None, :] < ids[:, None]
    my_owner = lax.dynamic_slice_in_dim(owners, nbg * g, nbg)
    my_rank = jnp.sum(((my_owner[:, None] == my_owner[None, :]) & earlier).astype(jnp.int32), axis=1)
    meta = jnp.concatenate([g[None].astype(jnp.int32), my_owner, my_rank])
    grouped = owners.reshape(groups, nbg)
    same = grouped[:, :, None] == grouped[:, None, :]
    rank = jnp.sum((same & earlier[None]).astype(jnp.int32), axis=2)
    firsts = rank == 0
    before = jnp.sum((firsts[:, None, :] & earlier[None]).astype(jnp.int32), axis=2)
    n_first = jnp.sum(firsts.astype(jnp.int32), axis=1, keepdims=True)
    spot = jnp.where(firsts, before, n_first + ids[None] - before)
    sits = spot[:, None, :] == ids[None, :, None]
    order = jnp.sum(jnp.where(sits, ids[None, None, :], 0), axis=2)
    by_order = [
        lax.dynamic_index_in_dim(jnp.sum(jnp.where(sits, t[:, None, :], 0), axis=2), g, 0, False)
        for t in (jnp.broadcast_to(ids[None], grouped.shape), grouped, rank)
    ]

    def exchange(x, after=None):
        if after is not None:
            x, after = lax.optimization_barrier((x, after))
        return lax.all_to_all(x, "shard", 0, 0, tiled=True)

    norm = None
    coded = []
    for c, start in enumerate(starts):
        last = c == len(starts) - 1
        code = sum_replicas(gradients, received[c], second_moment, start, meta, norm, shards, slots, last)
        coded.append(code)
        norm = None if last else code[-1]
    early = []
    for code in coded[:-1]:
        early.append(exchange(code[0], early[-1] if early else None))
    arrived = []
    for k in range(slots):
        arrived.append(early + [exchange(coded[-1][k], arrived[-1][-1] if k else early[-1])])

    backs = []
    for k in range(slots):
        update = owner_work(inverse_roots, arrived[k], k)
        backs.append(exchange(update.reshape(shards, rows, width), backs[-1] if k else None))

    def to_all(new):
        a, b = new
        prev_a = lax.ppermute(a, "groups", shift(1))
        after_b = lax.ppermute(b, "groups", shift(3))
        prev_b = lax.ppermute(b, "groups", shift(1))
        after_a = lax.ppermute(a, "groups", shift(3))
        far_a = lax.ppermute(prev_a, "groups", shift(1))
        far_b = lax.ppermute(after_b, "groups", shift(3))
        return [a, b, prev_a, prev_b, after_a, after_b, far_a, far_b]

    def places(lo, hi):
        out = []
        for n in (0, 3, 1, 2):
            h = (g + n) % groups
            out.append(nbg * h + lax.dynamic_index_in_dim(order, h, 0, False)[lo:hi])
        return jnp.concatenate(out)

    def table(lo, hi):
        return jnp.concatenate([t[lo:hi] for t in by_order])

    out_shape = jax.ShapeDtypeStruct((total_blocks, rows, width), jnp.bfloat16)
    where = places(half, nbg)
    far = 3 * half
    tables = [table(0, half), table(half, nbg), places(0, half), where[:far], where[far:]]
    tables = pass_tables(tables)
    new = renew(tables[0], weights, backs[:1])
    pieces0 = to_all(new)
    late = pass_tables(tables[1:2], [pieces0[2], pieces0[5]])
    new = renew(late[0], weights, backs)
    pieces1 = to_all(new)
    out = scatter_blocks(tables[2], pieces0, out_shape)
    out = scatter_blocks(tables[3], pieces1[:6], out_shape, base=out)
    return scatter_blocks(tables[4], pieces1[6:], out_shape, base=out)


def solution(mesh):
    return jax.shard_map(
        body,
        mesh=mesh,
        in_specs=(
            P("groups", None, "shard", None),
            P("groups", "shard", None),
            P("groups", "shard", None, None, None, None),
            P(),
            P("groups", "shard", None),
        ),
        out_specs=P(None, "shard", None),
        check_vma=False,
    )
```

time: 288 us -> 278 us (0.965)
  Pallas kernels: 69.7 us -> 53.6 us
  waiting for transfers between devices: 112 us -> 122 us
  other arithmetic: 5.5 us -> 1.5 us
    pallas_call x6 -> x7, Pallas kernels: 50.1 us -> 38.5 us  [the longest x2 23.6 us: owner_work(): pl.pallas_call(functools.partial(owner_kernel, slot), out_shape=jax.Shape...]
    ppermute x2, waiting for transfers between devices: 8.17 us -> 11.3 us  [to_all(): far_b = lax.ppermute(after_b, 'groups', shift(3))]
    all_to_all x5, waiting for transfers between devices: 24 us -> 26.9 us  [exchange(): return lax.all_to_all(x, 'shard', 0, 0, tiled=True)]
    unnamed x50 -> x18, local copies, waits for them, and re-layouts: 7.07 us -> 8.23 us
  transfers between devices with their start and end apart: 26 -> 26, of which waited for: 14 -> 14; matrix products, arithmetic and copies ran while one was open for 3% -> 2% of each run, Pallas kernels for 22% -> 18%
where the time goes in v2:
time: 278 us; the launch traced here: 276 us
  waiting for transfers between devices  122 us (44%)
  starting transfers between devices  57.3 us (21%)
  Pallas kernels  53.6 us (19%)
  blocking collectives  27.1 us (10%)
  local copies, waits for them, and re-layouts  13.1 us (5%)
    ppermute x9, waiting for transfers between devices, body(): lax.ppermute(p, 'groups', shift(n))  67.7 us
    all_to_all x5, starting transfers between devices, exchange(): return lax.all_to_all(x, 'shard', 0, 0, tiled=True)  31.6 us
    all_to_all x1, blocking collectives, exchange(): return lax.all_to_all(x, 'shard', 0, 0, tiled=True)  27.1 us
    all_to_all x5, waiting for transfers between devices, exchange(): return lax.all_to_all(x, 'shard', 0, 0, tiled=True)  26.9 us
    pallas_call x2, Pallas kernels, owner_work(): pl.pallas_call(functools.partial(owner_kernel, slot), out_shape=jax.Shape...  23.6 us
    pallas_call x3, Pallas kernels, sum_replicas(): pl.pallas_call(functools.partial(sum_kernel, start, before is None, last)...  12.5 us
    ppermute x9, starting transfers between devices, body(): lax.ppermute(p, 'groups', shift(n))  11.8 us
    ppermute x2, waiting for transfers between devices, to_all(): prev_a = lax.ppermute(a, 'groups', shift(1))  11.4 us
  transfers between devices with their start and end apart: 26, of which 14 were waited for; matrix products, arithmetic and copies ran while one was open for 2% of the time, Pallas kernels for 18%

profile of v2, /device:TPU:1, one launch (start us, length us, event | category | flops | bytes accessed | tf_op | source)
XLA Modules:
  0.0 275.6 jit_solution(4750777755626872238)
XLA Ops:
  1.3 2.1 collective-permute-start
  6.8 6.4 %collective-permute-done.one = bf16[24,8,1024]{2,1,0:T(8,128)(2,1)S(1)} collective-permute-done((bf16[24,8,1024]{2,1,0:T(8,128)(2,1)S(1)}, bf16[24,8,1024]{2,1,0:T(8,128)(2,1)S(1)}, u32[]{:S(2)}, u32[]{:S(2)}) %collective-permute-start) | collective-permute-done | bytes 393248 | tf_op jit(solution)/shard_map/ppermute | solution.py:318
  13.2 9.7 %collective-permute-done.2.three = bf16[24,8,1024]{2,1,0:T(8,128)(2,1)S(1)} collective-permute-done((bf16[24,8,1024]{2,1,0:T(8,128)(2,1)S(1)}, bf16[24,8,1024]{2,1,0:T(8,128)(2,1)S(1)}, u32[]{:S(2)}, u32[]{:S(2)}) %collective-permute-start.2) | collective-permute-done | bytes 393248 | tf_op jit(solution)/shard_map/ppermute | solution.py:318
  22.8 3.5 %shard_map.56 = (s16[32,2,8,1152]{3,2,1,0:T(8,128)(2,1)}, f32[24,1,128]{2,1,0:T(1,128)S(1)}) custom-call(s32[49]{0:T(128)S(1)} %pad_add_fusion.4.meta, bf16[1,96,32,1024]{3,2,1,0:T(8,128)(2,1)} %gradients.5, bf16[24,8,1024]{2,1,0:T(8,128)(2,1)S(1)} %collective-permute-done.one, bf16[24,8,1024]{2,1,0:T(8,128)(2,1)S(1)} %collective-permute-done.1.two, ...), custom_call_target="tpu_custom_call" | custom-call | tf_op jit(solution)/shard_map/pallas_call | solution.py:122
  26.4 9.6 %all-to-all-start = ((s16[32,2,8,1152]{3,2,1,0:T(8,128)(2,1)}), s16[32,2,8,1152]{3,2,1,0:T(8,128)(2,1)S(1)}, u32[]{:S(2)}, u32[]{:S(2)}) async-start(s16[32,2,8,1152]{3,2,1,0:T(8,128)(2,1)} %get-tuple-element.42), calls=%async_computation | async-start | bytes 2359296 | tf_op jit(solution)/shard_map/all_to_all | solution.py:342
  40.3 8.8 %collective-permute-done.3.one = bf16[24,8,1024]{2,1,0:T(8,128)(2,1)S(1)} collective-permute-done((bf16[24,8,1024]{2,1,0:T(8,128)(2,1)S(1)}, bf16[24,8,1024]{2,1,0:T(8,128)(2,1)S(1)}, u32[]{:S(2)}, u32[]{:S(2)}) %collective-permute-start.3) | collective-permute-done | bytes 393248 | tf_op jit(solution)/shard_map/ppermute | solution.py:318
  49.1 8.6 %collective-permute-done.5.three = bf16[24,8,1024]{2,1,0:T(8,128)(2,1)S(1)} collective-permute-done((bf16[24,8,1024]{2,1,0:T(8,128)(2,1)S(1)}, bf16[24,8,1024]{2,1,0:T(8,128)(2,1)S(1)}, u32[]{:S(2)}, u32[]{:S(2)}) %collective-permute-start.5) | collective-permute-done | bytes 393248 | tf_op jit(solution)/shard_map/ppermute | solution.py:318
  57.7 3.6 %shard_map.57 = (s16[32,2,8,1152]{3,2,1,0:T(8,128)(2,1)S(1)}, f32[24,1,128]{2,1,0:T(1,128)S(1)}) custom-call(s32[49]{0:T(128)S(1)} %pad_add_fusion.4.meta, bf16[1,96,32,1024]{3,2,1,0:T(8,128)(2,1)} %gradients.5, bf16[24,8,1024]{2,1,0:T(8,128)(2,1)S(1)} %collective-permute-done.3.one, bf16[24,8,1024]{2,1,0:T(8,128)(2,1)S(1)} %collective-permute-done.4.two, ...), custom_call_target="tpu_custom_call" | custom-call | tf_op jit(solution)/shard_map/pallas_call | solution.py:122
  62.3 8.1 %all-to-all-start.1 = ((s16[32,2,8,1152]{3,2,1,0:T(8,128)(2,1)}), s16[32,2,8,1152]{3,2,1,0:T(8,128)(2,1)S(1)}, u32[]{:S(2)}, u32[]{:S(2)}) async-start(s16[32,2,8,1152]{3,2,1,0:T(8,128)(2,1)} %copy-done.5), calls=%async_computation.1 | async-start | bytes 2359296 | tf_op jit(solution)/shard_map/all_to_all | solution.py:342
  76.0 16.4 %collective-permute-done.6.one = bf16[24,16,1024]{2,1,0:T(8,128)(2,1)S(1)} collective-permute-done((bf16[24,16,1024]{2,1,0:T(8,128)(2,1)S(1)}, bf16[24,16,1024]{2,1,0:T(8,128)(2,1)S(1)}, u32[]{:S(2)}, u32[]{:S(2)}) %collective-permute-start.6) | collective-permute-done | bytes 786464 | tf_op jit(solution)/shard_map/ppermute | solution.py:318
  92.4 17.8 %collective-permute-done.8.three = bf16[24,16,1024]{2,1,0:T(8,128)(2,1)S(1)} collective-permute-done((bf16[24,16,1024]{2,1,0:T(8,128)(2,1)S(1)}, bf16[24,16,1024]{2,1,0:T(8,128)(2,1)S(1)}, u32[]{:S(2)}, u32[]{:S(2)}) %collective-permute-start.8) | collective-permute-done | bytes 786464 | tf_op jit(solution)/shard_map/ppermute | solution.py:318
  110.2 5.4 %shard_map.58 = (s16[32,16,1152]{2,1,0:T(8,128)(2,1)S(1)}, s16[32,16,1152]{2,1,0:T(8,128)(2,1)S(1)}) custom-call(s32[49]{0:T(128)S(1)} %pad_add_fusion.4.meta, bf16[1,96,32,1024]{3,2,1,0:T(8,128)(2,1)} %gradients.5, bf16[24,16,1024]{2,1,0:T(8,128)(2,1)S(1)} %collective-permute-done.6.one, bf16[24,16,1024]{2,1,0:T(8,128)(2,1)S(1)} %collective-permute-done.7.two, ...), custom_call_target="tpu_custom_call" | custom-call | tf_op jit(solution)/shard_map/pallas_call | solution.py:122
  117.6 27.1 %all_to_all.30.refs_2_ = s16[32,16,1152]{2,1,0:T(8,128)(2,1)} all-to-all(s16[32,16,1152]{2,1,0:T(8,128)(2,1)} %copy-done.7), channel_id=1, replica_groups=mesh['groups'=4,'shard'=32] {'shard'}, dimensions={0} | all-to-all | bytes 2359296 | tf_op jit(solution)/shard_map/all_to_all | solution.py:342
  144.7 4.7 %all-to-all-start.4 = ((s16[32,16,1152]{2,1,0:T(8,128)(2,1)}), s16[32,16,1152]{2,1,0:T(8,128)(2,1)}, u32[]{:S(2)}, u32[]{:S(2)}) async-start(s16[32,16,1152]{2,1,0:T(8,128)(2,1)} %copy-done.6), calls=%async_computation.4 | async-start | bytes 2359296 | tf_op jit(solution)/shard_map/all_to_all | solution.py:342
  150.7 11.2 %shard_map.59 = bf16[1024,1024]{1,0:T(8,128)(2,1)S(1)} custom-call(bf16[1,1,2,2,1024,1024]{5,4,3,2,1,0:T(8,128)(2,1)} %all_roots.3, s16[32,2,8,1152]{3,2,1,0:T(8,128)(2,1)S(1)} %all-to-all-done.refs_0_, s16[32,2,8,1152]{3,2,1,0:T(8,128)(2,1)S(1)} %all-to-all-done.1.refs_1_, s16[32,16,1152]{2,1,0:T(8,128)(2,1)S(1)} %copy-done.4), custom_call_target="tpu_custom_call" | custom-call | tf_op jit(solution)/shard_map/pallas_call | solution.py:193
  163.2 4.7 %all-to-all-done.4.refs_2_ = s16[32,16,1152]{2,1,0:T(8,128)(2,1)} async-done(((s16[32,16,1152]{2,1,0:T(8,128)(2,1)}), s16[32,16,1152]{2,1,0:T(8,128)(2,1)}, u32[]{:S(2)}, u32[]{:S(2)}) %all-to-all-start.4) | async-done | bytes 1179680 | tf_op jit(solution)/shard_map/all_to_all | solution.py:342
  167.9 4.0 %all-to-all-start.3 = ((bf16[32,32,1024]{2,1,0:T(8,128)(2,1)}), bf16[32,32,1024]{2,1,0:T(8,128)(2,1)S(1)}, u32[]{:S(2)}, u32[]{:S(2)}) async-start(bf16[32,32,1024]{2,1,0:T(8,128)(2,1)} %bitcast.50), calls=%async_computation.3 | async-start | bytes 4194304 | tf_op jit(solution)/shard_map/all_to_all | solution.py:342
  174.2 12.4 %shard_map.63 = bf16[1024,1024]{1,0:T(8,128)(2,1)S(1)} custom-call(bf16[1,1,2,2,1024,1024]{5,4,3,2,1,0:T(8,128)(2,1)} %all_roots.3, s16[32,2,8,1152]{3,2,1,0:T(8,128)(2,1)S(1)} %all-to-all-done.refs_0_, s16[32,2,8,1152]{3,2,1,0:T(8,128)(2,1)S(1)} %copy-done.1, s16[32,16,1152]{2,1,0:T(8,128)(2,1)} %all-to-all-done.4.refs_2_), custom_call_target="tpu_custom_call" | custom-call | tf_op jit(solution)/shard_map/pallas_call | solution.py:193
  188.0 12.1 %all-to-all-done.3.refs_0_ = bf16[32,32,1024]{2,1,0:T(8,128)(2,1)S(1)} async-done(((bf16[32,32,1024]{2,1,0:T(8,128)(2,1)}), bf16[32,32,1024]{2,1,0:T(8,128)(2,1)S(1)}, u32[]{:S(2)}, u32[]{:S(2)}) %all-to-all-start.3) | async-done | bytes 2097184 | tf_op jit(solution)/shard_map/all_to_all | solution.py:342
  200.1 5.2 %all-to-all-start.5 = ((bf16[32,32,1024]{2,1,0:T(8,128)(2,1)}), bf16[32,32,1024]{2,1,0:T(8,128)(2,1)}, u32[]{:S(2)}, u32[]{:S(2)}) async-start(bf16[32,32,1024]{2,1,0:T(8,128)(2,1)} %bitcast.49), calls=%async_computation.5 | async-start | bytes 4194304 | tf_op jit(solution)/shard_map/all_to_all | solution.py:342
  207.2 3.7 %shard_map.60 = (bf16[6,32,1024]{2,1,0:T(8,128)(2,1)S(1)}, bf16[6,32,1024]{2,1,0:T(8,128)(2,1)}) custom-call(s32[36]{0:T(128)S(1)} %get-tuple-element.38.table, bf16[24,32,1024]{2,1,0:T(8,128)(2,1)} %weights.3, bf16[32,32,1024]{2,1,0:T(8,128)(2,1)S(1)} %all-to-all-done.3.refs_0_), custom_call_target="tpu_custom_call" | custom-call | tf_op jit(solution)/shard_map/pallas_call | solution.py:235
  213.6 2.7 collective-permute-start.11
  216.3 6.2 %collective-permute-done.9.refs_2_.refs_1_ = bf16[6,32,1024]{2,1,0:T(8,128)(2,1)S(1)} collective-permute-done((bf16[6,32,1024]{2,1,0:T(8,128)(2,1)S(1)}, bf16[6,32,1024]{2,1,0:T(8,128)(2,1)S(1)}, u32[]{:S(2)}, u32[]{:S(2)}) %collective-permute-start.9) | collective-permute-done | bytes 393248 | tf_op jit(solution)/shard_map/ppermute | solution.py:365
  223.7 10.1 %all-to-all-done.5.refs_1_ = bf16[32,32,1024]{2,1,0:T(8,128)(2,1)} async-done(((bf16[32,32,1024]{2,1,0:T(8,128)(2,1)}), bf16[32,32,1024]{2,1,0:T(8,128)(2,1)}, u32[]{:S(2)}, u32[]{:S(2)}) %all-to-all-start.5) | async-done | bytes 2097184 | tf_op jit(solution)/shard_map/all_to_all | solution.py:342
  233.8 4.3 %shard_map.64 = (bf16[6,32,1024]{2,1,0:T(8,128)(2,1)S(1)}, bf16[6,32,1024]{2,1,0:T(8,128)(2,1)S(1)}) custom-call(s32[36]{0:T(128)S(1)} %shard_map.62.table, bf16[24,32,1024]{2,1,0:T(8,128)(2,1)} %weights.3, bf16[32,32,1024]{2,1,0:T(8,128)(2,1)S(1)} %all-to-all-done.3.refs_0_, bf16[32,32,1024]{2,1,0:T(8,128)(2,1)} %all-to-all-done.5.refs_1_), custom_call_target="tpu_custom_call" | custom-call | tf_op jit(solution)/shard_map/pallas_call | solution.py:235
  244.0 5.2 %collective-permute-done.15.refs_2_ = bf16[6,32,1024]{2,1,0:T(8,128)(2,1)S(1)} collective-permute-done((bf16[6,32,1024]{2,1,0:T(8,128)(2,1)S(1)}, bf16[6,32,1024]{2,1,0:T(8,128)(2,1)S(1)}, u32[]{:S(2)}, u32[]{:S(2)}) %collective-permute-start.15) | collective-permute-done | bytes 393248 | tf_op jit(solution)/shard_map/ppermute | solution.py:365
  249.2 2.7 collective-permute-start.20
  251.9 5.1 %collective-permute-done.14.refs_7_ = bf16[6,32,1024]{2,1,0:T(8,128)(2,1)S(1)} collective-permute-done((bf16[6,32,1024]{2,1,0:T(8,128)(2,1)S(1)}, bf16[6,32,1024]{2,1,0:T(8,128)(2,1)S(1)}, u32[]{:S(2)}, u32[]{:S(2)}) %collective-permute-start.14) | collective-permute-done | bytes 393248 | tf_op jit(solution)/shard_map/ppermute | solution.py:370
  257.0 3.4 %shard_map.61.base = bf16[96,32,1024]{2,1,0:T(8,128)(2,1)} custom-call(s32[48]{0:T(128)S(1)} %get-tuple-element.37.place, bf16[6,32,1024]{2,1,0:T(8,128)(2,1)S(1)} %get-tuple-element.57.refs_0_, bf16[6,32,1024]{2,1,0:T(8,128)(2,1)} %get-tuple-element.58.refs_1_, bf16[6,32,1024]{2,1,0:T(8,128)(2,1)S(1)} %collective-permute-done.9.refs_2_.refs_1_, ...), custom_call_target="tpu_custom_call" | custom-call | tf_op jit(solution)/shard_map/pallas_call | solution.py:285
  260.4 5.0 %collective-permute-done.17.refs_4_ = bf16[6,32,1024]{2,1,0:T(8,128)(2,1)S(1)} collective-permute-done((bf16[6,32,1024]{2,1,0:T(8,128)(2,1)S(1)}, bf16[6,32,1024]{2,1,0:T(8,128)(2,1)S(1)}, u32[]{:S(2)}, u32[]{:S(2)}) %collective-permute-start.17) | collective-permute-done | bytes 393248 | tf_op jit(solution)/shard_map/ppermute | solution.py:368
  265.4 2.2 shard_map.65.base
  267.7 6.2 %collective-permute-done.20.refs_1_ = bf16[6,32,1024]{2,1,0:T(8,128)(2,1)S(1)} collective-permute-done((bf16[6,32,1024]{2,1,0:T(8,128)(2,1)S(1)}, bf16[6,32,1024]{2,1,0:T(8,128)(2,1)S(1)}, u32[]{:S(2)}, u32[]{:S(2)}) %collective-permute-start.20) | collective-permute-done | bytes 393248 | tf_op jit(solution)/shard_map/ppermute | solution.py:370
  (75 shorter events, 36.9 us)
Async XLA Ops:
  0.0 6.4 %copy-start.8 = (s32[96]{0:T(128)S(1)}, s32[96]{0:T(128)}, u32[]{:S(2)}) copy-start(s32[96]{0:T(128)} %param.8) | copy-start | bytes 1156
  1.3 11.8 %collective-permute-start = (bf16[24,8,1024]{2,1,0:T(8,128)(2,1)S(1)}, bf16[24,8,1024]{2,1,0:T(8,128)(2,1)S(1)}, u32[]{:S(2)}, u32[]{:S(2)}) collective-permute-start(bf16[24,8,1024]{2,1,0:T(8,128)(2,1)S(1)} %get-tuple-element.39), channel_id=1, source_target_pairs={{0,32},{32,64},{64,96},{96,0},{1,33},{33,65},{65,97},{97,1},{2,34}... | collective-permute-start | bytes 1179656 | tf_op jit(solution)/shard_map/ppermute | solution.py:318
  3.4 9.7 %collective-permute-start.1 = (bf16[24,8,1024]{2,1,0:T(8,128)(2,1)S(1)}, bf16[24,8,1024]{2,1,0:T(8,128)(2,1)S(1)}, u32[]{:S(2)}, u32[]{:S(2)}) collective-permute-start(bf16[24,8,1024]{2,1,0:T(8,128)(2,1)S(1)} %get-tuple-element.40), channel_id=1, source_target_pairs={{0,96},{32,0},{64,32},{96,64},{1,97},{33,1},{65,33},{97,65},{2,98}... | collective-permute-start | bytes 1179656 | tf_op jit(solution)/shard_map/ppermute | solution.py:318
  4.8 18.1 %collective-permute-start.2 = (bf16[24,8,1024]{2,1,0:T(8,128)(2,1)S(1)}, bf16[24,8,1024]{2,1,0:T(8,128)(2,1)S(1)}, u32[]{:S(2)}, u32[]{:S(2)}) collective-permute-start(bf16[24,8,1024]{2,1,0:T(8,128)(2,1)S(1)} %get-tuple-element.41), channel_id=1, source_target_pairs={{0,64},{32,96},{64,0},{96,32},{1,65},{33,97},{65,1},{97,33},{2,66}... | collective-permute-start | bytes 1179656 | tf_op jit(solution)/shard_map/ppermute | solution.py:318
  26.4 35.9 %all-to-all-start = ((s16[32,2,8,1152]{3,2,1,0:T(8,128)(2,1)}), s16[32,2,8,1152]{3,2,1,0:T(8,128)(2,1)S(1)}, u32[]{:S(2)}, u32[]{:S(2)}) async-start(s16[32,2,8,1152]{3,2,1,0:T(8,128)(2,1)} %get-tuple-element.42), calls=%async_computation | async-start | bytes 2359296 | tf_op jit(solution)/shard_map/all_to_all | solution.py:342
  37.3 11.7 %collective-permute-start.3 = (bf16[24,8,1024]{2,1,0:T(8,128)(2,1)S(1)}, bf16[24,8,1024]{2,1,0:T(8,128)(2,1)S(1)}, u32[]{:S(2)}, u32[]{:S(2)}) collective-permute-start(bf16[24,8,1024]{2,1,0:T(8,128)(2,1)S(1)} %get-tuple-element.44), channel_id=1, source_target_pairs={{0,32},{32,64},{64,96},{96,0},{1,33},{33,65},{65,97},{97,1},{2,34}... | collective-permute-start | bytes 1179656 | tf_op jit(solution)/shard_map/ppermute | solution.py:318
  38.3 10.8 %collective-permute-start.4 = (bf16[24,8,1024]{2,1,0:T(8,128)(2,1)S(1)}, bf16[24,8,1024]{2,1,0:T(8,128)(2,1)S(1)}, u32[]{:S(2)}, u32[]{:S(2)}) collective-permute-start(bf16[24,8,1024]{2,1,0:T(8,128)(2,1)S(1)} %get-tuple-element.45), channel_id=1, source_target_pairs={{0,96},{32,0},{64,32},{96,64},{1,97},{33,1},{65,33},{97,65},{2,98}... | collective-permute-start | bytes 1179656 | tf_op jit(solution)/shard_map/ppermute | solution.py:318
  40.1 17.6 %collective-permute-start.5 = (bf16[24,8,1024]{2,1,0:T(8,128)(2,1)S(1)}, bf16[24,8,1024]{2,1,0:T(8,128)(2,1)S(1)}, u32[]{:S(2)}, u32[]{:S(2)}) collective-permute-start(bf16[24,8,1024]{2,1,0:T(8,128)(2,1)S(1)} %get-tuple-element.46), channel_id=1, source_target_pairs={{0,64},{32,96},{64,0},{96,32},{1,65},{33,97},{65,1},{97,33},{2,66}... | collective-permute-start | bytes 1179656 | tf_op jit(solution)/shard_map/ppermute | solution.py:318
  62.3 55.3 %all-to-all-start.1 = ((s16[32,2,8,1152]{3,2,1,0:T(8,128)(2,1)}), s16[32,2,8,1152]{3,2,1,0:T(8,128)(2,1)S(1)}, u32[]{:S(2)}, u32[]{:S(2)}) async-start(s16[32,2,8,1152]{3,2,1,0:T(8,128)(2,1)} %copy-done.5), calls=%async_computation.1 | async-start | bytes 2359296 | tf_op jit(solution)/shard_map/all_to_all | solution.py:342
  72.2 20.1 %collective-permute-start.6 = (bf16[24,16,1024]{2,1,0:T(8,128)(2,1)S(1)}, bf16[24,16,1024]{2,1,0:T(8,128)(2,1)S(1)}, u32[]{:S(2)}, u32[]{:S(2)}) collective-permute-start(bf16[24,16,1024]{2,1,0:T(8,128)(2,1)S(1)} %get-tuple-element.51), channel_id=1, source_target_pairs={{0,32},{32,64},{64,96},{96,0},{1,33},{33,65},{65,97},{97,1},{2,34}... | collective-permute-start | bytes 2359304 | tf_op jit(solution)/shard_map/ppermute | solution.py:318
  73.2 19.2 %collective-permute-start.7 = (bf16[24,16,1024]{2,1,0:T(8,128)(2,1)S(1)}, bf16[24,16,1024]{2,1,0:T(8,128)(2,1)S(1)}, u32[]{:S(2)}, u32[]{:S(2)}) collective-permute-start(bf16[24,16,1024]{2,1,0:T(8,128)(2,1)S(1)} %get-tuple-element.52), channel_id=1, source_target_pairs={{0,96},{32,0},{64,32},{96,64},{1,97},{33,1},{65,33},{97,65},{2,98}... | collective-permute-start | bytes 2359304 | tf_op jit(solution)/shard_map/ppermute | solution.py:318
  75.0 35.2 %collective-permute-start.8 = (bf16[24,16,1024]{2,1,0:T(8,128)(2,1)S(1)}, bf16[24,16,1024]{2,1,0:T(8,128)(2,1)S(1)}, u32[]{:S(2)}, u32[]{:S(2)}) collective-permute-start(bf16[24,16,1024]{2,1,0:T(8,128)(2,1)S(1)} %get-tuple-element.53), channel_id=1, source_target_pairs={{0,64},{32,96},{64,0},{96,32},{1,65},{33,97},{65,1},{97,33},{2,66}... | collective-permute-start | bytes 2359304 | tf_op jit(solution)/shard_map/ppermute | solution.py:318
  117.6 31.8 %copy-start = (s16[32,2,8,1152]{3,2,1,0:T(8,128)(2,1)}, s16[32,2,8,1152]{3,2,1,0:T(8,128)(2,1)S(1)}, u32[]{:S(2)}) copy-start(s16[32,2,8,1152]{3,2,1,0:T(8,128)(2,1)S(1)} %all-to-all-done.1.refs_1_) | copy-start | bytes 3538948
  144.7 23.2 %all-to-all-start.4 = ((s16[32,16,1152]{2,1,0:T(8,128)(2,1)}), s16[32,16,1152]{2,1,0:T(8,128)(2,1)}, u32[]{:S(2)}, u32[]{:S(2)}) async-start(s16[32,16,1152]{2,1,0:T(8,128)(2,1)} %copy-done.6), calls=%async_computation.4 | async-start | bytes 2359296 | tf_op jit(solution)/shard_map/all_to_all | solution.py:342
  149.4 1.3 copy-start.4
  161.9 1.3 copy-start.3
  167.9 32.2 %all-to-all-start.3 = ((bf16[32,32,1024]{2,1,0:T(8,128)(2,1)}), bf16[32,32,1024]{2,1,0:T(8,128)(2,1)S(1)}, u32[]{:S(2)}, u32[]{:S(2)}) async-start(bf16[32,32,1024]{2,1,0:T(8,128)(2,1)} %bitcast.50), calls=%async_computation.3 | async-start | bytes 4194304 | tf_op jit(solution)/shard_map/all_to_all | solution.py:342
  172.9 1.3 copy-start.1
  186.6 1.3 copy-start.2
  200.1 33.6 %all-to-all-start.5 = ((bf16[32,32,1024]{2,1,0:T(8,128)(2,1)}), bf16[32,32,1024]{2,1,0:T(8,128)(2,1)}, u32[]{:S(2)}, u32[]{:S(2)}) async-start(bf16[32,32,1024]{2,1,0:T(8,128)(2,1)} %bitcast.49), calls=%async_computation.5 | async-start | bytes 4194304 | tf_op jit(solution)/shard_map/all_to_all | solution.py:342
  210.9 11.6 %collective-permute-start.9 = (bf16[6,32,1024]{2,1,0:T(8,128)(2,1)S(1)}, bf16[6,32,1024]{2,1,0:T(8,128)(2,1)S(1)}, u32[]{:S(2)}, u32[]{:S(2)}) collective-permute-start(bf16[6,32,1024]{2,1,0:T(8,128)(2,1)S(1)} %get-tuple-element.57.refs_0_), channel_id=1, source_target_pairs={{0,32},{32,64},{64,96},{96,0},{1,33},{33,65},{65,97},{97,1},{2,34}... | collective-permute-start | bytes 1179656 | tf_op jit(solution)/shard_map/ppermute | solution.py:365
  211.8 10.7 %collective-permute-start.12 = (bf16[6,32,1024]{2,1,0:T(8,128)(2,1)}, bf16[6,32,1024]{2,1,0:T(8,128)(2,1)S(1)}, u32[]{:S(2)}, u32[]{:S(2)}) collective-permute-start(bf16[6,32,1024]{2,1,0:T(8,128)(2,1)} %get-tuple-element.58.refs_1_), channel_id=1, source_target_pairs={{0,96},{32,0},{64,32},{96,64},{1,97},{33,1},{65,33},{97,65},{2,98}... | collective-permute-start | bytes 1179656 | tf_op jit(solution)/shard_map/ppermute | solution.py:366
  213.6 27.2 %collective-permute-start.10 = (bf16[6,32,1024]{2,1,0:T(8,128)(2,1)}, bf16[6,32,1024]{2,1,0:T(8,128)(2,1)}, u32[]{:S(2)}, u32[]{:S(2)}) collective-permute-start(bf16[6,32,1024]{2,1,0:T(8,128)(2,1)} %get-tuple-element.58.refs_1_), channel_id=1, source_target_pairs={{0,32},{32,64},{64,96},{96,0},{1,33},{33,65},{65,97},{97,1},{2,34}... | collective-permute-start | bytes 1179656 | tf_op jit(solution)/shard_map/ppermute | solution.py:367
  213.6 27.7 %collective-permute-start.11 = (bf16[6,32,1024]{2,1,0:T(8,128)(2,1)S(1)}, bf16[6,32,1024]{2,1,0:T(8,128)(2,1)}, u32[]{:S(2)}, u32[]{:S(2)}) collective-permute-start(bf16[6,32,1024]{2,1,0:T(8,128)(2,1)S(1)} %get-tuple-element.57.refs_0_), channel_id=1, source_target_pairs={{0,96},{32,0},{64,32},{96,64},{1,97},{33,1},{65,33},{97,65},{2,98}... | collective-permute-start | bytes 1179656 | tf_op jit(solution)/shard_map/ppermute | solution.py:368
  222.5 19.8 %collective-permute-start.13 = (bf16[6,32,1024]{2,1,0:T(8,128)(2,1)S(1)}, bf16[6,32,1024]{2,1,0:T(8,128)(2,1)}, u32[]{:S(2)}, u32[]{:S(2)}) collective-permute-start(bf16[6,32,1024]{2,1,0:T(8,128)(2,1)S(1)} %collective-permute-done.9.refs_2_.refs_1_), channel_id=1, source_target_pairs={{0,32},{32,64},{64,96},{96,0},{1,33},{33,65},{65,97},{97,1},{2,34}... | collective-permute-start | bytes 1179656 | tf_op jit(solution)/shard_map/ppermute | solution.py:369
  238.1 11.1 %collective-permute-start.15 = (bf16[6,32,1024]{2,1,0:T(8,128)(2,1)S(1)}, bf16[6,32,1024]{2,1,0:T(8,128)(2,1)S(1)}, u32[]{:S(2)}, u32[]{:S(2)}) collective-permute-start(bf16[6,32,1024]{2,1,0:T(8,128)(2,1)S(1)} %get-tuple-element.63.refs_0_), channel_id=1, source_target_pairs={{0,32},{32,64},{64,96},{96,0},{1,33},{33,65},{65,97},{97,1},{2,34}... | collective-permute-start | bytes 1179656 | tf_op jit(solution)/shard_map/ppermute | solution.py:365
  239.0 10.2 %collective-permute-start.18 = (bf16[6,32,1024]{2,1,0:T(8,128)(2,1)S(1)}, bf16[6,32,1024]{2,1,0:T(8,128)(2,1)S(1)}, u32[]{:S(2)}, u32[]{:S(2)}) collective-permute-start(bf16[6,32,1024]{2,1,0:T(8,128)(2,1)S(1)} %get-tuple-element.64.refs_1_), channel_id=1, source_target_pairs={{0,96},{32,0},{64,32},{96,64},{1,97},{33,1},{65,33},{97,65},{2,98}... | collective-permute-start | bytes 1179656 | tf_op jit(solution)/shard_map/ppermute | solution.py:366
  240.8 16.2 %collective-permute-start.14 = (bf16[6,32,1024]{2,1,0:T(8,128)(2,1)S(1)}, bf16[6,32,1024]{2,1,0:T(8,128)(2,1)S(1)}, u32[]{:S(2)}, u32[]{:S(2)}) collective-permute-start(bf16[6,32,1024]{2,1,0:T(8,128)(2,1)S(1)} %collective-permute-done.12.refs_5_.refs_2_), channel_id=1, source_target_pairs={{0,96},{32,0},{64,32},{96,64},{1,97},{33,1},{65,33},{97,65},{2,98}... | collective-permute-start | bytes 1179656 | tf_op jit(solution)/shard_map/ppermute | solution.py:370
  241.3 19.1 %collective-permute-start.16 = (bf16[6,32,1024]{2,1,0:T(8,128)(2,1)S(1)}, bf16[6,32,1024]{2,1,0:T(8,128)(2,1)S(1)}, u32[]{:S(2)}, u32[]{:S(2)}) collective-permute-start(bf16[6,32,1024]{2,1,0:T(8,128)(2,1)S(1)} %get-tuple-element.64.refs_1_), channel_id=1, source_target_pairs={{0,32},{32,64},{64,96},{96,0},{1,33},{33,65},{65,97},{97,1},{2,34}... | collective-permute-start | bytes 1179656 | tf_op jit(solution)/shard_map/ppermute | solution.py:367
  242.3 23.1 %collective-permute-start.17 = (bf16[6,32,1024]{2,1,0:T(8,128)(2,1)S(1)}, bf16[6,32,1024]{2,1,0:T(8,128)(2,1)S(1)}, u32[]{:S(2)}, u32[]{:S(2)}) collective-permute-start(bf16[6,32,1024]{2,1,0:T(8,128)(2,1)S(1)} %get-tuple-element.63.refs_0_), channel_id=1, source_target_pairs={{0,96},{32,0},{64,32},{96,64},{1,97},{33,1},{65,33},{97,65},{2,98}... | collective-permute-start | bytes 1179656 | tf_op jit(solution)/shard_map/ppermute | solution.py:368
  249.2 18.5 %collective-permute-start.19 = (bf16[6,32,1024]{2,1,0:T(8,128)(2,1)S(1)}, bf16[6,32,1024]{2,1,0:T(8,128)(2,1)S(1)}, u32[]{:S(2)}, u32[]{:S(2)}) collective-permute-start(bf16[6,32,1024]{2,1,0:T(8,128)(2,1)S(1)} %collective-permute-done.15.refs_2_), channel_id=1, source_target_pairs={{0,32},{32,64},{64,96},{96,0},{1,33},{33,65},{65,97},{97,1},{2,34}... | collective-permute-start | bytes 1179656 | tf_op jit(solution)/shard_map/ppermute | solution.py:369
  249.2 24.6 %collective-permute-start.20 = (bf16[6,32,1024]{2,1,0:T(8,128)(2,1)S(1)}, bf16[6,32,1024]{2,1,0:T(8,128)(2,1)S(1)}, u32[]{:S(2)}, u32[]{:S(2)}) collective-permute-start(bf16[6,32,1024]{2,1,0:T(8,128)(2,1)S(1)} %collective-permute-done.18.refs_5_), channel_id=1, source_target_pairs={{0,96},{32,0},{64,32},{96,64},{1,97},{33,1},{65,33},{97,65},{2,98}... | collective-permute-start | bytes 1179656 | tf_op jit(solution)/shard_map/ppermute | solution.py:370
  (3 other events, 3.1 us)

commit v3 on v2

--- a/solution.py
+++ b/solution.py
@@ -9,7 +9,7 @@
 
 
 LANES = 128
-CHUNKS = (8, 8, 16)
+CHUNKS = (8, 8, 8, 8)
 TALL = 256
 ANY = pl.BlockSpec(memory_space=pl.ANY)
 SMEM = pl.BlockSpec(memory_space=pltpu.SMEM)
@@ -63,11 +63,9 @@
         parts = [total[:, j : j + LANES] for j in range(0, width, LANES)]
         top = functools.reduce(jnp.maximum, [jnp.abs(p) for p in parts])
         if last:
-            top = jnp.maximum(top[:8], top[8:])
+            top = jnp.maximum(top, pltpu.roll(top, 4, 0))
         power = jnp.floor(jnp.log2(jnp.maximum(top, 1e-30)) + 1e-4) - 14.0
         grow = jnp.exp2(-power)
-        if last:
-            grow = jnp.concatenate([grow, grow], axis=0)
         for j, p in enumerate(parts):
             codes[at, :, j * LANES : (j + 1) * LANES] = jnp.round(p * grow).astype(jnp.int32).astype(jnp.int16)
         squares = functools.reduce(jnp.add, [adam[:, j : j + LANES] for j in range(0, width, LANES)])
@@ -82,9 +80,8 @@
         scaled = squares * jnp.exp2(14.0 - scale)
         high = jnp.floor(scaled)
         low = jnp.floor((scaled - high) * 16384.0)
-        row = lax.broadcasted_iota(jnp.int32, (8, LANES), 0)
-        full = jnp.where(row == 0, scale, jnp.where(row == 1, high, low))
-        full = jnp.concatenate([power, full], axis=0)
+        row = lax.broadcasted_iota(jnp.int32, power.shape, 0)
+        full = jnp.where(row < 4, power, jnp.where(row == 4, scale, jnp.where(row == 5, high, low)))
         codes[at, :, width:] = full.astype(jnp.int32).astype(jnp.int16)
 
     def block(at, _):
@@ -142,29 +139,22 @@
     for x in loads:
         x.start()
     n_src = arrived[0].shape[0]
-    early, final = arrived[:-1], arrived[-1]
-    top = sum(a.shape[-2] for a in early)
-    rows = top + final.shape[-2]
-
-    def step_of(powers):
-        return jnp.exp2(powers.astype(jnp.int32).astype(jnp.float32))
+    per = arrived[0].shape[-2]
+    rows = per * len(arrived)
 
     def unpack(n, graft):
-        at = pl.ds(pl.multiple_of(n * rows, rows), top)
-        got = [a[n, slot] for a in early]
-        steps = [step_of(x[:, width:]) for x in got]
-        for j in range(0, width, LANES):
-            value = [x[:, j : j + LANES].astype(jnp.int32).astype(jnp.float32) * t for x, t in zip(got, steps)]
-            high[at, j : j + LANES], low[at, j : j + LANES] = two_parts(jnp.concatenate(value, axis=0))
-        at = pl.ds(pl.multiple_of(n * rows + top, top), rows - top)
-        got = final[n]
-        tail = got[:, width:].astype(jnp.int32).astype(jnp.float32)
-        step = jnp.exp2(tail[:8])
-        step = jnp.concatenate([step, step], axis=0)
-        for j in range(0, width, LANES):
-            value = got[:, j : j + LANES].astype(jnp.int32).astype(jnp.float32) * step
-            high[at, j : j + LANES], low[at, j : j + LANES] = two_parts(value)
-        return graft + jnp.exp2(tail[8:9] - 14.0) * (tail[9:10] + tail[10:11] * (1.0 / 16384.0))
+        codes = [a[n, slot] if len(a.shape) == 4 else a[n] for a in arrived]
+        tails = [x[:, width:].astype(jnp.int32).astype(jnp.float32) for x in codes]
+        norm = tails[-1]
+        row = lax.broadcasted_iota(jnp.int32, norm.shape, 0)
+        tails[-1] = jnp.where(row < 4, norm, pltpu.roll(norm, 4, 0))
+        steps = [jnp.exp2(t) for t in tails]
+        for c in range(0, len(codes), 2):
+            at = pl.ds(pl.multiple_of(n * rows + c * per, 2 * per), 2 * per)
+            for j in range(0, width, LANES):
+                value = [x[:, j : j + LANES].astype(jnp.int32).astype(jnp.float32) * t for x, t in zip(codes[c : c + 2], steps[c : c + 2])]
+                high[at, j : j + LANES], low[at, j : j + LANES] = two_parts(jnp.concatenate(value, axis=0))
+        return graft + jnp.exp2(norm[4:5] - 14.0) * (norm[5:6] + norm[6:7] * (1.0 / 16384.0))
 
     graft = lax.fori_loop(0, n_src, unpack, jnp.zeros((1, LANES), jnp.float32))
     graft = jnp.sum(graft, axis=1, keepdims=True)

time: 278 us -> 284 us (1.022)
  starting transfers between devices: 57.3 us -> 70.2 us
  blocking collectives: 27.1 us -> 19.5 us
  Pallas kernels: 53.6 us -> 57.2 us
    all_to_all x5 -> x6, starting transfers between devices: 31.6 us -> 42.1 us  [exchange(): return lax.all_to_all(x, 'shard', 0, 0, tiled=True)]
    all_to_all x1, blocking collectives: 27.1 us -> 19.5 us  [exchange(): return lax.all_to_all(x, 'shard', 0, 0, tiled=True)]
    all_to_all x5 -> x6, waiting for transfers between devices: 26.9 us -> 21.1 us  [exchange(): return lax.all_to_all(x, 'shard', 0, 0, tiled=True)]
    ppermute x9 -> x12, waiting for transfers between devices: 67.7 us -> 70.9 us  [body(): lax.ppermute(p, 'groups', shift(n))]
    ppermute x9 -> x12, starting transfers between devices: 11.8 us -> 14.5 us  [body(): lax.ppermute(p, 'groups', shift(n))]
    pallas_call x3 -> x4, Pallas kernels: 12.5 us -> 14.7 us  [sum_replicas(): pl.pallas_call(functools.partial(sum_kernel, start, before is None, last)...]
    unnamed x18 -> x16, local copies, waits for them, and re-layouts: 8.23 us -> 6.59 us
  transfers between devices with their start and end apart: 26 -> 30, of which waited for: 14 -> 16; matrix products, arithmetic and copies ran while one was open for 2% -> 2% of each run, Pallas kernels for 18% -> 19%
where the time goes in v3:
time: 284 us; the launch traced here: 281 us
  waiting for transfers between devices  120 us (42%)
  starting transfers between devices  70.2 us (25%)
  Pallas kernels  57.2 us (20%)
  blocking collectives  19.5 us (7%)
  local copies, waits for them, and re-layouts  12.3 us (4%)
    ppermute x12, waiting for transfers between devices, body(): lax.ppermute(p, 'groups', shift(n))  70.9 us
    all_to_all x6, starting transfers between devices, exchange(): return lax.all_to_all(x, 'shard', 0, 0, tiled=True)  42.1 us
    pallas_call x2, Pallas kernels, owner_work(): pl.pallas_call(functools.partial(owner_kernel, slot), out_shape=jax.Shape...  24.9 us
    all_to_all x6, waiting for transfers between devices, exchange(): return lax.all_to_all(x, 'shard', 0, 0, tiled=True)  21.1 us
    all_to_all x1, blocking collectives, exchange(): return lax.all_to_all(x, 'shard', 0, 0, tiled=True)  19.5 us
    pallas_call x4, Pallas kernels, sum_replicas(): pl.pallas_call(functools.partial(sum_kernel, start, before is None, last)...  14.7 us
    ppermute x12, starting transfers between devices, body(): lax.ppermute(p, 'groups', shift(n))  14.5 us
    ppermute x2, waiting for transfers between devices, to_all(): prev_a = lax.ppermute(a, 'groups', shift(1))  12 us
  transfers between devices with their start and end apart: 30, of which 16 were waited for; matrix products, arithmetic and copies ran while one was open for 2% of the time, Pallas kernels for 19%

profile of v3, /device:TPU:1, one launch (start us, length us, event | category | flops | bytes accessed | tf_op | source)
XLA Modules:
  0.0 281.1 jit_solution(8963187752647466443)
XLA Ops:
  6.8 6.4 %collective-permute-done.one = bf16[24,8,1024]{2,1,0:T(8,128)(2,1)S(1)} collective-permute-done((bf16[24,8,1024]{2,1,0:T(8,128)(2,1)S(1)}, bf16[24,8,1024]{2,1,0:T(8,128)(2,1)S(1)}, u32[]{:S(2)}, u32[]{:S(2)}) %collective-permute-start) | collective-permute-done | bytes 393248 | tf_op jit(solution)/shard_map/ppermute | solution.py:308
  13.2 9.7 %collective-permute-done.2.three = bf16[24,8,1024]{2,1,0:T(8,128)(2,1)S(1)} collective-permute-done((bf16[24,8,1024]{2,1,0:T(8,128)(2,1)S(1)}, bf16[24,8,1024]{2,1,0:T(8,128)(2,1)S(1)}, u32[]{:S(2)}, u32[]{:S(2)}) %collective-permute-start.2) | collective-permute-done | bytes 393248 | tf_op jit(solution)/shard_map/ppermute | solution.py:308
  22.8 3.5 %shard_map.56 = (s16[32,2,8,1152]{3,2,1,0:T(8,128)(2,1)}, f32[24,1,128]{2,1,0:T(1,128)S(1)}) custom-call(s32[49]{0:T(128)S(1)} %pad_add_fusion.4.meta, bf16[1,96,32,1024]{3,2,1,0:T(8,128)(2,1)} %gradients.7, bf16[24,8,1024]{2,1,0:T(8,128)(2,1)S(1)} %collective-permute-done.one, bf16[24,8,1024]{2,1,0:T(8,128)(2,1)S(1)} %collective-permute-done.1.two, ...), custom_call_target="tpu_custom_call" | custom-call | tf_op jit(solution)/shard_map/pallas_call | solution.py:119
  26.4 9.6 %all-to-all-start = ((s16[32,2,8,1152]{3,2,1,0:T(8,128)(2,1)}), s16[32,2,8,1152]{3,2,1,0:T(8,128)(2,1)S(1)}, u32[]{:S(2)}, u32[]{:S(2)}) async-start(s16[32,2,8,1152]{3,2,1,0:T(8,128)(2,1)} %get-tuple-element.49), calls=%async_computation | async-start | bytes 2359296 | tf_op jit(solution)/shard_map/all_to_all | solution.py:332
  40.3 8.8 %collective-permute-done.3.one = bf16[24,8,1024]{2,1,0:T(8,128)(2,1)S(1)} collective-permute-done((bf16[24,8,1024]{2,1,0:T(8,128)(2,1)S(1)}, bf16[24,8,1024]{2,1,0:T(8,128)(2,1)S(1)}, u32[]{:S(2)}, u32[]{:S(2)}) %collective-permute-start.3) | collective-permute-done | bytes 393248 | tf_op jit(solution)/shard_map/ppermute | solution.py:308
  49.1 8.6 %collective-permute-done.5.three = bf16[24,8,1024]{2,1,0:T(8,128)(2,1)S(1)} collective-permute-done((bf16[24,8,1024]{2,1,0:T(8,128)(2,1)S(1)}, bf16[24,8,1024]{2,1,0:T(8,128)(2,1)S(1)}, u32[]{:S(2)}, u32[]{:S(2)}) %collective-permute-start.5) | collective-permute-done | bytes 393248 | tf_op jit(solution)/shard_map/ppermute | solution.py:308
  57.7 3.5 %shard_map.57 = (s16[32,2,8,1152]{3,2,1,0:T(8,128)(2,1)}, f32[24,1,128]{2,1,0:T(1,128)S(1)}) custom-call(s32[49]{0:T(128)S(1)} %pad_add_fusion.4.meta, bf16[1,96,32,1024]{3,2,1,0:T(8,128)(2,1)} %gradients.7, bf16[24,8,1024]{2,1,0:T(8,128)(2,1)S(1)} %collective-permute-done.3.one, bf16[24,8,1024]{2,1,0:T(8,128)(2,1)S(1)} %collective-permute-done.4.two, ...), custom_call_target="tpu_custom_call" | custom-call | tf_op jit(solution)/shard_map/pallas_call | solution.py:119
  61.2 8.1 %all-to-all-start.1 = ((s16[32,2,8,1152]{3,2,1,0:T(8,128)(2,1)}), s16[32,2,8,1152]{3,2,1,0:T(8,128)(2,1)S(1)}, u32[]{:S(2)}, u32[]{:S(2)}) async-start(s16[32,2,8,1152]{3,2,1,0:T(8,128)(2,1)} %get-tuple-element.56), calls=%async_computation.1 | async-start | bytes 2359296 | tf_op jit(solution)/shard_map/all_to_all | solution.py:332
  74.4 8.0 %collective-permute-done.6.one = bf16[24,8,1024]{2,1,0:T(8,128)(2,1)S(1)} collective-permute-done((bf16[24,8,1024]{2,1,0:T(8,128)(2,1)S(1)}, bf16[24,8,1024]{2,1,0:T(8,128)(2,1)S(1)}, u32[]{:S(2)}, u32[]{:S(2)}) %collective-permute-start.6) | collective-permute-done | bytes 393248 | tf_op jit(solution)/shard_map/ppermute | solution.py:308
  82.4 9.4 %collective-permute-done.8.three = bf16[24,8,1024]{2,1,0:T(8,128)(2,1)S(1)} collective-permute-done((bf16[24,8,1024]{2,1,0:T(8,128)(2,1)S(1)}, bf16[24,8,1024]{2,1,0:T(8,128)(2,1)S(1)}, u32[]{:S(2)}, u32[]{:S(2)}) %collective-permute-start.8) | collective-permute-done | bytes 393248 | tf_op jit(solution)/shard_map/ppermute | solution.py:308
  91.8 3.5 %shard_map.58 = (s16[32,2,8,1152]{3,2,1,0:T(8,128)(2,1)}, f32[24,1,128]{2,1,0:T(1,128)S(1)}) custom-call(s32[49]{0:T(128)S(1)} %pad_add_fusion.4.meta, bf16[1,96,32,1024]{3,2,1,0:T(8,128)(2,1)} %gradients.7, bf16[24,8,1024]{2,1,0:T(8,128)(2,1)S(1)} %collective-permute-done.6.one, bf16[24,8,1024]{2,1,0:T(8,128)(2,1)S(1)} %collective-permute-done.7.two, ...), custom_call_target="tpu_custom_call" | custom-call | tf_op jit(solution)/shard_map/pallas_call | solution.py:119
  95.4 8.1 %all-to-all-start.2 = ((s16[32,2,8,1152]{3,2,1,0:T(8,128)(2,1)}), s16[32,2,8,1152]{3,2,1,0:T(8,128)(2,1)}, u32[]{:S(2)}, u32[]{:S(2)}) async-start(s16[32,2,8,1152]{3,2,1,0:T(8,128)(2,1)} %get-tuple-element.63), calls=%async_computation.2 | async-start | bytes 2359296 | tf_op jit(solution)/shard_map/all_to_all | solution.py:332
  107.6 7.8 %collective-permute-done.10.two = bf16[24,8,1024]{2,1,0:T(8,128)(2,1)S(1)} collective-permute-done((bf16[24,8,1024]{2,1,0:T(8,128)(2,1)S(1)}, bf16[24,8,1024]{2,1,0:T(8,128)(2,1)S(1)}, u32[]{:S(2)}, u32[]{:S(2)}) %collective-permute-start.10) | collective-permute-done | bytes 393248 | tf_op jit(solution)/shard_map/ppermute | solution.py:308
  115.4 3.0 %collective-permute-done.11.three = bf16[24,8,1024]{2,1,0:T(8,128)(2,1)S(1)} collective-permute-done((bf16[24,8,1024]{2,1,0:T(8,128)(2,1)S(1)}, bf16[24,8,1024]{2,1,0:T(8,128)(2,1)S(1)}, u32[]{:S(2)}, u32[]{:S(2)}) %collective-permute-start.11) | collective-permute-done | bytes 393248 | tf_op jit(solution)/shard_map/ppermute | solution.py:308
  118.4 9.2 %collective-permute-done.9.one = bf16[24,8,1024]{2,1,0:T(8,128)(2,1)S(1)} collective-permute-done((bf16[24,8,1024]{2,1,0:T(8,128)(2,1)S(1)}, bf16[24,8,1024]{2,1,0:T(8,128)(2,1)S(1)}, u32[]{:S(2)}, u32[]{:S(2)}) %collective-permute-start.9) | collective-permute-done | bytes 393248 | tf_op jit(solution)/shard_map/ppermute | solution.py:308
  127.6 4.1 %shard_map.59 = (s16[32,8,1152]{2,1,0:T(8,128)(2,1)S(1)}, s16[32,8,1152]{2,1,0:T(8,128)(2,1)S(1)}) custom-call(s32[49]{0:T(128)S(1)} %pad_add_fusion.4.meta, bf16[1,96,32,1024]{3,2,1,0:T(8,128)(2,1)} %gradients.7, bf16[24,8,1024]{2,1,0:T(8,128)(2,1)S(1)} %collective-permute-done.9.one, bf16[24,8,1024]{2,1,0:T(8,128)(2,1)S(1)} %collective-permute-done.10.two, ...), custom_call_target="tpu_custom_call" | custom-call | tf_op jit(solution)/shard_map/pallas_call | solution.py:119
  132.5 19.5 %all_to_all.35.refs_3_ = s16[32,8,1152]{2,1,0:T(8,128)(2,1)S(1)} all-to-all(s16[32,8,1152]{2,1,0:T(8,128)(2,1)S(1)} %get-tuple-element.70), channel_id=1, replica_groups=mesh['groups'=4,'shard'=32] {'shard'}, dimensions={0} | all-to-all | bytes 1179648 | tf_op jit(solution)/shard_map/all_to_all | solution.py:332
  152.0 3.9 %all-to-all-start.5 = ((s16[32,8,1152]{2,1,0:T(8,128)(2,1)}), s16[32,8,1152]{2,1,0:T(8,128)(2,1)S(1)}, u32[]{:S(2)}, u32[]{:S(2)}) async-start(s16[32,8,1152]{2,1,0:T(8,128)(2,1)} %copy-done.6), calls=%async_computation.5 | async-start | bytes 1179648 | tf_op jit(solution)/shard_map/all_to_all | solution.py:332
  155.9 12.4 %shard_map.60 = bf16[1024,1024]{1,0:T(8,128)(2,1)S(1)} custom-call(bf16[1,1,2,2,1024,1024]{5,4,3,2,1,0:T(8,128)(2,1)} %all_roots.3, s16[32,2,8,1152]{3,2,1,0:T(8,128)(2,1)S(1)} %all-to-all-done.refs_0_, s16[32,2,8,1152]{3,2,1,0:T(8,128)(2,1)S(1)} %all-to-all-done.1.refs_1_, s16[32,2,8,1152]{3,2,1,0:T(8,128)(2,1)} %all-to-all-done.2.refs_2_, ...), custom_call_target="tpu_custom_call" | custom-call | tf_op jit(solution)/shard_map/pallas_call | solution.py:183
  170.5 7.2 %all-to-all-start.4 = ((bf16[32,32,1024]{2,1,0:T(8,128)(2,1)}), bf16[32,32,1024]{2,1,0:T(8,128)(2,1)S(1)}, u32[]{:S(2)}, u32[]{:S(2)}) async-start(bf16[32,32,1024]{2,1,0:T(8,128)(2,1)} %bitcast.56), calls=%async_computation.4 | async-start | bytes 4194304 | tf_op jit(solution)/shard_map/all_to_all | solution.py:332
  181.0 12.4 %shard_map.64 = bf16[1024,1024]{1,0:T(8,128)(2,1)S(1)} custom-call(bf16[1,1,2,2,1024,1024]{5,4,3,2,1,0:T(8,128)(2,1)} %all_roots.3, s16[32,2,8,1152]{3,2,1,0:T(8,128)(2,1)S(1)} %all-to-all-done.refs_0_, s16[32,2,8,1152]{3,2,1,0:T(8,128)(2,1)S(1)} %copy-done.1, s16[32,2,8,1152]{3,2,1,0:T(8,128)(2,1)} %all-to-all-done.2.refs_2_, s16[32,8,1152]{2,1,0:T(8,128)(2,1)S(1)} %copy-done.5), custom_call_target="tpu_custom_call" | custom-call | tf_op jit(solution)/shard_map/pallas_call | solution.py:183
  194.8 11.2 %all-to-all-done.4.refs_0_ = bf16[32,32,1024]{2,1,0:T(8,128)(2,1)S(1)} async-done(((bf16[32,32,1024]{2,1,0:T(8,128)(2,1)}), bf16[32,32,1024]{2,1,0:T(8,128)(2,1)S(1)}, u32[]{:S(2)}, u32[]{:S(2)}) %all-to-all-start.4) | async-done | bytes 2097184 | tf_op jit(solution)/shard_map/all_to_all | solution.py:332
  206.0 5.2 %all-to-all-start.6 = ((bf16[32,32,1024]{2,1,0:T(8,128)(2,1)}), bf16[32,32,1024]{2,1,0:T(8,128)(2,1)}, u32[]{:S(2)}, u32[]{:S(2)}) async-start(bf16[32,32,1024]{2,1,0:T(8,128)(2,1)} %bitcast.55), calls=%async_computation.6 | async-start | bytes 4194304 | tf_op jit(solution)/shard_map/all_to_all | solution.py:332
  213.1 3.7 %shard_map.61 = (bf16[6,32,1024]{2,1,0:T(8,128)(2,1)}, bf16[6,32,1024]{2,1,0:T(8,128)(2,1)}) custom-call(s32[36]{0:T(128)S(1)} %get-tuple-element.45.table, bf16[24,32,1024]{2,1,0:T(8,128)(2,1)} %weights.3, bf16[32,32,1024]{2,1,0:T(8,128)(2,1)S(1)} %all-to-all-done.4.refs_0_), custom_call_target="tpu_custom_call" | custom-call | tf_op jit(solution)/shard_map/pallas_call | solution.py:225
  222.2 6.4 %collective-permute-done.12.refs_2_.refs_1_ = bf16[6,32,1024]{2,1,0:T(8,128)(2,1)S(1)} collective-permute-done((bf16[6,32,1024]{2,1,0:T(8,128)(2,1)}, bf16[6,32,1024]{2,1,0:T(8,128)(2,1)S(1)}, u32[]{:S(2)}, u32[]{:S(2)}) %collective-permute-start.12) | collective-permute-done | bytes 393248 | tf_op jit(solution)/shard_map/ppermute | solution.py:355
  229.8 9.8 %all-to-all-done.6.refs_1_ = bf16[32,32,1024]{2,1,0:T(8,128)(2,1)} async-done(((bf16[32,32,1024]{2,1,0:T(8,128)(2,1)}), bf16[32,32,1024]{2,1,0:T(8,128)(2,1)}, u32[]{:S(2)}, u32[]{:S(2)}) %all-to-all-start.6) | async-done | bytes 2097184 | tf_op jit(solution)/shard_map/all_to_all | solution.py:332
  239.7 4.3 %shard_map.65 = (bf16[6,32,1024]{2,1,0:T(8,128)(2,1)S(1)}, bf16[6,32,1024]{2,1,0:T(8,128)(2,1)S(1)}) custom-call(s32[36]{0:T(128)S(1)} %shard_map.63.table, bf16[24,32,1024]{2,1,0:T(8,128)(2,1)} %weights.3, bf16[32,32,1024]{2,1,0:T(8,128)(2,1)S(1)} %all-to-all-done.4.refs_0_, bf16[32,32,1024]{2,1,0:T(8,128)(2,1)} %all-to-all-done.6.refs_1_), custom_call_target="tpu_custom_call" | custom-call | tf_op jit(solution)/shard_map/pallas_call | solution.py:225
  249.5 5.6 %collective-permute-done.18.refs_2_ = bf16[6,32,1024]{2,1,0:T(8,128)(2,1)S(1)} collective-permute-done((bf16[6,32,1024]{2,1,0:T(8,128)(2,1)S(1)}, bf16[6,32,1024]{2,1,0:T(8,128)(2,1)S(1)}, u32[]{:S(2)}, u32[]{:S(2)}) %collective-permute-start.18) | collective-permute-done | bytes 393248 | tf_op jit(solution)/shard_map/ppermute | solution.py:355
  257.8 4.7 %collective-permute-done.17.refs_7_ = bf16[6,32,1024]{2,1,0:T(8,128)(2,1)S(1)} collective-permute-done((bf16[6,32,1024]{2,1,0:T(8,128)(2,1)S(1)}, bf16[6,32,1024]{2,1,0:T(8,128)(2,1)S(1)}, u32[]{:S(2)}, u32[]{:S(2)}) %collective-permute-start.17) | collective-permute-done | bytes 393248 | tf_op jit(solution)/shard_map/ppermute | solution.py:360
  262.5 3.5 %shard_map.62.base = bf16[96,32,1024]{2,1,0:T(8,128)(2,1)} custom-call(s32[48]{0:T(128)S(1)} %get-tuple-element.44.place, bf16[6,32,1024]{2,1,0:T(8,128)(2,1)} %get-tuple-element.71.refs_0_, bf16[6,32,1024]{2,1,0:T(8,128)(2,1)} %get-tuple-element.72.refs_1_, bf16[6,32,1024]{2,1,0:T(8,128)(2,1)S(1)} %collective-permute-done.12.refs_2_.refs_1_, ...), custom_call_target="tpu_custom_call" | custom-call | tf_op jit(solution)/shard_map/pallas_call | solution.py:275
  266.1 4.9 %collective-permute-done.20.refs_4_ = bf16[6,32,1024]{2,1,0:T(8,128)(2,1)S(1)} collective-permute-done((bf16[6,32,1024]{2,1,0:T(8,128)(2,1)S(1)}, bf16[6,32,1024]{2,1,0:T(8,128)(2,1)S(1)}, u32[]{:S(2)}, u32[]{:S(2)}) %collective-permute-start.20) | collective-permute-done | bytes 393248 | tf_op jit(solution)/shard_map/ppermute | solution.py:358
  273.2 6.2 %collective-permute-done.23.refs_1_ = bf16[6,32,1024]{2,1,0:T(8,128)(2,1)S(1)} collective-permute-done((bf16[6,32,1024]{2,1,0:T(8,128)(2,1)S(1)}, bf16[6,32,1024]{2,1,0:T(8,128)(2,1)S(1)}, u32[]{:S(2)}, u32[]{:S(2)}) %collective-permute-start.23) | collective-permute-done | bytes 393248 | tf_op jit(solution)/shard_map/ppermute | solution.py:360
  (83 shorter events, 48.1 us)
Async XLA Ops:
  0.0 6.4 %copy-start.7 = (s32[96]{0:T(128)S(1)}, s32[96]{0:T(128)}, u32[]{:S(2)}) copy-start(s32[96]{0:T(128)} %param.8) | copy-start | bytes 1156
  1.3 11.8 %collective-permute-start = (bf16[24,8,1024]{2,1,0:T(8,128)(2,1)S(1)}, bf16[24,8,1024]{2,1,0:T(8,128)(2,1)S(1)}, u32[]{:S(2)}, u32[]{:S(2)}) collective-permute-start(bf16[24,8,1024]{2,1,0:T(8,128)(2,1)S(1)} %get-tuple-element.46), channel_id=1, source_target_pairs={{0,32},{32,64},{64,96},{96,0},{1,33},{33,65},{65,97},{97,1},{2,34}... | collective-permute-start | bytes 1179656 | tf_op jit(solution)/shard_map/ppermute | solution.py:308
  3.4 9.7 %collective-permute-start.1 = (bf16[24,8,1024]{2,1,0:T(8,128)(2,1)S(1)}, bf16[24,8,1024]{2,1,0:T(8,128)(2,1)S(1)}, u32[]{:S(2)}, u32[]{:S(2)}) collective-permute-start(bf16[24,8,1024]{2,1,0:T(8,128)(2,1)S(1)} %get-tuple-element.47), channel_id=1, source_target_pairs={{0,96},{32,0},{64,32},{96,64},{1,97},{33,1},{65,33},{97,65},{2,98}... | collective-permute-start | bytes 1179656 | tf_op jit(solution)/shard_map/ppermute | solution.py:308
  4.8 18.1 %collective-permute-start.2 = (bf16[24,8,1024]{2,1,0:T(8,128)(2,1)S(1)}, bf16[24,8,1024]{2,1,0:T(8,128)(2,1)S(1)}, u32[]{:S(2)}, u32[]{:S(2)}) collective-permute-start(bf16[24,8,1024]{2,1,0:T(8,128)(2,1)S(1)} %get-tuple-element.48), channel_id=1, source_target_pairs={{0,64},{32,96},{64,0},{96,32},{1,65},{33,97},{65,1},{97,33},{2,66}... | collective-permute-start | bytes 1179656 | tf_op jit(solution)/shard_map/ppermute | solution.py:308
  26.4 34.9 %all-to-all-start = ((s16[32,2,8,1152]{3,2,1,0:T(8,128)(2,1)}), s16[32,2,8,1152]{3,2,1,0:T(8,128)(2,1)S(1)}, u32[]{:S(2)}, u32[]{:S(2)}) async-start(s16[32,2,8,1152]{3,2,1,0:T(8,128)(2,1)} %get-tuple-element.49), calls=%async_computation | async-start | bytes 2359296 | tf_op jit(solution)/shard_map/all_to_all | solution.py:332
  37.3 11.7 %collective-permute-start.3 = (bf16[24,8,1024]{2,1,0:T(8,128)(2,1)S(1)}, bf16[24,8,1024]{2,1,0:T(8,128)(2,1)S(1)}, u32[]{:S(2)}, u32[]{:S(2)}) collective-permute-start(bf16[24,8,1024]{2,1,0:T(8,128)(2,1)S(1)} %get-tuple-element.51), channel_id=1, source_target_pairs={{0,32},{32,64},{64,96},{96,0},{1,33},{33,65},{65,97},{97,1},{2,34}... | collective-permute-start | bytes 1179656 | tf_op jit(solution)/shard_map/ppermute | solution.py:308
  38.3 10.8 %collective-permute-start.4 = (bf16[24,8,1024]{2,1,0:T(8,128)(2,1)S(1)}, bf16[24,8,1024]{2,1,0:T(8,128)(2,1)S(1)}, u32[]{:S(2)}, u32[]{:S(2)}) collective-permute-start(bf16[24,8,1024]{2,1,0:T(8,128)(2,1)S(1)} %get-tuple-element.52), channel_id=1, source_target_pairs={{0,96},{32,0},{64,32},{96,64},{1,97},{33,1},{65,33},{97,65},{2,98}... | collective-permute-start | bytes 1179656 | tf_op jit(solution)/shard_map/ppermute | solution.py:308
  40.1 17.6 %collective-permute-start.5 = (bf16[24,8,1024]{2,1,0:T(8,128)(2,1)S(1)}, bf16[24,8,1024]{2,1,0:T(8,128)(2,1)S(1)}, u32[]{:S(2)}, u32[]{:S(2)}) collective-permute-start(bf16[24,8,1024]{2,1,0:T(8,128)(2,1)S(1)} %get-tuple-element.53), channel_id=1, source_target_pairs={{0,64},{32,96},{64,0},{96,32},{1,65},{33,97},{65,1},{97,33},{2,66}... | collective-permute-start | bytes 1179656 | tf_op jit(solution)/shard_map/ppermute | solution.py:308
  61.2 34.1 %all-to-all-start.1 = ((s16[32,2,8,1152]{3,2,1,0:T(8,128)(2,1)}), s16[32,2,8,1152]{3,2,1,0:T(8,128)(2,1)S(1)}, u32[]{:S(2)}, u32[]{:S(2)}) async-start(s16[32,2,8,1152]{3,2,1,0:T(8,128)(2,1)} %get-tuple-element.56), calls=%async_computation.1 | async-start | bytes 2359296 | tf_op jit(solution)/shard_map/all_to_all | solution.py:332
  70.7 11.7 %collective-permute-start.6 = (bf16[24,8,1024]{2,1,0:T(8,128)(2,1)S(1)}, bf16[24,8,1024]{2,1,0:T(8,128)(2,1)S(1)}, u32[]{:S(2)}, u32[]{:S(2)}) collective-permute-start(bf16[24,8,1024]{2,1,0:T(8,128)(2,1)S(1)} %get-tuple-element.58), channel_id=1, source_target_pairs={{0,32},{32,64},{64,96},{96,0},{1,33},{33,65},{65,97},{97,1},{2,34}... | collective-permute-start | bytes 1179656 | tf_op jit(solution)/shard_map/ppermute | solution.py:308
  71.6 10.8 %collective-permute-start.7 = (bf16[24,8,1024]{2,1,0:T(8,128)(2,1)S(1)}, bf16[24,8,1024]{2,1,0:T(8,128)(2,1)S(1)}, u32[]{:S(2)}, u32[]{:S(2)}) collective-permute-start(bf16[24,8,1024]{2,1,0:T(8,128)(2,1)S(1)} %get-tuple-element.59), channel_id=1, source_target_pairs={{0,96},{32,0},{64,32},{96,64},{1,97},{33,1},{65,33},{97,65},{2,98}... | collective-permute-start | bytes 1179656 | tf_op jit(solution)/shard_map/ppermute | solution.py:308
  73.4 18.4 %collective-permute-start.8 = (bf16[24,8,1024]{2,1,0:T(8,128)(2,1)S(1)}, bf16[24,8,1024]{2,1,0:T(8,128)(2,1)S(1)}, u32[]{:S(2)}, u32[]{:S(2)}) collective-permute-start(bf16[24,8,1024]{2,1,0:T(8,128)(2,1)S(1)} %get-tuple-element.60), channel_id=1, source_target_pairs={{0,64},{32,96},{64,0},{96,32},{1,65},{33,97},{65,1},{97,33},{2,66}... | collective-permute-start | bytes 1179656 | tf_op jit(solution)/shard_map/ppermute | solution.py:308
  95.4 60.5 %copy-start = (s16[32,2,8,1152]{3,2,1,0:T(8,128)(2,1)}, s16[32,2,8,1152]{3,2,1,0:T(8,128)(2,1)S(1)}, u32[]{:S(2)}) copy-start(s16[32,2,8,1152]{3,2,1,0:T(8,128)(2,1)S(1)} %all-to-all-done.1.refs_1_) | copy-start | bytes 3538948
  95.4 37.1 %all-to-all-start.2 = ((s16[32,2,8,1152]{3,2,1,0:T(8,128)(2,1)}), s16[32,2,8,1152]{3,2,1,0:T(8,128)(2,1)}, u32[]{:S(2)}, u32[]{:S(2)}) async-start(s16[32,2,8,1152]{3,2,1,0:T(8,128)(2,1)} %get-tuple-element.63), calls=%async_computation.2 | async-start | bytes 2359296 | tf_op jit(solution)/shard_map/all_to_all | solution.py:332
  104.9 10.5 %collective-permute-start.10 = (bf16[24,8,1024]{2,1,0:T(8,128)(2,1)S(1)}, bf16[24,8,1024]{2,1,0:T(8,128)(2,1)S(1)}, u32[]{:S(2)}, u32[]{:S(2)}) collective-permute-start(bf16[24,8,1024]{2,1,0:T(8,128)(2,1)S(1)} %get-tuple-element.66), channel_id=1, source_target_pairs={{0,96},{32,0},{64,32},{96,64},{1,97},{33,1},{65,33},{97,65},{2,98}... | collective-permute-start | bytes 1179656 | tf_op jit(solution)/shard_map/ppermute | solution.py:308
  106.6 11.7 %collective-permute-start.11 = (bf16[24,8,1024]{2,1,0:T(8,128)(2,1)S(1)}, bf16[24,8,1024]{2,1,0:T(8,128)(2,1)S(1)}, u32[]{:S(2)}, u32[]{:S(2)}) collective-permute-start(bf16[24,8,1024]{2,1,0:T(8,128)(2,1)S(1)} %get-tuple-element.67), channel_id=1, source_target_pairs={{0,64},{32,96},{64,0},{96,32},{1,65},{33,97},{65,1},{97,33},{2,66}... | collective-permute-start | bytes 1179656 | tf_op jit(solution)/shard_map/ppermute | solution.py:308
  107.6 20.0 %collective-permute-start.9 = (bf16[24,8,1024]{2,1,0:T(8,128)(2,1)S(1)}, bf16[24,8,1024]{2,1,0:T(8,128)(2,1)S(1)}, u32[]{:S(2)}, u32[]{:S(2)}) collective-permute-start(bf16[24,8,1024]{2,1,0:T(8,128)(2,1)S(1)} %get-tuple-element.65), channel_id=1, source_target_pairs={{0,32},{32,64},{64,96},{96,0},{1,33},{33,65},{65,97},{97,1},{2,34}... | collective-permute-start | bytes 1179656 | tf_op jit(solution)/shard_map/ppermute | solution.py:308
  152.0 17.6 %all-to-all-start.5 = ((s16[32,8,1152]{2,1,0:T(8,128)(2,1)}), s16[32,8,1152]{2,1,0:T(8,128)(2,1)S(1)}, u32[]{:S(2)}, u32[]{:S(2)}) async-start(s16[32,8,1152]{2,1,0:T(8,128)(2,1)} %copy-done.6), calls=%async_computation.5 | async-start | bytes 1179648 | tf_op jit(solution)/shard_map/all_to_all | solution.py:332
  170.5 35.5 %all-to-all-start.4 = ((bf16[32,32,1024]{2,1,0:T(8,128)(2,1)}), bf16[32,32,1024]{2,1,0:T(8,128)(2,1)S(1)}, u32[]{:S(2)}, u32[]{:S(2)}) async-start(bf16[32,32,1024]{2,1,0:T(8,128)(2,1)} %bitcast.56), calls=%async_computation.4 | async-start | bytes 4194304 | tf_op jit(solution)/shard_map/all_to_all | solution.py:332
  206.0 33.6 %all-to-all-start.6 = ((bf16[32,32,1024]{2,1,0:T(8,128)(2,1)}), bf16[32,32,1024]{2,1,0:T(8,128)(2,1)}, u32[]{:S(2)}, u32[]{:S(2)}) async-start(bf16[32,32,1024]{2,1,0:T(8,128)(2,1)} %bitcast.55), calls=%async_computation.6 | async-start | bytes 4194304 | tf_op jit(solution)/shard_map/all_to_all | solution.py:332
  216.8 11.8 %collective-permute-start.12 = (bf16[6,32,1024]{2,1,0:T(8,128)(2,1)}, bf16[6,32,1024]{2,1,0:T(8,128)(2,1)S(1)}, u32[]{:S(2)}, u32[]{:S(2)}) collective-permute-start(bf16[6,32,1024]{2,1,0:T(8,128)(2,1)} %get-tuple-element.71.refs_0_), channel_id=1, source_target_pairs={{0,32},{32,64},{64,96},{96,0},{1,33},{33,65},{65,97},{97,1},{2,34}... | collective-permute-start | bytes 1179656 | tf_op jit(solution)/shard_map/ppermute | solution.py:355
  216.9 11.8 %collective-permute-start.15 = (bf16[6,32,1024]{2,1,0:T(8,128)(2,1)}, bf16[6,32,1024]{2,1,0:T(8,128)(2,1)S(1)}, u32[]{:S(2)}, u32[]{:S(2)}) collective-permute-start(bf16[6,32,1024]{2,1,0:T(8,128)(2,1)} %get-tuple-element.72.refs_1_), channel_id=1, source_target_pairs={{0,96},{32,0},{64,32},{96,64},{1,97},{33,1},{65,33},{97,65},{2,98}... | collective-permute-start | bytes 1179656 | tf_op jit(solution)/shard_map/ppermute | solution.py:356
  219.6 27.1 %collective-permute-start.13 = (bf16[6,32,1024]{2,1,0:T(8,128)(2,1)}, bf16[6,32,1024]{2,1,0:T(8,128)(2,1)}, u32[]{:S(2)}, u32[]{:S(2)}) collective-permute-start(bf16[6,32,1024]{2,1,0:T(8,128)(2,1)} %get-tuple-element.72.refs_1_), channel_id=1, source_target_pairs={{0,32},{32,64},{64,96},{96,0},{1,33},{33,65},{65,97},{97,1},{2,34}... | collective-permute-start | bytes 1179656 | tf_op jit(solution)/shard_map/ppermute | solution.py:357
  219.6 27.2 %collective-permute-start.14 = (bf16[6,32,1024]{2,1,0:T(8,128)(2,1)}, bf16[6,32,1024]{2,1,0:T(8,128)(2,1)}, u32[]{:S(2)}, u32[]{:S(2)}) collective-permute-start(bf16[6,32,1024]{2,1,0:T(8,128)(2,1)} %get-tuple-element.71.refs_0_), channel_id=1, source_target_pairs={{0,96},{32,0},{64,32},{96,64},{1,97},{33,1},{65,33},{97,65},{2,98}... | collective-permute-start | bytes 1179656 | tf_op jit(solution)/shard_map/ppermute | solution.py:358
  228.7 19.5 %collective-permute-start.16 = (bf16[6,32,1024]{2,1,0:T(8,128)(2,1)S(1)}, bf16[6,32,1024]{2,1,0:T(8,128)(2,1)}, u32[]{:S(2)}, u32[]{:S(2)}) collective-permute-start(bf16[6,32,1024]{2,1,0:T(8,128)(2,1)S(1)} %collective-permute-done.12.refs_2_.refs_1_), channel_id=1, source_target_pairs={{0,32},{32,64},{64,96},{96,0},{1,33},{33,65},{65,97},{97,1},{2,34}... | collective-permute-start | bytes 1179656 | tf_op jit(solution)/shard_map/ppermute | solution.py:359
  244.0 11.1 %collective-permute-start.18 = (bf16[6,32,1024]{2,1,0:T(8,128)(2,1)S(1)}, bf16[6,32,1024]{2,1,0:T(8,128)(2,1)S(1)}, u32[]{:S(2)}, u32[]{:S(2)}) collective-permute-start(bf16[6,32,1024]{2,1,0:T(8,128)(2,1)S(1)} %get-tuple-element.77.refs_0_), channel_id=1, source_target_pairs={{0,32},{32,64},{64,96},{96,0},{1,33},{33,65},{65,97},{97,1},{2,34}... | collective-permute-start | bytes 1179656 | tf_op jit(solution)/shard_map/ppermute | solution.py:355
  244.0 11.1 %collective-permute-start.21 = (bf16[6,32,1024]{2,1,0:T(8,128)(2,1)S(1)}, bf16[6,32,1024]{2,1,0:T(8,128)(2,1)S(1)}, u32[]{:S(2)}, u32[]{:S(2)}) collective-permute-start(bf16[6,32,1024]{2,1,0:T(8,128)(2,1)S(1)} %get-tuple-element.78.refs_1_), channel_id=1, source_target_pairs={{0,96},{32,0},{64,32},{96,64},{1,97},{33,1},{65,33},{97,65},{2,98}... | collective-permute-start | bytes 1179656 | tf_op jit(solution)/shard_map/ppermute | solution.py:356
  246.7 15.8 %collective-permute-start.17 = (bf16[6,32,1024]{2,1,0:T(8,128)(2,1)S(1)}, bf16[6,32,1024]{2,1,0:T(8,128)(2,1)S(1)}, u32[]{:S(2)}, u32[]{:S(2)}) collective-permute-start(bf16[6,32,1024]{2,1,0:T(8,128)(2,1)S(1)} %collective-permute-done.15.refs_5_.refs_2_), channel_id=1, source_target_pairs={{0,96},{32,0},{64,32},{96,64},{1,97},{33,1},{65,33},{97,65},{2,98}... | collective-permute-start | bytes 1179656 | tf_op jit(solution)/shard_map/ppermute | solution.py:360
  246.7 19.3 %collective-permute-start.19 = (bf16[6,32,1024]{2,1,0:T(8,128)(2,1)S(1)}, bf16[6,32,1024]{2,1,0:T(8,128)(2,1)S(1)}, u32[]{:S(2)}, u32[]{:S(2)}) collective-permute-start(bf16[6,32,1024]{2,1,0:T(8,128)(2,1)S(1)} %get-tuple-element.78.refs_1_), channel_id=1, source_target_pairs={{0,32},{32,64},{64,96},{96,0},{1,33},{33,65},{65,97},{97,1},{2,34}... | collective-permute-start | bytes 1179656 | tf_op jit(solution)/shard_map/ppermute | solution.py:357
  248.2 22.7 %collective-permute-start.20 = (bf16[6,32,1024]{2,1,0:T(8,128)(2,1)S(1)}, bf16[6,32,1024]{2,1,0:T(8,128)(2,1)S(1)}, u32[]{:S(2)}, u32[]{:S(2)}) collective-permute-start(bf16[6,32,1024]{2,1,0:T(8,128)(2,1)S(1)} %get-tuple-element.77.refs_0_), channel_id=1, source_target_pairs={{0,96},{32,0},{64,32},{96,64},{1,97},{33,1},{65,33},{97,65},{2,98}... | collective-permute-start | bytes 1179656 | tf_op jit(solution)/shard_map/ppermute | solution.py:358
  255.1 18.1 %collective-permute-start.22 = (bf16[6,32,1024]{2,1,0:T(8,128)(2,1)S(1)}, bf16[6,32,1024]{2,1,0:T(8,128)(2,1)S(1)}, u32[]{:S(2)}, u32[]{:S(2)}) collective-permute-start(bf16[6,32,1024]{2,1,0:T(8,128)(2,1)S(1)} %collective-permute-done.18.refs_2_), channel_id=1, source_target_pairs={{0,32},{32,64},{64,96},{96,0},{1,33},{33,65},{65,97},{97,1},{2,34}... | collective-permute-start | bytes 1179656 | tf_op jit(solution)/shard_map/ppermute | solution.py:359
  255.1 24.3 %collective-permute-start.23 = (bf16[6,32,1024]{2,1,0:T(8,128)(2,1)S(1)}, bf16[6,32,1024]{2,1,0:T(8,128)(2,1)S(1)}, u32[]{:S(2)}, u32[]{:S(2)}) collective-permute-start(bf16[6,32,1024]{2,1,0:T(8,128)(2,1)S(1)} %collective-permute-done.21.refs_5_), channel_id=1, source_target_pairs={{0,96},{32,0},{64,32},{96,64},{1,97},{33,1},{65,33},{97,65},{2,98}... | collective-permute-start | bytes 1179656 | tf_op jit(solution)/shard_map/ppermute | solution.py:360
  (6 other events, 6.6 us)

commit v4 on v3

--- a/solution.py
+++ b/solution.py
@@ -36,9 +36,9 @@
     return jnp.dot(a, b, preferred_element_type=jnp.float32)
 
 
-def sum_kernel(start, first, last, meta, gradients, one, two, three, old_all, *refs):
+def sum_kernel(start, offset, first, last, n_base, meta, gradients, one, two, three, old_all, *refs):
     before = None if first else refs[0]
-    outs = refs[0 if first else 1 : -5]
+    outs = refs[(0 if first else 1) + n_base : -5]
     norms = None if last else outs[-1]
     outs = outs if last else outs[:-1]
     own, old, codes, in_sems, sems = refs[-5:]
@@ -87,40 +87,38 @@
     def block(at, _):
         code_block(at)
         owner, rank = meta[1 + at], meta[1 + nbg + at]
-        if not last:
-            slots = outs[0].shape[1]
-            pltpu.make_async_copy(codes.at[at], outs[0].at[owner, jnp.minimum(rank, slots - 1)], sems.at[at]).start()
+        if len(outs) == 1:
+            to = outs[0].at[owner, jnp.minimum(rank, outs[0].shape[1] - 1), to_rows]
+            pltpu.make_async_copy(codes.at[at], to, sems.at[at]).start()
         else:
             for k, out in enumerate(outs):
 
                 @pl.when(rank == k)
                 def _():
-                    pltpu.make_async_copy(codes.at[at], out.at[owner], sems.at[at]).start()
+                    pltpu.make_async_copy(codes.at[at], out.at[owner, to_rows], sems.at[at]).start()
 
         return 0
 
+    to_rows = pl.ds(offset, per)
     lax.fori_loop(0, nbg, block, 0)
-    to = outs[0].at[0] if last else outs[0].at[0, 0]
+    done = outs[0].at[0, 0, to_rows] if len(outs) == 1 else outs[0].at[0, to_rows]
     for n in range(nbg):
-        pltpu.make_async_copy(codes.at[n], to, sems.at[n]).wait()
-
-
-def sum_replicas(gradients, received, old, start, meta, before, shards, slots, last):
+        pltpu.make_async_copy(codes.at[n], done, sems.at[n]).wait()
+
+
+def sum_replicas(gradients, received, old, start, meta, before, last, offset, shapes, base):
     nbg, per, width = received[0].shape
     columns = width + LANES
-    if last:
-        shapes = [jax.ShapeDtypeStruct((shards, per, columns), jnp.int16)] * slots
-    else:
-        shapes = [
-            jax.ShapeDtypeStruct((shards, slots, per, columns), jnp.int16),
-            jax.ShapeDtypeStruct((nbg, 1, LANES), jnp.float32),
-        ]
+    out_shapes = [pltpu.HBM(x, jnp.int16) for x in shapes]
+    if not last:
+        out_shapes.append(jax.ShapeDtypeStruct((nbg, 1, LANES), jnp.float32))
     carried = [] if before is None else [before]
+    base = [in_hbm(x) for x in base]
     return pl.pallas_call(
-        functools.partial(sum_kernel, start, before is None, last),
-        out_shape=shapes,
-        in_specs=[SMEM, ANY, VMEM, VMEM, VMEM, ANY] + [VMEM] * len(carried),
-        out_specs=[ANY] * slots if last else [ANY, VMEM],
+        functools.partial(sum_kernel, start, offset, before is None, last, len(base)),
+        out_shape=out_shapes,
+        in_specs=[SMEM, ANY, VMEM, VMEM, VMEM, ANY] + [VMEM] * len(carried) + [ANY] * len(base),
+        out_specs=[ANY] * len(shapes) + ([] if last else [VMEM]),
         scratch_shapes=[
             pltpu.VMEM((nbg, per, width), jnp.bfloat16),
             pltpu.VMEM((nbg, per, width), jnp.bfloat16),
@@ -128,32 +126,32 @@
             pltpu.SemaphoreType.DMA((2,)),
             pltpu.SemaphoreType.DMA((nbg,)),
         ],
+        input_output_aliases={6 + len(carried) + n: n for n in range(len(base))},
         compiler_params=SMALL,
-    )(meta, in_hbm(gradients), *[in_vmem(r) for r in received], in_hbm(old), *carried)
+    )(meta, in_hbm(gradients), *[in_vmem(r) for r in received], in_hbm(old), *carried, *base)
 
 
 def owner_kernel(slot, all_roots, *refs):
-    arrived, update, high, low, pre, roots, sems = refs[:-6], *refs[-6:]
+    early, late, out, high, low, pre, roots, update, sems, out_sems = refs
     width = update.shape[0]
     loads = [pltpu.make_async_copy(all_roots.at[0, 0, slot, k], roots.at[k], sems.at[k]) for k in (1, 0)]
     for x in loads:
         x.start()
-    n_src = arrived[0].shape[0]
-    per = arrived[0].shape[-2]
-    rows = per * len(arrived)
+    n_src, per = late.shape[:2]
+    rows = 2 * per
 
     def unpack(n, graft):
-        codes = [a[n, slot] if len(a.shape) == 4 else a[n] for a in arrived]
+        codes = [early[n, slot], late[n]]
         tails = [x[:, width:].astype(jnp.int32).astype(jnp.float32) for x in codes]
-        norm = tails[-1]
+        norm = tails[1][8:]
         row = lax.broadcasted_iota(jnp.int32, norm.shape, 0)
-        tails[-1] = jnp.where(row < 4, norm, pltpu.roll(norm, 4, 0))
-        steps = [jnp.exp2(t) for t in tails]
-        for c in range(0, len(codes), 2):
-            at = pl.ds(pl.multiple_of(n * rows + c * per, 2 * per), 2 * per)
+        tails[1] = jnp.concatenate([tails[1][:8], jnp.where(row < 4, norm, pltpu.roll(norm, 4, 0))], axis=0)
+        for c, (code, tail) in enumerate(zip(codes, tails)):
+            at = pl.ds(pl.multiple_of(n * rows + c * per, per), per)
+            step = jnp.exp2(tail)
             for j in range(0, width, LANES):
-                value = [x[:, j : j + LANES].astype(jnp.int32).astype(jnp.float32) * t for x, t in zip(codes[c : c + 2], steps[c : c + 2])]
-                high[at, j : j + LANES], low[at, j : j + LANES] = two_parts(jnp.concatenate(value, axis=0))
+                value = code[:, j : j + LANES].astype(jnp.int32).astype(jnp.float32) * step
+                high[at, j : j + LANES], low[at, j : j + LANES] = two_parts(value)
         return graft + jnp.exp2(norm[4:5] - 14.0) * (norm[5:6] + norm[6:7] * (1.0 / 16384.0))
 
     graft = lax.fori_loop(0, n_src, unpack, jnp.zeros((1, LANES), jnp.float32))
@@ -173,24 +171,31 @@
         square = square + jnp.sum(got * got, axis=0, keepdims=True)
     square = jnp.sum(square, axis=1, keepdims=True)
     scale = jnp.sqrt(graft) / jnp.sqrt(square + 1e-06)
-    for m in range(0, width, TALL):
+    copies = []
+    for n, m in enumerate(range(0, width, TALL)):
         at = pl.ds(m, TALL)
         update[at, :] = (scale * pre[at, :]).astype(jnp.bfloat16)
+        copies.append(pltpu.make_async_copy(update.at[at], out.at[at], out_sems.at[n]))
+        copies[-1].start()
+    for c in copies:
+        c.wait()
 
 
 def owner_work(roots, arrived, slot):
     width = roots.shape[-1]
     return pl.pallas_call(
         functools.partial(owner_kernel, slot),
-        out_shape=jax.ShapeDtypeStruct((width, width), jnp.bfloat16),
+        out_shape=pltpu.HBM((width, width), jnp.bfloat16),
         in_specs=[ANY] + [VMEM] * len(arrived),
-        out_specs=VMEM,
+        out_specs=ANY,
         scratch_shapes=[
             pltpu.VMEM((width, width), jnp.bfloat16),
             pltpu.VMEM((width, width), jnp.bfloat16),
             pltpu.VMEM((width, width), jnp.float32),
             pltpu.VMEM((2, width, width), jnp.bfloat16),
+            pltpu.VMEM((width, width), jnp.bfloat16),
             pltpu.SemaphoreType.DMA((2,)),
+            pltpu.SemaphoreType.DMA((width // TALL,)),
         ],
         compiler_params=LARGE,
     )(in_hbm(roots), *[in_vmem(a) for a in arrived])
@@ -331,19 +336,26 @@
             x, after = lax.optimization_barrier((x, after))
         return lax.all_to_all(x, "shard", 0, 0, tiled=True)
 
+    columns = width + LANES
     norm = None
     coded = []
-    for c, start in enumerate(starts):
-        last = c == len(starts) - 1
-        code = sum_replicas(gradients, received[c], second_moment, start, meta, norm, shards, slots, last)
+    for c in range(0, len(starts), 2):
+        tall = CHUNKS[c] + CHUNKS[c + 1]
+        final = c + 2 == len(starts)
+        shapes = [(shards, tall, columns)] * slots if final else [(shards, slots, tall, columns)]
+        code = []
+        for d in (c, c + 1):
+            last = final and d > c
+            code = sum_replicas(
+                gradients, received[d], second_moment, starts[d], meta, norm, last, starts[d] - starts[c], shapes, code
+            )
+            norm = None if last else code[-1]
+            code = code[: len(shapes)]
         coded.append(code)
-        norm = None if last else code[-1]
-    early = []
-    for code in coded[:-1]:
-        early.append(exchange(code[0], early[-1] if early else None))
+    early = exchange(coded[0][0])
     arrived = []
     for k in range(slots):
-        arrived.append(early + [exchange(coded[-1][k], arrived[-1][-1] if k else early[-1])])
+        arrived.append([early, exchange(coded[1][k], arrived[-1][-1] if k else early)])
 
     backs = []
     for k in range(slots):

time: 284 us -> 258 us (0.908)
  starting transfers between devices: 70.2 us -> 53.6 us
  waiting for transfers between devices: 120 us -> 106 us
  blocking collectives: 19.5 us -> 27.4 us
  local copies, waits for them, and re-layouts: 12.3 us -> 8.45 us
    ppermute x12, waiting for transfers between devices: 70.9 us -> 49.3 us  [body(): lax.ppermute(p, 'groups', shift(n))]
    all_to_all x6 -> x4, starting transfers between devices: 42.1 us -> 22.9 us  [exchange(): return lax.all_to_all(x, 'shard', 0, 0, tiled=True)]
    all_to_all x1, blocking collectives: 19.5 us -> 27.4 us  [exchange(): return lax.all_to_all(x, 'shard', 0, 0, tiled=True)]
    all_to_all x6 -> x4, waiting for transfers between devices: 21.1 us -> 28.5 us  [exchange(): return lax.all_to_all(x, 'shard', 0, 0, tiled=True)]
    unnamed x16 -> x4, local copies, waits for them, and re-layouts: 6.59 us -> 1.27 us
  transfers between devices with their start and end apart: 30 -> 28, of which waited for: 16 -> 18; matrix products, arithmetic and copies ran while one was open for 2% -> 3% of each run, Pallas kernels for 19% -> 21%
where the time goes in v4:
time: 258 us; the launch traced here: 255 us
  waiting for transfers between devices  106 us (41%)
  Pallas kernels  58.2 us (23%)
  starting transfers between devices  53.6 us (21%)
  blocking collectives  27.4 us (11%)
  local copies, waits for them, and re-layouts  8.45 us (3%)
    ppermute x12, waiting for transfers between devices, body(): lax.ppermute(p, 'groups', shift(n))  49.3 us
    all_to_all x4, waiting for transfers between devices, exchange(): return lax.all_to_all(x, 'shard', 0, 0, tiled=True)  28.5 us
    all_to_all x1, blocking collectives, exchange(): return lax.all_to_all(x, 'shard', 0, 0, tiled=True)  27.4 us
    pallas_call x2, Pallas kernels, owner_work(): pl.pallas_call(functools.partial(owner_kernel, slot), out_shape=pltpu.HBM...  24.8 us
    all_to_all x4, starting transfers between devices, exchange(): return lax.all_to_all(x, 'shard', 0, 0, tiled=True)  22.9 us
    ppermute x12, starting transfers between devices, body(): lax.ppermute(p, 'groups', shift(n))  17.2 us
    pallas_call x4, Pallas kernels, sum_replicas(): pl.pallas_call(functools.partial(sum_kernel, start, offset, before is Non...  14.8 us
    ppermute x2, waiting for transfers between devices, to_all(): prev_a = lax.ppermute(a, 'groups', shift(1))  11.8 us
  transfers between devices with their start and end apart: 28, of which 18 were waited for; matrix products, arithmetic and copies ran while one was open for 3% of the time, Pallas kernels for 21%

profile of v4, /device:TPU:1, one launch (start us, length us, event | category | flops | bytes accessed | tf_op | source)
XLA Modules:
  0.0 255.2 jit_solution(11097871679547653377)
XLA Ops:
  16.0 7.6 %collective-permute-done.5.three = bf16[24,8,1024]{2,1,0:T(8,128)(2,1)S(1)} collective-permute-done((bf16[24,8,1024]{2,1,0:T(8,128)(2,1)S(1)}, bf16[24,8,1024]{2,1,0:T(8,128)(2,1)S(1)}, u32[]{:S(2)}, u32[]{:S(2)}) %collective-permute-start.5) | collective-permute-done | bytes 393248 | tf_op jit(solution)/shard_map/ppermute | solution.py:313
  23.6 3.5 %shard_map.56 = (s16[32,2,16,1152]{3,2,1,0:T(8,128)(2,1)}, f32[24,1,128]{2,1,0:T(1,128)S(1)}) custom-call(s32[49]{0:T(128)S(1)} %pad_add_fusion.4.meta, bf16[1,96,32,1024]{3,2,1,0:T(8,128)(2,1)} %gradients.7, bf16[24,8,1024]{2,1,0:T(8,128)(2,1)S(1)} %collective-permute-done.3.one, bf16[24,8,1024]{2,1,0:T(8,128)(2,1)S(1)} %collective-permute-done.4.two, ...), custom_call_target="tpu_custom_call" | custom-call | tf_op jit(solution)/shard_map/pallas_call | solution.py:117
  27.1 3.6 %collective-permute-done.one = bf16[24,8,1024]{2,1,0:T(8,128)(2,1)S(1)} collective-permute-done((bf16[24,8,1024]{2,1,0:T(8,128)(2,1)}, bf16[24,8,1024]{2,1,0:T(8,128)(2,1)S(1)}, u32[]{:S(2)}, u32[]{:S(2)}) %collective-permute-start) | collective-permute-done | bytes 393248 | tf_op jit(solution)/shard_map/ppermute | solution.py:313
  30.9 9.5 %collective-permute-done.2.three = bf16[24,8,1024]{2,1,0:T(8,128)(2,1)S(1)} collective-permute-done((bf16[24,8,1024]{2,1,0:T(8,128)(2,1)S(1)}, bf16[24,8,1024]{2,1,0:T(8,128)(2,1)S(1)}, u32[]{:S(2)}, u32[]{:S(2)}) %collective-permute-start.2) | collective-permute-done | bytes 393248 | tf_op jit(solution)/shard_map/ppermute | solution.py:313
  40.4 3.5 %shard_map.57 = (s16[32,2,16,1152]{3,2,1,0:T(8,128)(2,1)}, f32[24,1,128]{2,1,0:T(1,128)S(1)}) custom-call(s32[49]{0:T(128)S(1)} %pad_add_fusion.4.meta, bf16[1,96,32,1024]{3,2,1,0:T(8,128)(2,1)} %gradients.7, bf16[24,8,1024]{2,1,0:T(8,128)(2,1)S(1)} %collective-permute-done.one, ...), custom_call_target="tpu_custom_call", output_to_operand_aliasing={{0}: (7, {})} | custom-call | tf_op jit(solution)/shard_map/pallas_call | solution.py:117
  44.0 9.6 %all-to-all-start = ((s16[32,2,16,1152]{3,2,1,0:T(8,128)(2,1)}), s16[32,2,16,1152]{3,2,1,0:T(8,128)(2,1)S(1)}, u32[]{:S(2)}, u32[]{:S(2)}) async-start(s16[32,2,16,1152]{3,2,1,0:T(8,128)(2,1)} %get-tuple-element.54), calls=%async_computation | async-start | bytes 4718592 | tf_op jit(solution)/shard_map/all_to_all | solution.py:337
  62.0 3.4 %collective-permute-done.10.two = bf16[24,8,1024]{2,1,0:T(8,128)(2,1)S(1)} collective-permute-done((bf16[24,8,1024]{2,1,0:T(8,128)(2,1)S(1)}, bf16[24,8,1024]{2,1,0:T(8,128)(2,1)S(1)}, u32[]{:S(2)}, u32[]{:S(2)}) %collective-permute-start.10) | collective-permute-done | bytes 393248 | tf_op jit(solution)/shard_map/ppermute | solution.py:313
  68.6 9.3 %collective-permute-done.9.one = bf16[24,8,1024]{2,1,0:T(8,128)(2,1)S(1)} collective-permute-done((bf16[24,8,1024]{2,1,0:T(8,128)(2,1)S(1)}, bf16[24,8,1024]{2,1,0:T(8,128)(2,1)S(1)}, u32[]{:S(2)}, u32[]{:S(2)}) %collective-permute-start.9) | collective-permute-done | bytes 393248 | tf_op jit(solution)/shard_map/ppermute | solution.py:313
  77.8 3.5 %shard_map.58 = (s16[32,16,1152]{2,1,0:T(8,128)(2,1)}, s16[32,16,1152]{2,1,0:T(8,128)(2,1)}, f32[24,1,128]{2,1,0:T(1,128)S(1)}) custom-call(s32[49]{0:T(128)S(1)} %pad_add_fusion.4.meta, bf16[1,96,32,1024]{3,2,1,0:T(8,128)(2,1)} %gradients.7, bf16[24,8,1024]{2,1,0:T(8,128)(2,1)S(1)} %collective-permute-done.9.one, ...), custom_call_target="tpu_custom_call" | custom-call | tf_op jit(solution)/shard_map/pallas_call | solution.py:117
  81.4 5.7 %collective-permute-done.6.one = bf16[24,8,1024]{2,1,0:T(8,128)(2,1)S(1)} collective-permute-done((bf16[24,8,1024]{2,1,0:T(8,128)(2,1)S(1)}, bf16[24,8,1024]{2,1,0:T(8,128)(2,1)S(1)}, u32[]{:S(2)}, u32[]{:S(2)}) %collective-permute-start.6) | collective-permute-done | bytes 393248 | tf_op jit(solution)/shard_map/ppermute | solution.py:313
  87.1 6.8 %collective-permute-done.8.three = bf16[24,8,1024]{2,1,0:T(8,128)(2,1)S(1)} collective-permute-done((bf16[24,8,1024]{2,1,0:T(8,128)(2,1)S(1)}, bf16[24,8,1024]{2,1,0:T(8,128)(2,1)S(1)}, u32[]{:S(2)}, u32[]{:S(2)}) %collective-permute-start.8) | collective-permute-done | bytes 393248 | tf_op jit(solution)/shard_map/ppermute | solution.py:313
  93.9 4.2 %shard_map.59 = (s16[32,16,1152]{2,1,0:T(8,128)(2,1)}, s16[32,16,1152]{2,1,0:T(8,128)(2,1)}) custom-call(s32[49]{0:T(128)S(1)} %pad_add_fusion.4.meta, bf16[1,96,32,1024]{3,2,1,0:T(8,128)(2,1)} %gradients.7, bf16[24,8,1024]{2,1,0:T(8,128)(2,1)S(1)} %collective-permute-done.6.one, ...), custom_call_target="tpu_custom_call", output_to_operand_aliasing={{0}: (7, {}), {1}: (8, {})} | custom-call | tf_op jit(solution)/shard_map/pallas_call | solution.py:117
  98.0 27.4 %all_to_all.25.refs_1_ = s16[32,16,1152]{2,1,0:T(8,128)(2,1)} all-to-all(s16[32,16,1152]{2,1,0:T(8,128)(2,1)} %get-tuple-element.68), channel_id=1, replica_groups=mesh['groups'=4,'shard'=32] {'shard'}, dimensions={0} | all-to-all | bytes 2359296 | tf_op jit(solution)/shard_map/all_to_all | solution.py:337
  125.4 4.0 %all-to-all-start.3 = ((s16[32,16,1152]{2,1,0:T(8,128)(2,1)}), s16[32,16,1152]{2,1,0:T(8,128)(2,1)S(1)}, u32[]{:S(2)}, u32[]{:S(2)}) async-start(s16[32,16,1152]{2,1,0:T(8,128)(2,1)} %get-tuple-element.73), calls=%async_computation.3 | async-start | bytes 2359296 | tf_op jit(solution)/shard_map/all_to_all | solution.py:337
  130.7 12.4 %shard_map.60 = bf16[1024,1024]{1,0:T(8,128)(2,1)} custom-call(bf16[1,1,2,2,1024,1024]{5,4,3,2,1,0:T(8,128)(2,1)} %all_roots.3, s16[32,2,16,1152]{3,2,1,0:T(8,128)(2,1)S(1)} %all-to-all-done.refs_0_, s16[32,16,1152]{2,1,0:T(8,128)(2,1)S(1)} %copy-done), custom_call_target="tpu_custom_call" | custom-call | tf_op jit(solution)/shard_map/pallas_call | solution.py:186
  143.1 4.8 %all-to-all-done.3.refs_1_ = s16[32,16,1152]{2,1,0:T(8,128)(2,1)S(1)} async-done(((s16[32,16,1152]{2,1,0:T(8,128)(2,1)}), s16[32,16,1152]{2,1,0:T(8,128)(2,1)S(1)}, u32[]{:S(2)}, u32[]{:S(2)}) %all-to-all-start.3) | async-done | bytes 1179680 | tf_op jit(solution)/shard_map/all_to_all | solution.py:337
  147.9 4.8 %all-to-all-start.2 = ((bf16[32,32,1024]{2,1,0:T(8,128)(2,1)}), bf16[32,32,1024]{2,1,0:T(8,128)(2,1)}, u32[]{:S(2)}, u32[]{:S(2)}) async-start(bf16[32,32,1024]{2,1,0:T(8,128)(2,1)} %bitcast.56), calls=%async_computation.2 | async-start | bytes 4194304 | tf_op jit(solution)/shard_map/all_to_all | solution.py:337
  153.7 12.4 %shard_map.64 = bf16[1024,1024]{1,0:T(8,128)(2,1)} custom-call(bf16[1,1,2,2,1024,1024]{5,4,3,2,1,0:T(8,128)(2,1)} %all_roots.3, s16[32,2,16,1152]{3,2,1,0:T(8,128)(2,1)S(1)} %all-to-all-done.refs_0_, s16[32,16,1152]{2,1,0:T(8,128)(2,1)S(1)} %all-to-all-done.3.refs_1_), custom_call_target="tpu_custom_call" | custom-call | tf_op jit(solution)/shard_map/pallas_call | solution.py:186
  166.1 14.7 %all-to-all-done.2.refs_0_ = bf16[32,32,1024]{2,1,0:T(8,128)(2,1)} async-done(((bf16[32,32,1024]{2,1,0:T(8,128)(2,1)}), bf16[32,32,1024]{2,1,0:T(8,128)(2,1)}, u32[]{:S(2)}, u32[]{:S(2)}) %all-to-all-start.2) | async-done | bytes 2097184 | tf_op jit(solution)/shard_map/all_to_all | solution.py:337
  180.8 4.5 %all-to-all-start.4 = ((bf16[32,32,1024]{2,1,0:T(8,128)(2,1)}), bf16[32,32,1024]{2,1,0:T(8,128)(2,1)S(1)}, u32[]{:S(2)}, u32[]{:S(2)}) async-start(bf16[32,32,1024]{2,1,0:T(8,128)(2,1)} %bitcast.55), calls=%async_computation.4 | async-start | bytes 4194304 | tf_op jit(solution)/shard_map/all_to_all | solution.py:337
  187.2 4.7 %shard_map.61 = (bf16[6,32,1024]{2,1,0:T(8,128)(2,1)S(1)}, bf16[6,32,1024]{2,1,0:T(8,128)(2,1)}) custom-call(s32[36]{0:T(128)S(1)} %get-tuple-element.44.table, bf16[24,32,1024]{2,1,0:T(8,128)(2,1)} %weights.3, bf16[32,32,1024]{2,1,0:T(8,128)(2,1)} %all-to-all-done.2.refs_0_), custom_call_target="tpu_custom_call" | custom-call | tf_op jit(solution)/shard_map/pallas_call | solution.py:230
  192.1 2.7 %collective-permute-start.15 = (bf16[6,32,1024]{2,1,0:T(8,128)(2,1)}, bf16[6,32,1024]{2,1,0:T(8,128)(2,1)S(1)}, u32[]{:S(2)}, u32[]{:S(2)}) collective-permute-start(bf16[6,32,1024]{2,1,0:T(8,128)(2,1)} %get-tuple-element.70.refs_1_), channel_id=1, source_target_pairs={{0,96},{32,0},{64,32},{96,64},{1,97},{33,1},{65,33},{97,65},{2,98}... | collective-permute-start | bytes 1179656 | tf_op jit(solution)/shard_map/ppermute | solution.py:368
  194.7 2.7 %collective-permute-start.14 = (bf16[6,32,1024]{2,1,0:T(8,128)(2,1)S(1)}, bf16[6,32,1024]{2,1,0:T(8,128)(2,1)}, u32[]{:S(2)}, u32[]{:S(2)}) collective-permute-start(bf16[6,32,1024]{2,1,0:T(8,128)(2,1)S(1)} %get-tuple-element.69.refs_0_), channel_id=1, source_target_pairs={{0,96},{32,0},{64,32},{96,64},{1,97},{33,1},{65,33},{97,65},{2,98}... | collective-permute-start | bytes 1179656 | tf_op jit(solution)/shard_map/ppermute | solution.py:370
  197.4 6.2 %collective-permute-done.12.refs_2_.refs_1_ = bf16[6,32,1024]{2,1,0:T(8,128)(2,1)S(1)} collective-permute-done((bf16[6,32,1024]{2,1,0:T(8,128)(2,1)S(1)}, bf16[6,32,1024]{2,1,0:T(8,128)(2,1)S(1)}, u32[]{:S(2)}, u32[]{:S(2)}) %collective-permute-start.12) | collective-permute-done | bytes 393248 | tf_op jit(solution)/shard_map/ppermute | solution.py:367
  204.7 9.0 %all-to-all-done.4.refs_1_ = bf16[32,32,1024]{2,1,0:T(8,128)(2,1)S(1)} async-done(((bf16[32,32,1024]{2,1,0:T(8,128)(2,1)}), bf16[32,32,1024]{2,1,0:T(8,128)(2,1)S(1)}, u32[]{:S(2)}, u32[]{:S(2)}) %all-to-all-start.4) | async-done | bytes 2097184 | tf_op jit(solution)/shard_map/all_to_all | solution.py:337
  213.7 4.3 %shard_map.65 = (bf16[6,32,1024]{2,1,0:T(8,128)(2,1)S(1)}, bf16[6,32,1024]{2,1,0:T(8,128)(2,1)S(1)}) custom-call(s32[36]{0:T(128)S(1)} %shard_map.63.table, bf16[24,32,1024]{2,1,0:T(8,128)(2,1)} %weights.3, bf16[32,32,1024]{2,1,0:T(8,128)(2,1)} %all-to-all-done.2.refs_0_, bf16[32,32,1024]{2,1,0:T(8,128)(2,1)S(1)} %all-to-all-done.4.refs_1_), custom_call_target="tpu_custom_call" | custom-call | tf_op jit(solution)/shard_map/pallas_call | solution.py:230
  223.6 5.6 %collective-permute-done.18.refs_2_ = bf16[6,32,1024]{2,1,0:T(8,128)(2,1)S(1)} collective-permute-done((bf16[6,32,1024]{2,1,0:T(8,128)(2,1)S(1)}, bf16[6,32,1024]{2,1,0:T(8,128)(2,1)S(1)}, u32[]{:S(2)}, u32[]{:S(2)}) %collective-permute-start.18) | collective-permute-done | bytes 393248 | tf_op jit(solution)/shard_map/ppermute | solution.py:367
  229.2 2.7 %collective-permute-start.23 = (bf16[6,32,1024]{2,1,0:T(8,128)(2,1)S(1)}, bf16[6,32,1024]{2,1,0:T(8,128)(2,1)S(1)}, u32[]{:S(2)}, u32[]{:S(2)}) collective-permute-start(bf16[6,32,1024]{2,1,0:T(8,128)(2,1)S(1)} %collective-permute-done.21.refs_5_), channel_id=1, source_target_pairs={{0,96},{32,0},{64,32},{96,64},{1,97},{33,1},{65,33},{97,65},{2,98}... | collective-permute-start | bytes 1179656 | tf_op jit(solution)/shard_map/ppermute | solution.py:372
  231.9 4.7 %collective-permute-done.17.refs_7_ = bf16[6,32,1024]{2,1,0:T(8,128)(2,1)S(1)} collective-permute-done((bf16[6,32,1024]{2,1,0:T(8,128)(2,1)S(1)}, bf16[6,32,1024]{2,1,0:T(8,128)(2,1)S(1)}, u32[]{:S(2)}, u32[]{:S(2)}) %collective-permute-start.17) | collective-permute-done | bytes 393248 | tf_op jit(solution)/shard_map/ppermute | solution.py:372
  236.6 3.4 %shard_map.62.base = bf16[96,32,1024]{2,1,0:T(8,128)(2,1)} custom-call(s32[48]{0:T(128)S(1)} %get-tuple-element.43.place, bf16[6,32,1024]{2,1,0:T(8,128)(2,1)S(1)} %get-tuple-element.69.refs_0_, bf16[6,32,1024]{2,1,0:T(8,128)(2,1)} %get-tuple-element.70.refs_1_, bf16[6,32,1024]{2,1,0:T(8,128)(2,1)S(1)} %collective-permute-done.12.refs_2_.refs_1_, ...), custom_call_target="tpu_custom_call" | custom-call | tf_op jit(solution)/shard_map/pallas_call | solution.py:280
  240.0 5.0 %collective-permute-done.20.refs_4_ = bf16[6,32,1024]{2,1,0:T(8,128)(2,1)S(1)} collective-permute-done((bf16[6,32,1024]{2,1,0:T(8,128)(2,1)S(1)}, bf16[6,32,1024]{2,1,0:T(8,128)(2,1)S(1)}, u32[]{:S(2)}, u32[]{:S(2)}) %collective-permute-start.20) | collective-permute-done | bytes 393248 | tf_op jit(solution)/shard_map/ppermute | solution.py:370
  247.3 6.2 %collective-permute-done.23.refs_1_ = bf16[6,32,1024]{2,1,0:T(8,128)(2,1)S(1)} collective-permute-done((bf16[6,32,1024]{2,1,0:T(8,128)(2,1)S(1)}, bf16[6,32,1024]{2,1,0:T(8,128)(2,1)S(1)}, u32[]{:S(2)}, u32[]{:S(2)}) %collective-permute-start.23) | collective-permute-done | bytes 393248 | tf_op jit(solution)/shard_map/ppermute | solution.py:372
  (67 shorter events, 42.4 us)
Async XLA Ops:
  0.0 15.7 %copy-start.1 = (s32[96]{0:T(128)S(1)}, s32[96]{0:T(128)}, u32[]{:S(2)}) copy-start(s32[96]{0:T(128)} %param.8) | copy-start | bytes 1156
  2.1 11.7 %collective-permute-start.3 = (bf16[24,8,1024]{2,1,0:T(8,128)(2,1)S(1)}, bf16[24,8,1024]{2,1,0:T(8,128)(2,1)S(1)}, u32[]{:S(2)}, u32[]{:S(2)}) collective-permute-start(bf16[24,8,1024]{2,1,0:T(8,128)(2,1)S(1)} %get-tuple-element.49), channel_id=1, source_target_pairs={{0,32},{32,64},{64,96},{96,0},{1,33},{33,65},{65,97},{97,1},{2,34}... | collective-permute-start | bytes 1179656 | tf_op jit(solution)/shard_map/ppermute | solution.py:313
  4.1 11.9 %collective-permute-start.4 = (bf16[24,8,1024]{2,1,0:T(8,128)(2,1)}, bf16[24,8,1024]{2,1,0:T(8,128)(2,1)S(1)}, u32[]{:S(2)}, u32[]{:S(2)}) collective-permute-start(bf16[24,8,1024]{2,1,0:T(8,128)(2,1)} %get-tuple-element.50), channel_id=1, source_target_pairs={{0,96},{32,0},{64,32},{96,64},{1,97},{33,1},{65,33},{97,65},{2,98}... | collective-permute-start | bytes 1179656 | tf_op jit(solution)/shard_map/ppermute | solution.py:313
  5.4 18.2 %collective-permute-start.5 = (bf16[24,8,1024]{2,1,0:T(8,128)(2,1)S(1)}, bf16[24,8,1024]{2,1,0:T(8,128)(2,1)S(1)}, u32[]{:S(2)}, u32[]{:S(2)}) collective-permute-start(bf16[24,8,1024]{2,1,0:T(8,128)(2,1)S(1)} %get-tuple-element.51), channel_id=1, source_target_pairs={{0,64},{32,96},{64,0},{96,32},{1,65},{33,97},{65,1},{97,33},{2,66}... | collective-permute-start | bytes 1179656 | tf_op jit(solution)/shard_map/ppermute | solution.py:313
  9.2 21.5 %collective-permute-start = (bf16[24,8,1024]{2,1,0:T(8,128)(2,1)}, bf16[24,8,1024]{2,1,0:T(8,128)(2,1)S(1)}, u32[]{:S(2)}, u32[]{:S(2)}) collective-permute-start(bf16[24,8,1024]{2,1,0:T(8,128)(2,1)} %get-tuple-element.46), channel_id=1, source_target_pairs={{0,32},{32,64},{64,96},{96,0},{1,33},{33,65},{65,97},{97,1},{2,34}... | collective-permute-start | bytes 1179656 | tf_op jit(solution)/shard_map/ppermute | solution.py:313
  9.5 21.5 %collective-permute-start.1 = (bf16[24,8,1024]{2,1,0:T(8,128)(2,1)S(1)}, bf16[24,8,1024]{2,1,0:T(8,128)(2,1)S(1)}, u32[]{:S(2)}, u32[]{:S(2)}) collective-permute-start(bf16[24,8,1024]{2,1,0:T(8,128)(2,1)S(1)} %get-tuple-element.47), channel_id=1, source_target_pairs={{0,96},{32,0},{64,32},{96,64},{1,97},{33,1},{65,33},{97,65},{2,98}... | collective-permute-start | bytes 1179656 | tf_op jit(solution)/shard_map/ppermute | solution.py:313
  13.8 26.6 %collective-permute-start.2 = (bf16[24,8,1024]{2,1,0:T(8,128)(2,1)S(1)}, bf16[24,8,1024]{2,1,0:T(8,128)(2,1)S(1)}, u32[]{:S(2)}, u32[]{:S(2)}) collective-permute-start(bf16[24,8,1024]{2,1,0:T(8,128)(2,1)S(1)} %get-tuple-element.48), channel_id=1, source_target_pairs={{0,64},{32,96},{64,0},{96,32},{1,65},{33,97},{65,1},{97,33},{2,66}... | collective-permute-start | bytes 1179656 | tf_op jit(solution)/shard_map/ppermute | solution.py:313
  44.0 54.1 %all-to-all-start = ((s16[32,2,16,1152]{3,2,1,0:T(8,128)(2,1)}), s16[32,2,16,1152]{3,2,1,0:T(8,128)(2,1)S(1)}, u32[]{:S(2)}, u32[]{:S(2)}) async-start(s16[32,2,16,1152]{3,2,1,0:T(8,128)(2,1)} %get-tuple-element.54), calls=%async_computation | async-start | bytes 4718592 | tf_op jit(solution)/shard_map/all_to_all | solution.py:337
  54.9 10.5 %collective-permute-start.10 = (bf16[24,8,1024]{2,1,0:T(8,128)(2,1)S(1)}, bf16[24,8,1024]{2,1,0:T(8,128)(2,1)S(1)}, u32[]{:S(2)}, u32[]{:S(2)}) collective-permute-start(bf16[24,8,1024]{2,1,0:T(8,128)(2,1)S(1)} %get-tuple-element.61), channel_id=1, source_target_pairs={{0,96},{32,0},{64,32},{96,64},{1,97},{33,1},{65,33},{97,65},{2,98}... | collective-permute-start | bytes 1179656 | tf_op jit(solution)/shard_map/ppermute | solution.py:313
  56.9 11.7 %collective-permute-start.11 = (bf16[24,8,1024]{2,1,0:T(8,128)(2,1)S(1)}, bf16[24,8,1024]{2,1,0:T(8,128)(2,1)S(1)}, u32[]{:S(2)}, u32[]{:S(2)}) collective-permute-start(bf16[24,8,1024]{2,1,0:T(8,128)(2,1)S(1)} %get-tuple-element.62), channel_id=1, source_target_pairs={{0,64},{32,96},{64,0},{96,32},{1,65},{33,97},{65,1},{97,33},{2,66}... | collective-permute-start | bytes 1179656 | tf_op jit(solution)/shard_map/ppermute | solution.py:313
  57.9 20.0 %collective-permute-start.9 = (bf16[24,8,1024]{2,1,0:T(8,128)(2,1)S(1)}, bf16[24,8,1024]{2,1,0:T(8,128)(2,1)S(1)}, u32[]{:S(2)}, u32[]{:S(2)}) collective-permute-start(bf16[24,8,1024]{2,1,0:T(8,128)(2,1)S(1)} %get-tuple-element.60), channel_id=1, source_target_pairs={{0,32},{32,64},{64,96},{96,0},{1,33},{33,65},{65,97},{97,1},{2,34}... | collective-permute-start | bytes 1179656 | tf_op jit(solution)/shard_map/ppermute | solution.py:313
  59.2 27.9 %collective-permute-start.6 = (bf16[24,8,1024]{2,1,0:T(8,128)(2,1)S(1)}, bf16[24,8,1024]{2,1,0:T(8,128)(2,1)S(1)}, u32[]{:S(2)}, u32[]{:S(2)}) collective-permute-start(bf16[24,8,1024]{2,1,0:T(8,128)(2,1)S(1)} %get-tuple-element.57), channel_id=1, source_target_pairs={{0,32},{32,64},{64,96},{96,0},{1,33},{33,65},{65,97},{97,1},{2,34}... | collective-permute-start | bytes 1179656 | tf_op jit(solution)/shard_map/ppermute | solution.py:313
  60.9 26.2 %collective-permute-start.7 = (bf16[24,8,1024]{2,1,0:T(8,128)(2,1)S(1)}, bf16[24,8,1024]{2,1,0:T(8,128)(2,1)S(1)}, u32[]{:S(2)}, u32[]{:S(2)}) collective-permute-start(bf16[24,8,1024]{2,1,0:T(8,128)(2,1)S(1)} %get-tuple-element.58), channel_id=1, source_target_pairs={{0,96},{32,0},{64,32},{96,64},{1,97},{33,1},{65,33},{97,65},{2,98}... | collective-permute-start | bytes 1179656 | tf_op jit(solution)/shard_map/ppermute | solution.py:313
  65.5 28.4 %collective-permute-start.8 = (bf16[24,8,1024]{2,1,0:T(8,128)(2,1)S(1)}, bf16[24,8,1024]{2,1,0:T(8,128)(2,1)S(1)}, u32[]{:S(2)}, u32[]{:S(2)}) collective-permute-start(bf16[24,8,1024]{2,1,0:T(8,128)(2,1)S(1)} %get-tuple-element.59), channel_id=1, source_target_pairs={{0,64},{32,96},{64,0},{96,32},{1,65},{33,97},{65,1},{97,33},{2,66}... | collective-permute-start | bytes 1179656 | tf_op jit(solution)/shard_map/ppermute | solution.py:313
  125.4 22.4 %all-to-all-start.3 = ((s16[32,16,1152]{2,1,0:T(8,128)(2,1)}), s16[32,16,1152]{2,1,0:T(8,128)(2,1)S(1)}, u32[]{:S(2)}, u32[]{:S(2)}) async-start(s16[32,16,1152]{2,1,0:T(8,128)(2,1)} %get-tuple-element.73), calls=%async_computation.3 | async-start | bytes 2359296 | tf_op jit(solution)/shard_map/all_to_all | solution.py:337
  129.4 1.3 copy-start
  147.9 32.9 %all-to-all-start.2 = ((bf16[32,32,1024]{2,1,0:T(8,128)(2,1)}), bf16[32,32,1024]{2,1,0:T(8,128)(2,1)}, u32[]{:S(2)}, u32[]{:S(2)}) async-start(bf16[32,32,1024]{2,1,0:T(8,128)(2,1)} %bitcast.56), calls=%async_computation.2 | async-start | bytes 4194304 | tf_op jit(solution)/shard_map/all_to_all | solution.py:337
  180.8 32.9 %all-to-all-start.4 = ((bf16[32,32,1024]{2,1,0:T(8,128)(2,1)}), bf16[32,32,1024]{2,1,0:T(8,128)(2,1)S(1)}, u32[]{:S(2)}, u32[]{:S(2)}) async-start(bf16[32,32,1024]{2,1,0:T(8,128)(2,1)} %bitcast.55), calls=%async_computation.4 | async-start | bytes 4194304 | tf_op jit(solution)/shard_map/all_to_all | solution.py:337
  192.0 11.6 %collective-permute-start.12 = (bf16[6,32,1024]{2,1,0:T(8,128)(2,1)S(1)}, bf16[6,32,1024]{2,1,0:T(8,128)(2,1)S(1)}, u32[]{:S(2)}, u32[]{:S(2)}) collective-permute-start(bf16[6,32,1024]{2,1,0:T(8,128)(2,1)S(1)} %get-tuple-element.69.refs_0_), channel_id=1, source_target_pairs={{0,32},{32,64},{64,96},{96,0},{1,33},{33,65},{65,97},{97,1},{2,34}... | collective-permute-start | bytes 1179656 | tf_op jit(solution)/shard_map/ppermute | solution.py:367
  192.1 11.5 %collective-permute-start.15 = (bf16[6,32,1024]{2,1,0:T(8,128)(2,1)}, bf16[6,32,1024]{2,1,0:T(8,128)(2,1)S(1)}, u32[]{:S(2)}, u32[]{:S(2)}) collective-permute-start(bf16[6,32,1024]{2,1,0:T(8,128)(2,1)} %get-tuple-element.70.refs_1_), channel_id=1, source_target_pairs={{0,96},{32,0},{64,32},{96,64},{1,97},{33,1},{65,33},{97,65},{2,98}... | collective-permute-start | bytes 1179656 | tf_op jit(solution)/shard_map/ppermute | solution.py:368
  194.7 26.1 %collective-permute-start.13 = (bf16[6,32,1024]{2,1,0:T(8,128)(2,1)}, bf16[6,32,1024]{2,1,0:T(8,128)(2,1)}, u32[]{:S(2)}, u32[]{:S(2)}) collective-permute-start(bf16[6,32,1024]{2,1,0:T(8,128)(2,1)} %get-tuple-element.70.refs_1_), channel_id=1, source_target_pairs={{0,32},{32,64},{64,96},{96,0},{1,33},{33,65},{65,97},{97,1},{2,34}... | collective-permute-start | bytes 1179656 | tf_op jit(solution)/shard_map/ppermute | solution.py:369
  194.7 26.1 %collective-permute-start.14 = (bf16[6,32,1024]{2,1,0:T(8,128)(2,1)S(1)}, bf16[6,32,1024]{2,1,0:T(8,128)(2,1)}, u32[]{:S(2)}, u32[]{:S(2)}) collective-permute-start(bf16[6,32,1024]{2,1,0:T(8,128)(2,1)S(1)} %get-tuple-element.69.refs_0_), channel_id=1, source_target_pairs={{0,96},{32,0},{64,32},{96,64},{1,97},{33,1},{65,33},{97,65},{2,98}... | collective-permute-start | bytes 1179656 | tf_op jit(solution)/shard_map/ppermute | solution.py:370
  203.6 18.7 %collective-permute-start.16 = (bf16[6,32,1024]{2,1,0:T(8,128)(2,1)S(1)}, bf16[6,32,1024]{2,1,0:T(8,128)(2,1)}, u32[]{:S(2)}, u32[]{:S(2)}) collective-permute-start(bf16[6,32,1024]{2,1,0:T(8,128)(2,1)S(1)} %collective-permute-done.12.refs_2_.refs_1_), channel_id=1, source_target_pairs={{0,32},{32,64},{64,96},{96,0},{1,33},{33,65},{65,97},{97,1},{2,34}... | collective-permute-start | bytes 1179656 | tf_op jit(solution)/shard_map/ppermute | solution.py:371
  218.0 11.1 %collective-permute-start.18 = (bf16[6,32,1024]{2,1,0:T(8,128)(2,1)S(1)}, bf16[6,32,1024]{2,1,0:T(8,128)(2,1)S(1)}, u32[]{:S(2)}, u32[]{:S(2)}) collective-permute-start(bf16[6,32,1024]{2,1,0:T(8,128)(2,1)S(1)} %get-tuple-element.75.refs_0_), channel_id=1, source_target_pairs={{0,32},{32,64},{64,96},{96,0},{1,33},{33,65},{65,97},{97,1},{2,34}... | collective-permute-start | bytes 1179656 | tf_op jit(solution)/shard_map/ppermute | solution.py:367
  218.1 11.1 %collective-permute-start.21 = (bf16[6,32,1024]{2,1,0:T(8,128)(2,1)S(1)}, bf16[6,32,1024]{2,1,0:T(8,128)(2,1)S(1)}, u32[]{:S(2)}, u32[]{:S(2)}) collective-permute-start(bf16[6,32,1024]{2,1,0:T(8,128)(2,1)S(1)} %get-tuple-element.76.refs_1_), channel_id=1, source_target_pairs={{0,96},{32,0},{64,32},{96,64},{1,97},{33,1},{65,33},{97,65},{2,98}... | collective-permute-start | bytes 1179656 | tf_op jit(solution)/shard_map/ppermute | solution.py:368
  220.8 15.8 %collective-permute-start.17 = (bf16[6,32,1024]{2,1,0:T(8,128)(2,1)S(1)}, bf16[6,32,1024]{2,1,0:T(8,128)(2,1)S(1)}, u32[]{:S(2)}, u32[]{:S(2)}) collective-permute-start(bf16[6,32,1024]{2,1,0:T(8,128)(2,1)S(1)} %collective-permute-done.15.refs_5_.refs_2_), channel_id=1, source_target_pairs={{0,96},{32,0},{64,32},{96,64},{1,97},{33,1},{65,33},{97,65},{2,98}... | collective-permute-start | bytes 1179656 | tf_op jit(solution)/shard_map/ppermute | solution.py:372
  220.8 19.2 %collective-permute-start.19 = (bf16[6,32,1024]{2,1,0:T(8,128)(2,1)S(1)}, bf16[6,32,1024]{2,1,0:T(8,128)(2,1)S(1)}, u32[]{:S(2)}, u32[]{:S(2)}) collective-permute-start(bf16[6,32,1024]{2,1,0:T(8,128)(2,1)S(1)} %get-tuple-element.76.refs_1_), channel_id=1, source_target_pairs={{0,32},{32,64},{64,96},{96,0},{1,33},{33,65},{65,97},{97,1},{2,34}... | collective-permute-start | bytes 1179656 | tf_op jit(solution)/shard_map/ppermute | solution.py:369
  222.3 22.7 %collective-permute-start.20 = (bf16[6,32,1024]{2,1,0:T(8,128)(2,1)S(1)}, bf16[6,32,1024]{2,1,0:T(8,128)(2,1)S(1)}, u32[]{:S(2)}, u32[]{:S(2)}) collective-permute-start(bf16[6,32,1024]{2,1,0:T(8,128)(2,1)S(1)} %get-tuple-element.75.refs_0_), channel_id=1, source_target_pairs={{0,96},{32,0},{64,32},{96,64},{1,97},{33,1},{65,33},{97,65},{2,98}... | collective-permute-start | bytes 1179656 | tf_op jit(solution)/shard_map/ppermute | solution.py:370
  229.2 18.1 %collective-permute-start.22 = (bf16[6,32,1024]{2,1,0:T(8,128)(2,1)S(1)}, bf16[6,32,1024]{2,1,0:T(8,128)(2,1)S(1)}, u32[]{:S(2)}, u32[]{:S(2)}) collective-permute-start(bf16[6,32,1024]{2,1,0:T(8,128)(2,1)S(1)} %collective-permute-done.18.refs_2_), channel_id=1, source_target_pairs={{0,32},{32,64},{64,96},{96,0},{1,33},{33,65},{65,97},{97,1},{2,34}... | collective-permute-start | bytes 1179656 | tf_op jit(solution)/shard_map/ppermute | solution.py:371
  229.2 24.3 %collective-permute-start.23 = (bf16[6,32,1024]{2,1,0:T(8,128)(2,1)S(1)}, bf16[6,32,1024]{2,1,0:T(8,128)(2,1)S(1)}, u32[]{:S(2)}, u32[]{:S(2)}) collective-permute-start(bf16[6,32,1024]{2,1,0:T(8,128)(2,1)S(1)} %collective-permute-done.21.refs_5_), channel_id=1, source_target_pairs={{0,96},{32,0},{64,32},{96,64},{1,97},{33,1},{65,33},{97,65},{2,98}... | collective-permute-start | bytes 1179656 | tf_op jit(solution)/shard_map/ppermute | solution.py:372

commit v5 on v4

--- a/solution.py
+++ b/solution.py
@@ -201,42 +201,54 @@
     )(in_hbm(roots), *[in_vmem(a) for a in arrived])
 
 
-def renew_kernel(count, table, weights, *refs):
-    backs, outs, held, sems = refs[:-4], refs[-4:-2], refs[-2], refs[-1]
-    copies = [pltpu.make_async_copy(weights.at[table[j]], held.at[j], sems.at[j]) for j in range(count)]
+def order_kernel(table, weights, out, sems):
+    copies = [pltpu.make_async_copy(weights.at[table[j]], out.at[j], sems.at[j]) for j in range(out.shape[0])]
     for c in copies:
         c.start()
-    half = count // 2
+    for c in copies:
+        c.wait()
+
+
+def order_blocks(table, weights):
+    count = table.shape[0]
+    return pl.pallas_call(
+        order_kernel,
+        out_shape=pltpu.VMEM((count,) + weights.shape[1:], weights.dtype),
+        in_specs=[SMEM, ANY],
+        out_specs=VMEM,
+        scratch_shapes=[pltpu.SemaphoreType.DMA((count,))],
+        compiler_params=SMALL,
+    )(table, in_hbm(weights))
+
+
+def renew_kernel(first, table, weights, *refs):
+    backs, outs = refs[:-2], refs[-2:]
+    half = outs[0].shape[0]
 
     def block(j, k):
-        grad = backs[k][table[count + j]].astype(jnp.float32)
-        stepped = held[j].astype(jnp.float32) - 0.5 * grad
+        grad = backs[k][table[j]].astype(jnp.float32)
+        stepped = weights[first + j].astype(jnp.float32) - 0.5 * grad
         scale = lax.rsqrt(jnp.mean(stepped * stepped, axis=1, keepdims=True) + 1e-06)
         outs[j // half][j % half] = (stepped * scale).astype(jnp.bfloat16)
 
-    for j in range(count):
-        copies[j].wait()
+    for j in range(2 * half):
         if len(backs) == 1:
             block(j, 0)
             continue
         for k in range(len(backs)):
-            pl.when(table[2 * count + j] == k)(functools.partial(block, j, k))
-
-
-def renew(table, weights, backs):
-    count = table.shape[0] // 3
-    rows, width = weights.shape[1:]
-    half = jax.ShapeDtypeStruct((count // 2, rows, width), jnp.bfloat16)
-    return pl.pallas_call(
-        functools.partial(renew_kernel, count),
+            pl.when(table[2 * half + j] == k)(functools.partial(block, j, k))
+
+
+def renew(table, weights, backs, first):
+    count = table.shape[0] // 2
+    half = pltpu.VMEM((count // 2,) + weights.shape[1:], jnp.bfloat16)
+    return pl.pallas_call(
+        functools.partial(renew_kernel, first),
         out_shape=(half, half),
-        in_specs=[SMEM, ANY] + [VMEM] * len(backs),
-        scratch_shapes=[
-            pltpu.VMEM((count, rows, width), jnp.bfloat16),
-            pltpu.SemaphoreType.DMA((count,)),
-        ],
+        in_specs=[SMEM] + [VMEM] * (1 + len(backs)),
+        out_specs=(VMEM, VMEM),
         compiler_params=SMALL,
-    )(table, in_hbm(weights), *[in_vmem(x) for x in backs])
+    )(table, in_vmem(weights), *[in_vmem(x) for x in backs])
 
 
 def pass_kernel(count, *refs):
@@ -380,17 +392,18 @@
         return jnp.concatenate(out)
 
     def table(lo, hi):
-        return jnp.concatenate([t[lo:hi] for t in by_order])
+        return jnp.concatenate([t[lo:hi] for t in by_order[1:]])
 
     out_shape = jax.ShapeDtypeStruct((total_blocks, rows, width), jnp.bfloat16)
     where = places(half, nbg)
     far = 3 * half
-    tables = [table(0, half), table(half, nbg), places(0, half), where[:far], where[far:]]
+    tables = [table(0, half), table(half, nbg), places(0, half), where[:far], where[far:], by_order[0]]
     tables = pass_tables(tables)
-    new = renew(tables[0], weights, backs[:1])
+    ordered = order_blocks(tables[5], weights)
+    new = renew(tables[0], ordered, backs[:1], 0)
     pieces0 = to_all(new)
     late = pass_tables(tables[1:2], [pieces0[2], pieces0[5]])
-    new = renew(late[0], weights, backs)
+    new = renew(late[0], ordered, backs, half)
     pieces1 = to_all(new)
     out = scatter_blocks(tables[2], pieces0, out_shape)
     out = scatter_blocks(tables[3], pieces1[:6], out_shape, base=out)

time: 258 us -> 258 us (level)
    pallas_call x2 -> x3, Pallas kernels: 9.03 us -> 8.15 us  [the longest x2 6 us: renew(): pl.pallas_call(functools.partial(renew_kernel, first), out_shape=(half, h...]
  transfers between devices with their start and end apart: 28 -> 28, of which waited for: 18 -> 18; matrix products, arithmetic and copies ran while one was open for 3% -> 3% of each run, Pallas kernels for 21% -> 20%
where the time goes in v5:
time: 258 us; the launch traced here: 256 us
  waiting for transfers between devices  106 us (41%)
  Pallas kernels  57.1 us (22%)
  starting transfers between devices  54.3 us (21%)
  blocking collectives  27.4 us (11%)
  local copies, waits for them, and re-layouts  8.39 us (3%)
    ppermute x12, waiting for transfers between devices, body(): lax.ppermute(p, 'groups', shift(n))  49.3 us
    all_to_all x4, waiting for transfers between devices, exchange(): return lax.all_to_all(x, 'shard', 0, 0, tiled=True)  29.1 us
    all_to_all x1, blocking collectives, exchange(): return lax.all_to_all(x, 'shard', 0, 0, tiled=True)  27.4 us
    pallas_call x2, Pallas kernels, owner_work(): pl.pallas_call(functools.partial(owner_kernel, slot), out_shape=pltpu.HBM...  24.8 us
    all_to_all x4, starting transfers between devices, exchange(): return lax.all_to_all(x, 'shard', 0, 0, tiled=True)  23.6 us
    ppermute x12, starting transfers between devices, body(): lax.ppermute(p, 'groups', shift(n))  17.2 us
    pallas_call x4, Pallas kernels, sum_replicas(): pl.pallas_call(functools.partial(sum_kernel, start, offset, before is Non...  14.8 us
    ppermute x2, waiting for transfers between devices, to_all(): prev_a = lax.ppermute(a, 'groups', shift(1))  11.8 us
  transfers between devices with their start and end apart: 28, of which 18 were waited for; matrix products, arithmetic and copies ran while one was open for 3% of the time, Pallas kernels for 20%

profile of v5, /device:TPU:1, one launch (start us, length us, event | category | flops | bytes accessed | tf_op | source)
XLA Modules:
  0.0 255.6 jit_solution(3797174510967084765)
XLA Ops:
  16.0 7.6 %collective-permute-done.5.three = bf16[24,8,1024]{2,1,0:T(8,128)(2,1)S(1)} collective-permute-done((bf16[24,8,1024]{2,1,0:T(8,128)(2,1)S(1)}, bf16[24,8,1024]{2,1,0:T(8,128)(2,1)S(1)}, u32[]{:S(2)}, u32[]{:S(2)}) %collective-permute-start.5) | collective-permute-done | bytes 393248 | tf_op jit(solution)/shard_map/ppermute | solution.py:325
  23.6 3.5 %shard_map.57 = (s16[32,2,16,1152]{3,2,1,0:T(8,128)(2,1)}, f32[24,1,128]{2,1,0:T(1,128)S(1)}) custom-call(s32[49]{0:T(128)S(1)} %pad_add_fusion.4.meta, bf16[1,96,32,1024]{3,2,1,0:T(8,128)(2,1)} %gradients.7, bf16[24,8,1024]{2,1,0:T(8,128)(2,1)S(1)} %collective-permute-done.3.one, bf16[24,8,1024]{2,1,0:T(8,128)(2,1)S(1)} %collective-permute-done.4.two, ...), custom_call_target="tpu_custom_call" | custom-call | tf_op jit(solution)/shard_map/pallas_call | solution.py:117
  27.1 3.6 %collective-permute-done.one = bf16[24,8,1024]{2,1,0:T(8,128)(2,1)S(1)} collective-permute-done((bf16[24,8,1024]{2,1,0:T(8,128)(2,1)}, bf16[24,8,1024]{2,1,0:T(8,128)(2,1)S(1)}, u32[]{:S(2)}, u32[]{:S(2)}) %collective-permute-start) | collective-permute-done | bytes 393248 | tf_op jit(solution)/shard_map/ppermute | solution.py:325
  30.9 9.5 %collective-permute-done.2.three = bf16[24,8,1024]{2,1,0:T(8,128)(2,1)S(1)} collective-permute-done((bf16[24,8,1024]{2,1,0:T(8,128)(2,1)S(1)}, bf16[24,8,1024]{2,1,0:T(8,128)(2,1)S(1)}, u32[]{:S(2)}, u32[]{:S(2)}) %collective-permute-start.2) | collective-permute-done | bytes 393248 | tf_op jit(solution)/shard_map/ppermute | solution.py:325
  40.4 3.5 %shard_map.58 = (s16[32,2,16,1152]{3,2,1,0:T(8,128)(2,1)}, f32[24,1,128]{2,1,0:T(1,128)S(1)}) custom-call(s32[49]{0:T(128)S(1)} %pad_add_fusion.4.meta, bf16[1,96,32,1024]{3,2,1,0:T(8,128)(2,1)} %gradients.7, bf16[24,8,1024]{2,1,0:T(8,128)(2,1)S(1)} %collective-permute-done.one, ...), custom_call_target="tpu_custom_call", output_to_operand_aliasing={{0}: (7, {})} | custom-call | tf_op jit(solution)/shard_map/pallas_call | solution.py:117
  44.0 9.6 %all-to-all-start = ((s16[32,2,16,1152]{3,2,1,0:T(8,128)(2,1)}), s16[32,2,16,1152]{3,2,1,0:T(8,128)(2,1)S(1)}, u32[]{:S(2)}, u32[]{:S(2)}) async-start(s16[32,2,16,1152]{3,2,1,0:T(8,128)(2,1)} %get-tuple-element.56), calls=%async_computation | async-start | bytes 4718592 | tf_op jit(solution)/shard_map/all_to_all | solution.py:349
  62.0 3.4 %collective-permute-done.10.two = bf16[24,8,1024]{2,1,0:T(8,128)(2,1)S(1)} collective-permute-done((bf16[24,8,1024]{2,1,0:T(8,128)(2,1)S(1)}, bf16[24,8,1024]{2,1,0:T(8,128)(2,1)S(1)}, u32[]{:S(2)}, u32[]{:S(2)}) %collective-permute-start.10) | collective-permute-done | bytes 393248 | tf_op jit(solution)/shard_map/ppermute | solution.py:325
  68.6 9.3 %collective-permute-done.9.one = bf16[24,8,1024]{2,1,0:T(8,128)(2,1)S(1)} collective-permute-done((bf16[24,8,1024]{2,1,0:T(8,128)(2,1)S(1)}, bf16[24,8,1024]{2,1,0:T(8,128)(2,1)S(1)}, u32[]{:S(2)}, u32[]{:S(2)}) %collective-permute-start.9) | collective-permute-done | bytes 393248 | tf_op jit(solution)/shard_map/ppermute | solution.py:325
  77.8 3.5 %shard_map.59 = (s16[32,16,1152]{2,1,0:T(8,128)(2,1)}, s16[32,16,1152]{2,1,0:T(8,128)(2,1)}, f32[24,1,128]{2,1,0:T(1,128)S(1)}) custom-call(s32[49]{0:T(128)S(1)} %pad_add_fusion.4.meta, bf16[1,96,32,1024]{3,2,1,0:T(8,128)(2,1)} %gradients.7, bf16[24,8,1024]{2,1,0:T(8,128)(2,1)S(1)} %collective-permute-done.9.one, ...), custom_call_target="tpu_custom_call" | custom-call | tf_op jit(solution)/shard_map/pallas_call | solution.py:117
  81.4 5.7 %collective-permute-done.6.one = bf16[24,8,1024]{2,1,0:T(8,128)(2,1)S(1)} collective-permute-done((bf16[24,8,1024]{2,1,0:T(8,128)(2,1)S(1)}, bf16[24,8,1024]{2,1,0:T(8,128)(2,1)S(1)}, u32[]{:S(2)}, u32[]{:S(2)}) %collective-permute-start.6) | collective-permute-done | bytes 393248 | tf_op jit(solution)/shard_map/ppermute | solution.py:325
  87.1 6.8 %collective-permute-done.8.three = bf16[24,8,1024]{2,1,0:T(8,128)(2,1)S(1)} collective-permute-done((bf16[24,8,1024]{2,1,0:T(8,128)(2,1)S(1)}, bf16[24,8,1024]{2,1,0:T(8,128)(2,1)S(1)}, u32[]{:S(2)}, u32[]{:S(2)}) %collective-permute-start.8) | collective-permute-done | bytes 393248 | tf_op jit(solution)/shard_map/ppermute | solution.py:325
  93.9 4.2 %shard_map.60 = (s16[32,16,1152]{2,1,0:T(8,128)(2,1)}, s16[32,16,1152]{2,1,0:T(8,128)(2,1)}) custom-call(s32[49]{0:T(128)S(1)} %pad_add_fusion.4.meta, bf16[1,96,32,1024]{3,2,1,0:T(8,128)(2,1)} %gradients.7, bf16[24,8,1024]{2,1,0:T(8,128)(2,1)S(1)} %collective-permute-done.6.one, ...), custom_call_target="tpu_custom_call", output_to_operand_aliasing={{0}: (7, {}), {1}: (8, {})} | custom-call | tf_op jit(solution)/shard_map/pallas_call | solution.py:117
  98.0 27.4 %all_to_all.25.refs_1_ = s16[32,16,1152]{2,1,0:T(8,128)(2,1)} all-to-all(s16[32,16,1152]{2,1,0:T(8,128)(2,1)} %get-tuple-element.70), channel_id=1, replica_groups=mesh['groups'=4,'shard'=32] {'shard'}, dimensions={0} | all-to-all | bytes 2359296 | tf_op jit(solution)/shard_map/all_to_all | solution.py:349
  125.4 4.0 %all-to-all-start.3 = ((s16[32,16,1152]{2,1,0:T(8,128)(2,1)}), s16[32,16,1152]{2,1,0:T(8,128)(2,1)S(1)}, u32[]{:S(2)}, u32[]{:S(2)}) async-start(s16[32,16,1152]{2,1,0:T(8,128)(2,1)} %get-tuple-element.75), calls=%async_computation.3 | async-start | bytes 2359296 | tf_op jit(solution)/shard_map/all_to_all | solution.py:349
  130.7 12.4 %shard_map.61 = bf16[1024,1024]{1,0:T(8,128)(2,1)} custom-call(bf16[1,1,2,2,1024,1024]{5,4,3,2,1,0:T(8,128)(2,1)} %all_roots.3, s16[32,2,16,1152]{3,2,1,0:T(8,128)(2,1)S(1)} %all-to-all-done.refs_0_, s16[32,16,1152]{2,1,0:T(8,128)(2,1)S(1)} %copy-done), custom_call_target="tpu_custom_call" | custom-call | tf_op jit(solution)/shard_map/pallas_call | solution.py:186
  143.1 4.8 %all-to-all-done.3.refs_1_ = s16[32,16,1152]{2,1,0:T(8,128)(2,1)S(1)} async-done(((s16[32,16,1152]{2,1,0:T(8,128)(2,1)}), s16[32,16,1152]{2,1,0:T(8,128)(2,1)S(1)}, u32[]{:S(2)}, u32[]{:S(2)}) %all-to-all-start.3) | async-done | bytes 1179680 | tf_op jit(solution)/shard_map/all_to_all | solution.py:349
  147.9 4.8 %all-to-all-start.2 = ((bf16[32,32,1024]{2,1,0:T(8,128)(2,1)}), bf16[32,32,1024]{2,1,0:T(8,128)(2,1)}, u32[]{:S(2)}, u32[]{:S(2)}) async-start(bf16[32,32,1024]{2,1,0:T(8,128)(2,1)} %bitcast.54), calls=%async_computation.2 | async-start | bytes 4194304 | tf_op jit(solution)/shard_map/all_to_all | solution.py:349
  153.4 12.5 %shard_map.65 = bf16[1024,1024]{1,0:T(8,128)(2,1)} custom-call(bf16[1,1,2,2,1024,1024]{5,4,3,2,1,0:T(8,128)(2,1)} %all_roots.3, s16[32,2,16,1152]{3,2,1,0:T(8,128)(2,1)S(1)} %all-to-all-done.refs_0_, s16[32,16,1152]{2,1,0:T(8,128)(2,1)S(1)} %all-to-all-done.3.refs_1_), custom_call_target="tpu_custom_call" | custom-call | tf_op jit(solution)/shard_map/pallas_call | solution.py:186
  165.8 15.0 %all-to-all-done.2.refs_0_ = bf16[32,32,1024]{2,1,0:T(8,128)(2,1)} async-done(((bf16[32,32,1024]{2,1,0:T(8,128)(2,1)}), bf16[32,32,1024]{2,1,0:T(8,128)(2,1)}, u32[]{:S(2)}, u32[]{:S(2)}) %all-to-all-start.2) | async-done | bytes 2097184 | tf_op jit(solution)/shard_map/all_to_all | solution.py:349
  180.8 5.2 %all-to-all-start.4 = ((bf16[32,32,1024]{2,1,0:T(8,128)(2,1)}), bf16[32,32,1024]{2,1,0:T(8,128)(2,1)}, u32[]{:S(2)}, u32[]{:S(2)}) async-start(bf16[32,32,1024]{2,1,0:T(8,128)(2,1)} %bitcast.53), calls=%async_computation.4 | async-start | bytes 4194304 | tf_op jit(solution)/shard_map/all_to_all | solution.py:349
  192.4 2.7 %collective-permute-start.15 = (bf16[6,32,1024]{2,1,0:T(8,128)(2,1)S(1)}, bf16[6,32,1024]{2,1,0:T(8,128)(2,1)S(1)}, u32[]{:S(2)}, u32[]{:S(2)}) collective-permute-start(bf16[6,32,1024]{2,1,0:T(8,128)(2,1)S(1)} %get-tuple-element.72.refs_1_), channel_id=1, source_target_pairs={{0,96},{32,0},{64,32},{96,64},{1,97},{33,1},{65,33},{97,65},{2,98}... | collective-permute-start | bytes 1179656 | tf_op jit(solution)/shard_map/ppermute | solution.py:380
  195.1 2.7 %collective-permute-start.14 = (bf16[6,32,1024]{2,1,0:T(8,128)(2,1)S(1)}, bf16[6,32,1024]{2,1,0:T(8,128)(2,1)}, u32[]{:S(2)}, u32[]{:S(2)}) collective-permute-start(bf16[6,32,1024]{2,1,0:T(8,128)(2,1)S(1)} %get-tuple-element.71.refs_0_), channel_id=1, source_target_pairs={{0,96},{32,0},{64,32},{96,64},{1,97},{33,1},{65,33},{97,65},{2,98}... | collective-permute-start | bytes 1179656 | tf_op jit(solution)/shard_map/ppermute | solution.py:382
  197.8 6.2 %collective-permute-done.12.refs_2_.refs_1_ = bf16[6,32,1024]{2,1,0:T(8,128)(2,1)S(1)} collective-permute-done((bf16[6,32,1024]{2,1,0:T(8,128)(2,1)S(1)}, bf16[6,32,1024]{2,1,0:T(8,128)(2,1)S(1)}, u32[]{:S(2)}, u32[]{:S(2)}) %collective-permute-start.12) | collective-permute-done | bytes 393248 | tf_op jit(solution)/shard_map/ppermute | solution.py:379
  205.2 9.3 %all-to-all-done.4.refs_1_ = bf16[32,32,1024]{2,1,0:T(8,128)(2,1)} async-done(((bf16[32,32,1024]{2,1,0:T(8,128)(2,1)}), bf16[32,32,1024]{2,1,0:T(8,128)(2,1)}, u32[]{:S(2)}, u32[]{:S(2)}) %all-to-all-start.4) | async-done | bytes 2097184 | tf_op jit(solution)/shard_map/all_to_all | solution.py:349
  214.5 4.0 %shard_map.66 = (bf16[6,32,1024]{2,1,0:T(8,128)(2,1)S(1)}, bf16[6,32,1024]{2,1,0:T(8,128)(2,1)S(1)}) custom-call(s32[24]{0:T(128)S(1)} %shard_map.64.table, bf16[24,32,1024]{2,1,0:T(8,128)(2,1)S(1)} %shard_map.56.weights, bf16[32,32,1024]{2,1,0:T(8,128)(2,1)} %all-to-all-done.2.refs_0_, bf16[32,32,1024]{2,1,0:T(8,128)(2,1)} %all-to-all-done.4.refs_1_), custom_call_target="tpu_custom_call" | custom-call | tf_op jit(solution)/shard_map/pallas_call | solution.py:245
  218.6 2.7 %collective-permute-start.21 = (bf16[6,32,1024]{2,1,0:T(8,128)(2,1)S(1)}, bf16[6,32,1024]{2,1,0:T(8,128)(2,1)S(1)}, u32[]{:S(2)}, u32[]{:S(2)}) collective-permute-start(bf16[6,32,1024]{2,1,0:T(8,128)(2,1)S(1)} %get-tuple-element.78.refs_1_), channel_id=1, source_target_pairs={{0,96},{32,0},{64,32},{96,64},{1,97},{33,1},{65,33},{97,65},{2,98}... | collective-permute-start | bytes 1179656 | tf_op jit(solution)/shard_map/ppermute | solution.py:380
  224.0 5.6 %collective-permute-done.18.refs_2_ = bf16[6,32,1024]{2,1,0:T(8,128)(2,1)S(1)} collective-permute-done((bf16[6,32,1024]{2,1,0:T(8,128)(2,1)S(1)}, bf16[6,32,1024]{2,1,0:T(8,128)(2,1)S(1)}, u32[]{:S(2)}, u32[]{:S(2)}) %collective-permute-start.18) | collective-permute-done | bytes 393248 | tf_op jit(solution)/shard_map/ppermute | solution.py:379
  229.6 2.7 %collective-permute-start.23 = (bf16[6,32,1024]{2,1,0:T(8,128)(2,1)S(1)}, bf16[6,32,1024]{2,1,0:T(8,128)(2,1)S(1)}, u32[]{:S(2)}, u32[]{:S(2)}) collective-permute-start(bf16[6,32,1024]{2,1,0:T(8,128)(2,1)S(1)} %collective-permute-done.21.refs_5_), channel_id=1, source_target_pairs={{0,96},{32,0},{64,32},{96,64},{1,97},{33,1},{65,33},{97,65},{2,98}... | collective-permute-start | bytes 1179656 | tf_op jit(solution)/shard_map/ppermute | solution.py:384
  232.3 4.7 %collective-permute-done.17.refs_7_ = bf16[6,32,1024]{2,1,0:T(8,128)(2,1)S(1)} collective-permute-done((bf16[6,32,1024]{2,1,0:T(8,128)(2,1)S(1)}, bf16[6,32,1024]{2,1,0:T(8,128)(2,1)S(1)}, u32[]{:S(2)}, u32[]{:S(2)}) %collective-permute-start.17) | collective-permute-done | bytes 393248 | tf_op jit(solution)/shard_map/ppermute | solution.py:384
  237.0 3.2 %shard_map.63.base = bf16[96,32,1024]{2,1,0:T(8,128)(2,1)} custom-call(s32[48]{0:T(128)S(1)} %get-tuple-element.44.place, bf16[6,32,1024]{2,1,0:T(8,128)(2,1)S(1)} %get-tuple-element.71.refs_0_, bf16[6,32,1024]{2,1,0:T(8,128)(2,1)S(1)} %get-tuple-element.72.refs_1_, bf16[6,32,1024]{2,1,0:T(8,128)(2,1)S(1)} %collective-permute-done.12.refs_2_.refs_1_, ...), custom_call_target="tpu_custom_call" | custom-call | tf_op jit(solution)/shard_map/pallas_call | solution.py:292
  240.2 5.2 %collective-permute-done.20.refs_4_ = bf16[6,32,1024]{2,1,0:T(8,128)(2,1)S(1)} collective-permute-done((bf16[6,32,1024]{2,1,0:T(8,128)(2,1)S(1)}, bf16[6,32,1024]{2,1,0:T(8,128)(2,1)S(1)}, u32[]{:S(2)}, u32[]{:S(2)}) %collective-permute-start.20) | collective-permute-done | bytes 393248 | tf_op jit(solution)/shard_map/ppermute | solution.py:382
  247.7 6.2 %collective-permute-done.23.refs_1_ = bf16[6,32,1024]{2,1,0:T(8,128)(2,1)S(1)} collective-permute-done((bf16[6,32,1024]{2,1,0:T(8,128)(2,1)S(1)}, bf16[6,32,1024]{2,1,0:T(8,128)(2,1)S(1)}, u32[]{:S(2)}, u32[]{:S(2)}) %collective-permute-start.23) | collective-permute-done | bytes 393248 | tf_op jit(solution)/shard_map/ppermute | solution.py:384
  (67 shorter events, 43.8 us)
Async XLA Ops:
  0.0 15.7 %copy-start.1 = (s32[96]{0:T(128)S(1)}, s32[96]{0:T(128)}, u32[]{:S(2)}) copy-start(s32[96]{0:T(128)} %param.8) | copy-start | bytes 1156
  2.1 11.7 %collective-permute-start.3 = (bf16[24,8,1024]{2,1,0:T(8,128)(2,1)S(1)}, bf16[24,8,1024]{2,1,0:T(8,128)(2,1)S(1)}, u32[]{:S(2)}, u32[]{:S(2)}) collective-permute-start(bf16[24,8,1024]{2,1,0:T(8,128)(2,1)S(1)} %get-tuple-element.51), channel_id=1, source_target_pairs={{0,32},{32,64},{64,96},{96,0},{1,33},{33,65},{65,97},{97,1},{2,34}... | collective-permute-start | bytes 1179656 | tf_op jit(solution)/shard_map/ppermute | solution.py:325
  4.1 11.9 %collective-permute-start.4 = (bf16[24,8,1024]{2,1,0:T(8,128)(2,1)}, bf16[24,8,1024]{2,1,0:T(8,128)(2,1)S(1)}, u32[]{:S(2)}, u32[]{:S(2)}) collective-permute-start(bf16[24,8,1024]{2,1,0:T(8,128)(2,1)} %get-tuple-element.52), channel_id=1, source_target_pairs={{0,96},{32,0},{64,32},{96,64},{1,97},{33,1},{65,33},{97,65},{2,98}... | collective-permute-start | bytes 1179656 | tf_op jit(solution)/shard_map/ppermute | solution.py:325
  5.4 18.2 %collective-permute-start.5 = (bf16[24,8,1024]{2,1,0:T(8,128)(2,1)S(1)}, bf16[24,8,1024]{2,1,0:T(8,128)(2,1)S(1)}, u32[]{:S(2)}, u32[]{:S(2)}) collective-permute-start(bf16[24,8,1024]{2,1,0:T(8,128)(2,1)S(1)} %get-tuple-element.53), channel_id=1, source_target_pairs={{0,64},{32,96},{64,0},{96,32},{1,65},{33,97},{65,1},{97,33},{2,66}... | collective-permute-start | bytes 1179656 | tf_op jit(solution)/shard_map/ppermute | solution.py:325
  9.2 21.5 %collective-permute-start = (bf16[24,8,1024]{2,1,0:T(8,128)(2,1)}, bf16[24,8,1024]{2,1,0:T(8,128)(2,1)S(1)}, u32[]{:S(2)}, u32[]{:S(2)}) collective-permute-start(bf16[24,8,1024]{2,1,0:T(8,128)(2,1)} %get-tuple-element.48), channel_id=1, source_target_pairs={{0,32},{32,64},{64,96},{96,0},{1,33},{33,65},{65,97},{97,1},{2,34}... | collective-permute-start | bytes 1179656 | tf_op jit(solution)/shard_map/ppermute | solution.py:325
  9.5 21.4 %collective-permute-start.1 = (bf16[24,8,1024]{2,1,0:T(8,128)(2,1)S(1)}, bf16[24,8,1024]{2,1,0:T(8,128)(2,1)S(1)}, u32[]{:S(2)}, u32[]{:S(2)}) collective-permute-start(bf16[24,8,1024]{2,1,0:T(8,128)(2,1)S(1)} %get-tuple-element.49), channel_id=1, source_target_pairs={{0,96},{32,0},{64,32},{96,64},{1,97},{33,1},{65,33},{97,65},{2,98}... | collective-permute-start | bytes 1179656 | tf_op jit(solution)/shard_map/ppermute | solution.py:325
  13.8 26.6 %collective-permute-start.2 = (bf16[24,8,1024]{2,1,0:T(8,128)(2,1)S(1)}, bf16[24,8,1024]{2,1,0:T(8,128)(2,1)S(1)}, u32[]{:S(2)}, u32[]{:S(2)}) collective-permute-start(bf16[24,8,1024]{2,1,0:T(8,128)(2,1)S(1)} %get-tuple-element.50), channel_id=1, source_target_pairs={{0,64},{32,96},{64,0},{96,32},{1,65},{33,97},{65,1},{97,33},{2,66}... | collective-permute-start | bytes 1179656 | tf_op jit(solution)/shard_map/ppermute | solution.py:325
  44.0 54.1 %all-to-all-start = ((s16[32,2,16,1152]{3,2,1,0:T(8,128)(2,1)}), s16[32,2,16,1152]{3,2,1,0:T(8,128)(2,1)S(1)}, u32[]{:S(2)}, u32[]{:S(2)}) async-start(s16[32,2,16,1152]{3,2,1,0:T(8,128)(2,1)} %get-tuple-element.56), calls=%async_computation | async-start | bytes 4718592 | tf_op jit(solution)/shard_map/all_to_all | solution.py:349
  54.9 10.5 %collective-permute-start.10 = (bf16[24,8,1024]{2,1,0:T(8,128)(2,1)S(1)}, bf16[24,8,1024]{2,1,0:T(8,128)(2,1)S(1)}, u32[]{:S(2)}, u32[]{:S(2)}) collective-permute-start(bf16[24,8,1024]{2,1,0:T(8,128)(2,1)S(1)} %get-tuple-element.63), channel_id=1, source_target_pairs={{0,96},{32,0},{64,32},{96,64},{1,97},{33,1},{65,33},{97,65},{2,98}... | collective-permute-start | bytes 1179656 | tf_op jit(solution)/shard_map/ppermute | solution.py:325
  56.9 11.7 %collective-permute-start.11 = (bf16[24,8,1024]{2,1,0:T(8,128)(2,1)S(1)}, bf16[24,8,1024]{2,1,0:T(8,128)(2,1)S(1)}, u32[]{:S(2)}, u32[]{:S(2)}) collective-permute-start(bf16[24,8,1024]{2,1,0:T(8,128)(2,1)S(1)} %get-tuple-element.64), channel_id=1, source_target_pairs={{0,64},{32,96},{64,0},{96,32},{1,65},{33,97},{65,1},{97,33},{2,66}... | collective-permute-start | bytes 1179656 | tf_op jit(solution)/shard_map/ppermute | solution.py:325
  57.9 20.0 %collective-permute-start.9 = (bf16[24,8,1024]{2,1,0:T(8,128)(2,1)S(1)}, bf16[24,8,1024]{2,1,0:T(8,128)(2,1)S(1)}, u32[]{:S(2)}, u32[]{:S(2)}) collective-permute-start(bf16[24,8,1024]{2,1,0:T(8,128)(2,1)S(1)} %get-tuple-element.62), channel_id=1, source_target_pairs={{0,32},{32,64},{64,96},{96,0},{1,33},{33,65},{65,97},{97,1},{2,34}... | collective-permute-start | bytes 1179656 | tf_op jit(solution)/shard_map/ppermute | solution.py:325
  59.2 27.9 %collective-permute-start.6 = (bf16[24,8,1024]{2,1,0:T(8,128)(2,1)S(1)}, bf16[24,8,1024]{2,1,0:T(8,128)(2,1)S(1)}, u32[]{:S(2)}, u32[]{:S(2)}) collective-permute-start(bf16[24,8,1024]{2,1,0:T(8,128)(2,1)S(1)} %get-tuple-element.59), channel_id=1, source_target_pairs={{0,32},{32,64},{64,96},{96,0},{1,33},{33,65},{65,97},{97,1},{2,34}... | collective-permute-start | bytes 1179656 | tf_op jit(solution)/shard_map/ppermute | solution.py:325
  60.9 26.2 %collective-permute-start.7 = (bf16[24,8,1024]{2,1,0:T(8,128)(2,1)S(1)}, bf16[24,8,1024]{2,1,0:T(8,128)(2,1)S(1)}, u32[]{:S(2)}, u32[]{:S(2)}) collective-permute-start(bf16[24,8,1024]{2,1,0:T(8,128)(2,1)S(1)} %get-tuple-element.60), channel_id=1, source_target_pairs={{0,96},{32,0},{64,32},{96,64},{1,97},{33,1},{65,33},{97,65},{2,98}... | collective-permute-start | bytes 1179656 | tf_op jit(solution)/shard_map/ppermute | solution.py:325
  65.5 28.4 %collective-permute-start.8 = (bf16[24,8,1024]{2,1,0:T(8,128)(2,1)S(1)}, bf16[24,8,1024]{2,1,0:T(8,128)(2,1)S(1)}, u32[]{:S(2)}, u32[]{:S(2)}) collective-permute-start(bf16[24,8,1024]{2,1,0:T(8,128)(2,1)S(1)} %get-tuple-element.61), channel_id=1, source_target_pairs={{0,64},{32,96},{64,0},{96,32},{1,65},{33,97},{65,1},{97,33},{2,66}... | collective-permute-start | bytes 1179656 | tf_op jit(solution)/shard_map/ppermute | solution.py:325
  125.4 22.4 %all-to-all-start.3 = ((s16[32,16,1152]{2,1,0:T(8,128)(2,1)}), s16[32,16,1152]{2,1,0:T(8,128)(2,1)S(1)}, u32[]{:S(2)}, u32[]{:S(2)}) async-start(s16[32,16,1152]{2,1,0:T(8,128)(2,1)} %get-tuple-element.75), calls=%async_computation.3 | async-start | bytes 2359296 | tf_op jit(solution)/shard_map/all_to_all | solution.py:349
  129.4 1.3 copy-start
  147.9 33.0 %all-to-all-start.2 = ((bf16[32,32,1024]{2,1,0:T(8,128)(2,1)}), bf16[32,32,1024]{2,1,0:T(8,128)(2,1)}, u32[]{:S(2)}, u32[]{:S(2)}) async-start(bf16[32,32,1024]{2,1,0:T(8,128)(2,1)} %bitcast.54), calls=%async_computation.2 | async-start | bytes 4194304 | tf_op jit(solution)/shard_map/all_to_all | solution.py:349
  180.8 33.7 %all-to-all-start.4 = ((bf16[32,32,1024]{2,1,0:T(8,128)(2,1)}), bf16[32,32,1024]{2,1,0:T(8,128)(2,1)}, u32[]{:S(2)}, u32[]{:S(2)}) async-start(bf16[32,32,1024]{2,1,0:T(8,128)(2,1)} %bitcast.53), calls=%async_computation.4 | async-start | bytes 4194304 | tf_op jit(solution)/shard_map/all_to_all | solution.py:349
  192.4 11.6 %collective-permute-start.12 = (bf16[6,32,1024]{2,1,0:T(8,128)(2,1)S(1)}, bf16[6,32,1024]{2,1,0:T(8,128)(2,1)S(1)}, u32[]{:S(2)}, u32[]{:S(2)}) collective-permute-start(bf16[6,32,1024]{2,1,0:T(8,128)(2,1)S(1)} %get-tuple-element.71.refs_0_), channel_id=1, source_target_pairs={{0,32},{32,64},{64,96},{96,0},{1,33},{33,65},{65,97},{97,1},{2,34}... | collective-permute-start | bytes 1179656 | tf_op jit(solution)/shard_map/ppermute | solution.py:379
  192.4 11.6 %collective-permute-start.15 = (bf16[6,32,1024]{2,1,0:T(8,128)(2,1)S(1)}, bf16[6,32,1024]{2,1,0:T(8,128)(2,1)S(1)}, u32[]{:S(2)}, u32[]{:S(2)}) collective-permute-start(bf16[6,32,1024]{2,1,0:T(8,128)(2,1)S(1)} %get-tuple-element.72.refs_1_), channel_id=1, source_target_pairs={{0,96},{32,0},{64,32},{96,64},{1,97},{33,1},{65,33},{97,65},{2,98}... | collective-permute-start | bytes 1179656 | tf_op jit(solution)/shard_map/ppermute | solution.py:380
  195.1 26.1 %collective-permute-start.13 = (bf16[6,32,1024]{2,1,0:T(8,128)(2,1)S(1)}, bf16[6,32,1024]{2,1,0:T(8,128)(2,1)S(1)}, u32[]{:S(2)}, u32[]{:S(2)}) collective-permute-start(bf16[6,32,1024]{2,1,0:T(8,128)(2,1)S(1)} %get-tuple-element.72.refs_1_), channel_id=1, source_target_pairs={{0,32},{32,64},{64,96},{96,0},{1,33},{33,65},{65,97},{97,1},{2,34}... | collective-permute-start | bytes 1179656 | tf_op jit(solution)/shard_map/ppermute | solution.py:381
  195.1 26.1 %collective-permute-start.14 = (bf16[6,32,1024]{2,1,0:T(8,128)(2,1)S(1)}, bf16[6,32,1024]{2,1,0:T(8,128)(2,1)}, u32[]{:S(2)}, u32[]{:S(2)}) collective-permute-start(bf16[6,32,1024]{2,1,0:T(8,128)(2,1)S(1)} %get-tuple-element.71.refs_0_), channel_id=1, source_target_pairs={{0,96},{32,0},{64,32},{96,64},{1,97},{33,1},{65,33},{97,65},{2,98}... | collective-permute-start | bytes 1179656 | tf_op jit(solution)/shard_map/ppermute | solution.py:382
  204.0 18.7 %collective-permute-start.16 = (bf16[6,32,1024]{2,1,0:T(8,128)(2,1)S(1)}, bf16[6,32,1024]{2,1,0:T(8,128)(2,1)}, u32[]{:S(2)}, u32[]{:S(2)}) collective-permute-start(bf16[6,32,1024]{2,1,0:T(8,128)(2,1)S(1)} %collective-permute-done.12.refs_2_.refs_1_), channel_id=1, source_target_pairs={{0,32},{32,64},{64,96},{96,0},{1,33},{33,65},{65,97},{97,1},{2,34}... | collective-permute-start | bytes 1179656 | tf_op jit(solution)/shard_map/ppermute | solution.py:383
  218.5 11.1 %collective-permute-start.18 = (bf16[6,32,1024]{2,1,0:T(8,128)(2,1)S(1)}, bf16[6,32,1024]{2,1,0:T(8,128)(2,1)S(1)}, u32[]{:S(2)}, u32[]{:S(2)}) collective-permute-start(bf16[6,32,1024]{2,1,0:T(8,128)(2,1)S(1)} %get-tuple-element.77.refs_0_), channel_id=1, source_target_pairs={{0,32},{32,64},{64,96},{96,0},{1,33},{33,65},{65,97},{97,1},{2,34}... | collective-permute-start | bytes 1179656 | tf_op jit(solution)/shard_map/ppermute | solution.py:379
  218.6 11.1 %collective-permute-start.21 = (bf16[6,32,1024]{2,1,0:T(8,128)(2,1)S(1)}, bf16[6,32,1024]{2,1,0:T(8,128)(2,1)S(1)}, u32[]{:S(2)}, u32[]{:S(2)}) collective-permute-start(bf16[6,32,1024]{2,1,0:T(8,128)(2,1)S(1)} %get-tuple-element.78.refs_1_), channel_id=1, source_target_pairs={{0,96},{32,0},{64,32},{96,64},{1,97},{33,1},{65,33},{97,65},{2,98}... | collective-permute-start | bytes 1179656 | tf_op jit(solution)/shard_map/ppermute | solution.py:380
  221.2 15.8 %collective-permute-start.17 = (bf16[6,32,1024]{2,1,0:T(8,128)(2,1)S(1)}, bf16[6,32,1024]{2,1,0:T(8,128)(2,1)S(1)}, u32[]{:S(2)}, u32[]{:S(2)}) collective-permute-start(bf16[6,32,1024]{2,1,0:T(8,128)(2,1)S(1)} %collective-permute-done.15.refs_5_.refs_2_), channel_id=1, source_target_pairs={{0,96},{32,0},{64,32},{96,64},{1,97},{33,1},{65,33},{97,65},{2,98}... | collective-permute-start | bytes 1179656 | tf_op jit(solution)/shard_map/ppermute | solution.py:384
  221.3 19.0 %collective-permute-start.19 = (bf16[6,32,1024]{2,1,0:T(8,128)(2,1)S(1)}, bf16[6,32,1024]{2,1,0:T(8,128)(2,1)S(1)}, u32[]{:S(2)}, u32[]{:S(2)}) collective-permute-start(bf16[6,32,1024]{2,1,0:T(8,128)(2,1)S(1)} %get-tuple-element.78.refs_1_), channel_id=1, source_target_pairs={{0,32},{32,64},{64,96},{96,0},{1,33},{33,65},{65,97},{97,1},{2,34}... | collective-permute-start | bytes 1179656 | tf_op jit(solution)/shard_map/ppermute | solution.py:381
  222.7 22.7 %collective-permute-start.20 = (bf16[6,32,1024]{2,1,0:T(8,128)(2,1)S(1)}, bf16[6,32,1024]{2,1,0:T(8,128)(2,1)S(1)}, u32[]{:S(2)}, u32[]{:S(2)}) collective-permute-start(bf16[6,32,1024]{2,1,0:T(8,128)(2,1)S(1)} %get-tuple-element.77.refs_0_), channel_id=1, source_target_pairs={{0,96},{32,0},{64,32},{96,64},{1,97},{33,1},{65,33},{97,65},{2,98}... | collective-permute-start | bytes 1179656 | tf_op jit(solution)/shard_map/ppermute | solution.py:382
  229.6 18.1 %collective-permute-start.22 = (bf16[6,32,1024]{2,1,0:T(8,128)(2,1)S(1)}, bf16[6,32,1024]{2,1,0:T(8,128)(2,1)S(1)}, u32[]{:S(2)}, u32[]{:S(2)}) collective-permute-start(bf16[6,32,1024]{2,1,0:T(8,128)(2,1)S(1)} %collective-permute-done.18.refs_2_), channel_id=1, source_target_pairs={{0,32},{32,64},{64,96},{96,0},{1,33},{33,65},{65,97},{97,1},{2,34}... | collective-permute-start | bytes 1179656 | tf_op jit(solution)/shard_map/ppermute | solution.py:383
  229.6 24.3 %collective-permute-start.23 = (bf16[6,32,1024]{2,1,0:T(8,128)(2,1)S(1)}, bf16[6,32,1024]{2,1,0:T(8,128)(2,1)S(1)}, u32[]{:S(2)}, u32[]{:S(2)}) collective-permute-start(bf16[6,32,1024]{2,1,0:T(8,128)(2,1)S(1)} %collective-permute-done.21.refs_5_), channel_id=1, source_target_pairs={{0,96},{32,0},{64,32},{96,64},{1,97},{33,1},{65,33},{97,65},{2,98}... | collective-permute-start | bytes 1179656 | tf_op jit(solution)/shard_map/ppermute | solution.py:384

commit v6 on v5

--- a/solution.py
+++ b/solution.py
@@ -221,34 +221,38 @@
     )(table, in_hbm(weights))
 
 
-def renew_kernel(first, table, weights, *refs):
-    backs, outs = refs[:-2], refs[-2:]
+def renew_kernel(first, slot, table, weights, back, *refs):
+    outs = refs[-2:]
+    made = refs[:-2]
     half = outs[0].shape[0]
 
-    def block(j, k):
-        grad = backs[k][table[j]].astype(jnp.float32)
+    def block(j):
+        grad = back[table[j]].astype(jnp.float32)
         stepped = weights[first + j].astype(jnp.float32) - 0.5 * grad
         scale = lax.rsqrt(jnp.mean(stepped * stepped, axis=1, keepdims=True) + 1e-06)
         outs[j // half][j % half] = (stepped * scale).astype(jnp.bfloat16)
 
+    def keep(j):
+        outs[j // half][j % half] = made[j // half][j % half]
+
     for j in range(2 * half):
-        if len(backs) == 1:
-            block(j, 0)
+        if not made:
+            block(j)
             continue
-        for k in range(len(backs)):
-            pl.when(table[2 * half + j] == k)(functools.partial(block, j, k))
-
-
-def renew(table, weights, backs, first):
+        pl.when(table[2 * half + j] == slot)(functools.partial(block, j))
+        pl.when(table[2 * half + j] != slot)(functools.partial(keep, j))
+
+
+def renew(table, weights, back, first, slot, made=()):
     count = table.shape[0] // 2
     half = pltpu.VMEM((count // 2,) + weights.shape[1:], jnp.bfloat16)
     return pl.pallas_call(
-        functools.partial(renew_kernel, first),
+        functools.partial(renew_kernel, first, slot),
         out_shape=(half, half),
-        in_specs=[SMEM] + [VMEM] * (1 + len(backs)),
+        in_specs=[SMEM] + [VMEM] * (2 + len(made)),
         out_specs=(VMEM, VMEM),
         compiler_params=SMALL,
-    )(table, in_vmem(weights), *[in_vmem(x) for x in backs])
+    )(table, in_vmem(weights), in_vmem(back), *[in_vmem(x) for x in made])
 
 
 def pass_kernel(count, *refs):
@@ -400,10 +404,11 @@
     tables = [table(0, half), table(half, nbg), places(0, half), where[:far], where[far:], by_order[0]]
     tables = pass_tables(tables)
     ordered = order_blocks(tables[5], weights)
-    new = renew(tables[0], ordered, backs[:1], 0)
+    new = renew(tables[0], ordered, backs[0], 0, 0)
     pieces0 = to_all(new)
     late = pass_tables(tables[1:2], [pieces0[2], pieces0[5]])
-    new = renew(late[0], ordered, backs, half)
+    made = renew(late[0], ordered, backs[0], half, 0)
+    new = renew(late[0], ordered, backs[1], half, 1, made)
     pieces1 = to_all(new)
     out = scatter_blocks(tables[2], pieces0, out_shape)
     out = scatter_blocks(tables[3], pieces1[:6], out_shape, base=out)

time: 258 us -> 259 us (level)
  local copies, waits for them, and re-layouts: 8.39 us -> 11.9 us
  waiting for transfers between devices: 106 us -> 103 us
    all_to_all x4, waiting for transfers between devices: 29.1 us -> 25.6 us  [exchange(): return lax.all_to_all(x, 'shard', 0, 0, tiled=True)]
    unnamed x4 -> x12, local copies, waits for them, and re-layouts: 1.27 us -> 4.76 us
    pallas_call x2 -> x3, Pallas kernels: 6 us -> 6.63 us  [renew(): pl.pallas_call(functools.partial(renew_kernel, first, slot), out_shape=(h...]
  transfers between devices with their start and end apart: 28 -> 28, of which waited for: 18 -> 18; matrix products, arithmetic and copies ran while one was open for 3% -> 3% of each run, Pallas kernels for 20% -> 21%
where the time goes in v6:
time: 259 us; the launch traced here: 256 us
  waiting for transfers between devices  103 us (40%)
  Pallas kernels  57.8 us (22%)
  starting transfers between devices  54.3 us (21%)
  blocking collectives  27.4 us (11%)
  local copies, waits for them, and re-layouts  11.9 us (5%)
    ppermute x12, waiting for transfers between devices, body(): lax.ppermute(p, 'groups', shift(n))  49.3 us
    all_to_all x1, blocking collectives, exchange(): return lax.all_to_all(x, 'shard', 0, 0, tiled=True)  27.4 us
    all_to_all x4, waiting for transfers between devices, exchange(): return lax.all_to_all(x, 'shard', 0, 0, tiled=True)  25.6 us
    pallas_call x2, Pallas kernels, owner_work(): pl.pallas_call(functools.partial(owner_kernel, slot), out_shape=pltpu.HBM...  24.9 us
    all_to_all x4, starting transfers between devices, exchange(): return lax.all_to_all(x, 'shard', 0, 0, tiled=True)  23.6 us
    ppermute x12, starting transfers between devices, body(): lax.ppermute(p, 'groups', shift(n))  17.2 us
    pallas_call x4, Pallas kernels, sum_replicas(): pl.pallas_call(functools.partial(sum_kernel, start, offset, before is Non...  14.8 us
    ppermute x2, waiting for transfers between devices, to_all(): prev_a = lax.ppermute(a, 'groups', shift(1))  11.8 us
  transfers between devices with their start and end apart: 28, of which 18 were waited for; matrix products, arithmetic and copies ran while one was open for 3% of the time, Pallas kernels for 21%

profile of v6, /device:TPU:1, one launch (start us, length us, event | category | flops | bytes accessed | tf_op | source)
XLA Modules:
  0.0 256.2 jit_solution(8122052952624268745)
XLA Ops:
  16.0 7.6 %collective-permute-done.5.three = bf16[24,8,1024]{2,1,0:T(8,128)(2,1)S(1)} collective-permute-done((bf16[24,8,1024]{2,1,0:T(8,128)(2,1)S(1)}, bf16[24,8,1024]{2,1,0:T(8,128)(2,1)S(1)}, u32[]{:S(2)}, u32[]{:S(2)}) %collective-permute-start.5) | collective-permute-done | bytes 393248 | tf_op jit(solution)/shard_map/ppermute | solution.py:329
  23.6 3.5 %shard_map.57 = (s16[32,2,16,1152]{3,2,1,0:T(8,128)(2,1)}, f32[24,1,128]{2,1,0:T(1,128)S(1)}) custom-call(s32[49]{0:T(128)S(1)} %pad_add_fusion.4.meta, bf16[1,96,32,1024]{3,2,1,0:T(8,128)(2,1)} %gradients.7, bf16[24,8,1024]{2,1,0:T(8,128)(2,1)S(1)} %collective-permute-done.3.one, bf16[24,8,1024]{2,1,0:T(8,128)(2,1)S(1)} %collective-permute-done.4.two, ...), custom_call_target="tpu_custom_call" | custom-call | tf_op jit(solution)/shard_map/pallas_call | solution.py:117
  27.1 3.6 %collective-permute-done.one = bf16[24,8,1024]{2,1,0:T(8,128)(2,1)S(1)} collective-permute-done((bf16[24,8,1024]{2,1,0:T(8,128)(2,1)}, bf16[24,8,1024]{2,1,0:T(8,128)(2,1)S(1)}, u32[]{:S(2)}, u32[]{:S(2)}) %collective-permute-start) | collective-permute-done | bytes 393248 | tf_op jit(solution)/shard_map/ppermute | solution.py:329
  30.9 9.5 %collective-permute-done.2.three = bf16[24,8,1024]{2,1,0:T(8,128)(2,1)S(1)} collective-permute-done((bf16[24,8,1024]{2,1,0:T(8,128)(2,1)S(1)}, bf16[24,8,1024]{2,1,0:T(8,128)(2,1)S(1)}, u32[]{:S(2)}, u32[]{:S(2)}) %collective-permute-start.2) | collective-permute-done | bytes 393248 | tf_op jit(solution)/shard_map/ppermute | solution.py:329
  40.4 3.5 %shard_map.58 = (s16[32,2,16,1152]{3,2,1,0:T(8,128)(2,1)}, f32[24,1,128]{2,1,0:T(1,128)S(1)}) custom-call(s32[49]{0:T(128)S(1)} %pad_add_fusion.4.meta, bf16[1,96,32,1024]{3,2,1,0:T(8,128)(2,1)} %gradients.7, bf16[24,8,1024]{2,1,0:T(8,128)(2,1)S(1)} %collective-permute-done.one, ...), custom_call_target="tpu_custom_call", output_to_operand_aliasing={{0}: (7, {})} | custom-call | tf_op jit(solution)/shard_map/pallas_call | solution.py:117
  44.0 9.6 %all-to-all-start = ((s16[32,2,16,1152]{3,2,1,0:T(8,128)(2,1)}), s16[32,2,16,1152]{3,2,1,0:T(8,128)(2,1)S(1)}, u32[]{:S(2)}, u32[]{:S(2)}) async-start(s16[32,2,16,1152]{3,2,1,0:T(8,128)(2,1)} %get-tuple-element.58), calls=%async_computation | async-start | bytes 4718592 | tf_op jit(solution)/shard_map/all_to_all | solution.py:353
  62.0 3.4 %collective-permute-done.10.two = bf16[24,8,1024]{2,1,0:T(8,128)(2,1)S(1)} collective-permute-done((bf16[24,8,1024]{2,1,0:T(8,128)(2,1)S(1)}, bf16[24,8,1024]{2,1,0:T(8,128)(2,1)S(1)}, u32[]{:S(2)}, u32[]{:S(2)}) %collective-permute-start.10) | collective-permute-done | bytes 393248 | tf_op jit(solution)/shard_map/ppermute | solution.py:329
  68.6 9.3 %collective-permute-done.9.one = bf16[24,8,1024]{2,1,0:T(8,128)(2,1)S(1)} collective-permute-done((bf16[24,8,1024]{2,1,0:T(8,128)(2,1)S(1)}, bf16[24,8,1024]{2,1,0:T(8,128)(2,1)S(1)}, u32[]{:S(2)}, u32[]{:S(2)}) %collective-permute-start.9) | collective-permute-done | bytes 393248 | tf_op jit(solution)/shard_map/ppermute | solution.py:329
  77.8 3.5 %shard_map.59 = (s16[32,16,1152]{2,1,0:T(8,128)(2,1)}, s16[32,16,1152]{2,1,0:T(8,128)(2,1)}, f32[24,1,128]{2,1,0:T(1,128)S(1)}) custom-call(s32[49]{0:T(128)S(1)} %pad_add_fusion.4.meta, bf16[1,96,32,1024]{3,2,1,0:T(8,128)(2,1)} %gradients.7, bf16[24,8,1024]{2,1,0:T(8,128)(2,1)S(1)} %collective-permute-done.9.one, ...), custom_call_target="tpu_custom_call" | custom-call | tf_op jit(solution)/shard_map/pallas_call | solution.py:117
  81.4 5.7 %collective-permute-done.6.one = bf16[24,8,1024]{2,1,0:T(8,128)(2,1)S(1)} collective-permute-done((bf16[24,8,1024]{2,1,0:T(8,128)(2,1)S(1)}, bf16[24,8,1024]{2,1,0:T(8,128)(2,1)S(1)}, u32[]{:S(2)}, u32[]{:S(2)}) %collective-permute-start.6) | collective-permute-done | bytes 393248 | tf_op jit(solution)/shard_map/ppermute | solution.py:329
  87.1 6.8 %collective-permute-done.8.three = bf16[24,8,1024]{2,1,0:T(8,128)(2,1)S(1)} collective-permute-done((bf16[24,8,1024]{2,1,0:T(8,128)(2,1)S(1)}, bf16[24,8,1024]{2,1,0:T(8,128)(2,1)S(1)}, u32[]{:S(2)}, u32[]{:S(2)}) %collective-permute-start.8) | collective-permute-done | bytes 393248 | tf_op jit(solution)/shard_map/ppermute | solution.py:329
  93.9 4.2 %shard_map.60 = (s16[32,16,1152]{2,1,0:T(8,128)(2,1)}, s16[32,16,1152]{2,1,0:T(8,128)(2,1)}) custom-call(s32[49]{0:T(128)S(1)} %pad_add_fusion.4.meta, bf16[1,96,32,1024]{3,2,1,0:T(8,128)(2,1)} %gradients.7, bf16[24,8,1024]{2,1,0:T(8,128)(2,1)S(1)} %collective-permute-done.6.one, ...), custom_call_target="tpu_custom_call", output_to_operand_aliasing={{0}: (7, {}), {1}: (8, {})} | custom-call | tf_op jit(solution)/shard_map/pallas_call | solution.py:117
  98.0 27.4 %all_to_all.25.refs_1_ = s16[32,16,1152]{2,1,0:T(8,128)(2,1)} all-to-all(s16[32,16,1152]{2,1,0:T(8,128)(2,1)} %get-tuple-element.72), channel_id=1, replica_groups=mesh['groups'=4,'shard'=32] {'shard'}, dimensions={0} | all-to-all | bytes 2359296 | tf_op jit(solution)/shard_map/all_to_all | solution.py:353
  125.4 4.0 %all-to-all-start.3 = ((s16[32,16,1152]{2,1,0:T(8,128)(2,1)}), s16[32,16,1152]{2,1,0:T(8,128)(2,1)S(1)}, u32[]{:S(2)}, u32[]{:S(2)}) async-start(s16[32,16,1152]{2,1,0:T(8,128)(2,1)} %get-tuple-element.77), calls=%async_computation.3 | async-start | bytes 2359296 | tf_op jit(solution)/shard_map/all_to_all | solution.py:353
  130.7 12.4 %shard_map.61 = bf16[1024,1024]{1,0:T(8,128)(2,1)} custom-call(bf16[1,1,2,2,1024,1024]{5,4,3,2,1,0:T(8,128)(2,1)} %all_roots.3, s16[32,2,16,1152]{3,2,1,0:T(8,128)(2,1)S(1)} %all-to-all-done.refs_0_, s16[32,16,1152]{2,1,0:T(8,128)(2,1)S(1)} %copy-done), custom_call_target="tpu_custom_call" | custom-call | tf_op jit(solution)/shard_map/pallas_call | solution.py:186
  143.1 4.8 %all-to-all-done.3.refs_1_ = s16[32,16,1152]{2,1,0:T(8,128)(2,1)S(1)} async-done(((s16[32,16,1152]{2,1,0:T(8,128)(2,1)}), s16[32,16,1152]{2,1,0:T(8,128)(2,1)S(1)}, u32[]{:S(2)}, u32[]{:S(2)}) %all-to-all-start.3) | async-done | bytes 1179680 | tf_op jit(solution)/shard_map/all_to_all | solution.py:353
  147.9 4.8 %all-to-all-start.2 = ((bf16[32,32,1024]{2,1,0:T(8,128)(2,1)}), bf16[32,32,1024]{2,1,0:T(8,128)(2,1)}, u32[]{:S(2)}, u32[]{:S(2)}) async-start(bf16[32,32,1024]{2,1,0:T(8,128)(2,1)} %bitcast.54), calls=%async_computation.2 | async-start | bytes 4194304 | tf_op jit(solution)/shard_map/all_to_all | solution.py:353
  153.4 12.5 %shard_map.65 = bf16[1024,1024]{1,0:T(8,128)(2,1)} custom-call(bf16[1,1,2,2,1024,1024]{5,4,3,2,1,0:T(8,128)(2,1)} %all_roots.3, s16[32,2,16,1152]{3,2,1,0:T(8,128)(2,1)S(1)} %all-to-all-done.refs_0_, s16[32,16,1152]{2,1,0:T(8,128)(2,1)S(1)} %all-to-all-done.3.refs_1_), custom_call_target="tpu_custom_call" | custom-call | tf_op jit(solution)/shard_map/pallas_call | solution.py:186
  165.8 15.0 %all-to-all-done.2.back = bf16[32,32,1024]{2,1,0:T(8,128)(2,1)} async-done(((bf16[32,32,1024]{2,1,0:T(8,128)(2,1)}), bf16[32,32,1024]{2,1,0:T(8,128)(2,1)}, u32[]{:S(2)}, u32[]{:S(2)}) %all-to-all-start.2) | async-done | bytes 2097184 | tf_op jit(solution)/shard_map/all_to_all | solution.py:353
  180.8 5.2 %all-to-all-start.4 = ((bf16[32,32,1024]{2,1,0:T(8,128)(2,1)}), bf16[32,32,1024]{2,1,0:T(8,128)(2,1)}, u32[]{:S(2)}, u32[]{:S(2)}) async-start(bf16[32,32,1024]{2,1,0:T(8,128)(2,1)} %bitcast.53), calls=%async_computation.4 | async-start | bytes 4194304 | tf_op jit(solution)/shard_map/all_to_all | solution.py:353
  192.4 2.7 %collective-permute-start.15 = (bf16[6,32,1024]{2,1,0:T(8,128)(2,1)S(1)}, bf16[6,32,1024]{2,1,0:T(8,128)(2,1)S(1)}, u32[]{:S(2)}, u32[]{:S(2)}) collective-permute-start(bf16[6,32,1024]{2,1,0:T(8,128)(2,1)S(1)} %get-tuple-element.74.refs_1_), channel_id=1, source_target_pairs={{0,96},{32,0},{64,32},{96,64},{1,97},{33,1},{65,33},{97,65},{2,98}... | collective-permute-start | bytes 1179656 | tf_op jit(solution)/shard_map/ppermute | solution.py:384
  195.1 2.7 %collective-permute-start.14 = (bf16[6,32,1024]{2,1,0:T(8,128)(2,1)S(1)}, bf16[6,32,1024]{2,1,0:T(8,128)(2,1)}, u32[]{:S(2)}, u32[]{:S(2)}) collective-permute-start(bf16[6,32,1024]{2,1,0:T(8,128)(2,1)S(1)} %get-tuple-element.73.refs_0_), channel_id=1, source_target_pairs={{0,96},{32,0},{64,32},{96,64},{1,97},{33,1},{65,33},{97,65},{2,98}... | collective-permute-start | bytes 1179656 | tf_op jit(solution)/shard_map/ppermute | solution.py:386
  197.8 6.2 %collective-permute-done.12.refs_2_.refs_1_ = bf16[6,32,1024]{2,1,0:T(8,128)(2,1)S(1)} collective-permute-done((bf16[6,32,1024]{2,1,0:T(8,128)(2,1)S(1)}, bf16[6,32,1024]{2,1,0:T(8,128)(2,1)S(1)}, u32[]{:S(2)}, u32[]{:S(2)}) %collective-permute-start.12) | collective-permute-done | bytes 393248 | tf_op jit(solution)/shard_map/ppermute | solution.py:383
  208.7 5.8 %all-to-all-done.4.back = bf16[32,32,1024]{2,1,0:T(8,128)(2,1)} async-done(((bf16[32,32,1024]{2,1,0:T(8,128)(2,1)}), bf16[32,32,1024]{2,1,0:T(8,128)(2,1)}, u32[]{:S(2)}, u32[]{:S(2)}) %all-to-all-start.4) | async-done | bytes 2097184 | tf_op jit(solution)/shard_map/all_to_all | solution.py:353
  216.5 2.6 %shard_map.67 = (bf16[6,32,1024]{2,1,0:T(8,128)(2,1)S(1)}, bf16[6,32,1024]{2,1,0:T(8,128)(2,1)S(1)}) custom-call(s32[24]{0:T(128)S(1)} %shard_map.64.table, bf16[24,32,1024]{2,1,0:T(8,128)(2,1)S(1)} %shard_map.56.weights, bf16[32,32,1024]{2,1,0:T(8,128)(2,1)} %all-to-all-done.4.back, bf16[6,32,1024]{2,1,0:T(8,128)(2,1)S(1)} %copy-done.2, ...), custom_call_target="tpu_custom_call" | custom-call | tf_op jit(solution)/shard_map/pallas_call | solution.py:249
  219.1 2.7 %collective-permute-start.21 = (bf16[6,32,1024]{2,1,0:T(8,128)(2,1)S(1)}, bf16[6,32,1024]{2,1,0:T(8,128)(2,1)S(1)}, u32[]{:S(2)}, u32[]{:S(2)}) collective-permute-start(bf16[6,32,1024]{2,1,0:T(8,128)(2,1)S(1)} %get-tuple-element.82.refs_1_), channel_id=1, source_target_pairs={{0,96},{32,0},{64,32},{96,64},{1,97},{33,1},{65,33},{97,65},{2,98}... | collective-permute-start | bytes 1179656 | tf_op jit(solution)/shard_map/ppermute | solution.py:384
  224.6 5.6 %collective-permute-done.18.refs_2_ = bf16[6,32,1024]{2,1,0:T(8,128)(2,1)S(1)} collective-permute-done((bf16[6,32,1024]{2,1,0:T(8,128)(2,1)S(1)}, bf16[6,32,1024]{2,1,0:T(8,128)(2,1)S(1)}, u32[]{:S(2)}, u32[]{:S(2)}) %collective-permute-start.18) | collective-permute-done | bytes 393248 | tf_op jit(solution)/shard_map/ppermute | solution.py:383
  230.2 2.7 %collective-permute-start.23 = (bf16[6,32,1024]{2,1,0:T(8,128)(2,1)S(1)}, bf16[6,32,1024]{2,1,0:T(8,128)(2,1)S(1)}, u32[]{:S(2)}, u32[]{:S(2)}) collective-permute-start(bf16[6,32,1024]{2,1,0:T(8,128)(2,1)S(1)} %collective-permute-done.21.refs_5_), channel_id=1, source_target_pairs={{0,96},{32,0},{64,32},{96,64},{1,97},{33,1},{65,33},{97,65},{2,98}... | collective-permute-start | bytes 1179656 | tf_op jit(solution)/shard_map/ppermute | solution.py:388
  232.9 4.7 %collective-permute-done.17.refs_7_ = bf16[6,32,1024]{2,1,0:T(8,128)(2,1)S(1)} collective-permute-done((bf16[6,32,1024]{2,1,0:T(8,128)(2,1)S(1)}, bf16[6,32,1024]{2,1,0:T(8,128)(2,1)S(1)}, u32[]{:S(2)}, u32[]{:S(2)}) %collective-permute-start.17) | collective-permute-done | bytes 393248 | tf_op jit(solution)/shard_map/ppermute | solution.py:388
  237.6 3.2 %shard_map.63.base = bf16[96,32,1024]{2,1,0:T(8,128)(2,1)} custom-call(s32[48]{0:T(128)S(1)} %get-tuple-element.46.place, bf16[6,32,1024]{2,1,0:T(8,128)(2,1)S(1)} %get-tuple-element.73.refs_0_, bf16[6,32,1024]{2,1,0:T(8,128)(2,1)S(1)} %get-tuple-element.74.refs_1_, bf16[6,32,1024]{2,1,0:T(8,128)(2,1)S(1)} %collective-permute-done.12.refs_2_.refs_1_, ...), custom_call_target="tpu_custom_call" | custom-call | tf_op jit(solution)/shard_map/pallas_call | solution.py:296
  240.8 5.2 %collective-permute-done.20.refs_4_ = bf16[6,32,1024]{2,1,0:T(8,128)(2,1)S(1)} collective-permute-done((bf16[6,32,1024]{2,1,0:T(8,128)(2,1)S(1)}, bf16[6,32,1024]{2,1,0:T(8,128)(2,1)S(1)}, u32[]{:S(2)}, u32[]{:S(2)}) %collective-permute-start.20) | collective-permute-done | bytes 393248 | tf_op jit(solution)/shard_map/ppermute | solution.py:386
  248.3 6.2 %collective-permute-done.23.refs_1_ = bf16[6,32,1024]{2,1,0:T(8,128)(2,1)S(1)} collective-permute-done((bf16[6,32,1024]{2,1,0:T(8,128)(2,1)S(1)}, bf16[6,32,1024]{2,1,0:T(8,128)(2,1)S(1)}, u32[]{:S(2)}, u32[]{:S(2)}) %collective-permute-start.23) | collective-permute-done | bytes 393248 | tf_op jit(solution)/shard_map/ppermute | solution.py:388
  (76 shorter events, 49.3 us)
Async XLA Ops:
  0.0 15.7 %copy-start.5 = (s32[96]{0:T(128)S(1)}, s32[96]{0:T(128)}, u32[]{:S(2)}) copy-start(s32[96]{0:T(128)} %param.8) | copy-start | bytes 1156
  2.1 11.7 %collective-permute-start.3 = (bf16[24,8,1024]{2,1,0:T(8,128)(2,1)S(1)}, bf16[24,8,1024]{2,1,0:T(8,128)(2,1)S(1)}, u32[]{:S(2)}, u32[]{:S(2)}) collective-permute-start(bf16[24,8,1024]{2,1,0:T(8,128)(2,1)S(1)} %get-tuple-element.53), channel_id=1, source_target_pairs={{0,32},{32,64},{64,96},{96,0},{1,33},{33,65},{65,97},{97,1},{2,34}... | collective-permute-start | bytes 1179656 | tf_op jit(solution)/shard_map/ppermute | solution.py:329
  4.1 11.9 %collective-permute-start.4 = (bf16[24,8,1024]{2,1,0:T(8,128)(2,1)}, bf16[24,8,1024]{2,1,0:T(8,128)(2,1)S(1)}, u32[]{:S(2)}, u32[]{:S(2)}) collective-permute-start(bf16[24,8,1024]{2,1,0:T(8,128)(2,1)} %get-tuple-element.54), channel_id=1, source_target_pairs={{0,96},{32,0},{64,32},{96,64},{1,97},{33,1},{65,33},{97,65},{2,98}... | collective-permute-start | bytes 1179656 | tf_op jit(solution)/shard_map/ppermute | solution.py:329
  5.4 18.2 %collective-permute-start.5 = (bf16[24,8,1024]{2,1,0:T(8,128)(2,1)S(1)}, bf16[24,8,1024]{2,1,0:T(8,128)(2,1)S(1)}, u32[]{:S(2)}, u32[]{:S(2)}) collective-permute-start(bf16[24,8,1024]{2,1,0:T(8,128)(2,1)S(1)} %get-tuple-element.55), channel_id=1, source_target_pairs={{0,64},{32,96},{64,0},{96,32},{1,65},{33,97},{65,1},{97,33},{2,66}... | collective-permute-start | bytes 1179656 | tf_op jit(solution)/shard_map/ppermute | solution.py:329
  9.2 21.5 %collective-permute-start = (bf16[24,8,1024]{2,1,0:T(8,128)(2,1)}, bf16[24,8,1024]{2,1,0:T(8,128)(2,1)S(1)}, u32[]{:S(2)}, u32[]{:S(2)}) collective-permute-start(bf16[24,8,1024]{2,1,0:T(8,128)(2,1)} %get-tuple-element.50), channel_id=1, source_target_pairs={{0,32},{32,64},{64,96},{96,0},{1,33},{33,65},{65,97},{97,1},{2,34}... | collective-permute-start | bytes 1179656 | tf_op jit(solution)/shard_map/ppermute | solution.py:329
  9.5 21.5 %collective-permute-start.1 = (bf16[24,8,1024]{2,1,0:T(8,128)(2,1)S(1)}, bf16[24,8,1024]{2,1,0:T(8,128)(2,1)S(1)}, u32[]{:S(2)}, u32[]{:S(2)}) collective-permute-start(bf16[24,8,1024]{2,1,0:T(8,128)(2,1)S(1)} %get-tuple-element.51), channel_id=1, source_target_pairs={{0,96},{32,0},{64,32},{96,64},{1,97},{33,1},{65,33},{97,65},{2,98}... | collective-permute-start | bytes 1179656 | tf_op jit(solution)/shard_map/ppermute | solution.py:329
  13.8 26.6 %collective-permute-start.2 = (bf16[24,8,1024]{2,1,0:T(8,128)(2,1)S(1)}, bf16[24,8,1024]{2,1,0:T(8,128)(2,1)S(1)}, u32[]{:S(2)}, u32[]{:S(2)}) collective-permute-start(bf16[24,8,1024]{2,1,0:T(8,128)(2,1)S(1)} %get-tuple-element.52), channel_id=1, source_target_pairs={{0,64},{32,96},{64,0},{96,32},{1,65},{33,97},{65,1},{97,33},{2,66}... | collective-permute-start | bytes 1179656 | tf_op jit(solution)/shard_map/ppermute | solution.py:329
  44.0 54.1 %all-to-all-start = ((s16[32,2,16,1152]{3,2,1,0:T(8,128)(2,1)}), s16[32,2,16,1152]{3,2,1,0:T(8,128)(2,1)S(1)}, u32[]{:S(2)}, u32[]{:S(2)}) async-start(s16[32,2,16,1152]{3,2,1,0:T(8,128)(2,1)} %get-tuple-element.58), calls=%async_computation | async-start | bytes 4718592 | tf_op jit(solution)/shard_map/all_to_all | solution.py:353
  54.9 10.5 %collective-permute-start.10 = (bf16[24,8,1024]{2,1,0:T(8,128)(2,1)S(1)}, bf16[24,8,1024]{2,1,0:T(8,128)(2,1)S(1)}, u32[]{:S(2)}, u32[]{:S(2)}) collective-permute-start(bf16[24,8,1024]{2,1,0:T(8,128)(2,1)S(1)} %get-tuple-element.65), channel_id=1, source_target_pairs={{0,96},{32,0},{64,32},{96,64},{1,97},{33,1},{65,33},{97,65},{2,98}... | collective-permute-start | bytes 1179656 | tf_op jit(solution)/shard_map/ppermute | solution.py:329
  56.9 11.7 %collective-permute-start.11 = (bf16[24,8,1024]{2,1,0:T(8,128)(2,1)S(1)}, bf16[24,8,1024]{2,1,0:T(8,128)(2,1)S(1)}, u32[]{:S(2)}, u32[]{:S(2)}) collective-permute-start(bf16[24,8,1024]{2,1,0:T(8,128)(2,1)S(1)} %get-tuple-element.66), channel_id=1, source_target_pairs={{0,64},{32,96},{64,0},{96,32},{1,65},{33,97},{65,1},{97,33},{2,66}... | collective-permute-start | bytes 1179656 | tf_op jit(solution)/shard_map/ppermute | solution.py:329
  57.9 20.0 %collective-permute-start.9 = (bf16[24,8,1024]{2,1,0:T(8,128)(2,1)S(1)}, bf16[24,8,1024]{2,1,0:T(8,128)(2,1)S(1)}, u32[]{:S(2)}, u32[]{:S(2)}) collective-permute-start(bf16[24,8,1024]{2,1,0:T(8,128)(2,1)S(1)} %get-tuple-element.64), channel_id=1, source_target_pairs={{0,32},{32,64},{64,96},{96,0},{1,33},{33,65},{65,97},{97,1},{2,34}... | collective-permute-start | bytes 1179656 | tf_op jit(solution)/shard_map/ppermute | solution.py:329
  59.2 27.9 %collective-permute-start.6 = (bf16[24,8,1024]{2,1,0:T(8,128)(2,1)S(1)}, bf16[24,8,1024]{2,1,0:T(8,128)(2,1)S(1)}, u32[]{:S(2)}, u32[]{:S(2)}) collective-permute-start(bf16[24,8,1024]{2,1,0:T(8,128)(2,1)S(1)} %get-tuple-element.61), channel_id=1, source_target_pairs={{0,32},{32,64},{64,96},{96,0},{1,33},{33,65},{65,97},{97,1},{2,34}... | collective-permute-start | bytes 1179656 | tf_op jit(solution)/shard_map/ppermute | solution.py:329
  60.9 26.2 %collective-permute-start.7 = (bf16[24,8,1024]{2,1,0:T(8,128)(2,1)S(1)}, bf16[24,8,1024]{2,1,0:T(8,128)(2,1)S(1)}, u32[]{:S(2)}, u32[]{:S(2)}) collective-permute-start(bf16[24,8,1024]{2,1,0:T(8,128)(2,1)S(1)} %get-tuple-element.62), channel_id=1, source_target_pairs={{0,96},{32,0},{64,32},{96,64},{1,97},{33,1},{65,33},{97,65},{2,98}... | collective-permute-start | bytes 1179656 | tf_op jit(solution)/shard_map/ppermute | solution.py:329
  65.5 28.4 %collective-permute-start.8 = (bf16[24,8,1024]{2,1,0:T(8,128)(2,1)S(1)}, bf16[24,8,1024]{2,1,0:T(8,128)(2,1)S(1)}, u32[]{:S(2)}, u32[]{:S(2)}) collective-permute-start(bf16[24,8,1024]{2,1,0:T(8,128)(2,1)S(1)} %get-tuple-element.63), channel_id=1, source_target_pairs={{0,64},{32,96},{64,0},{96,32},{1,65},{33,97},{65,1},{97,33},{2,66}... | collective-permute-start | bytes 1179656 | tf_op jit(solution)/shard_map/ppermute | solution.py:329
  125.4 22.4 %all-to-all-start.3 = ((s16[32,16,1152]{2,1,0:T(8,128)(2,1)}), s16[32,16,1152]{2,1,0:T(8,128)(2,1)S(1)}, u32[]{:S(2)}, u32[]{:S(2)}) async-start(s16[32,16,1152]{2,1,0:T(8,128)(2,1)} %get-tuple-element.77), calls=%async_computation.3 | async-start | bytes 2359296 | tf_op jit(solution)/shard_map/all_to_all | solution.py:353
  129.4 1.3 copy-start
  147.9 32.9 %all-to-all-start.2 = ((bf16[32,32,1024]{2,1,0:T(8,128)(2,1)}), bf16[32,32,1024]{2,1,0:T(8,128)(2,1)}, u32[]{:S(2)}, u32[]{:S(2)}) async-start(bf16[32,32,1024]{2,1,0:T(8,128)(2,1)} %bitcast.54), calls=%async_computation.2 | async-start | bytes 4194304 | tf_op jit(solution)/shard_map/all_to_all | solution.py:353
  180.8 33.6 %all-to-all-start.4 = ((bf16[32,32,1024]{2,1,0:T(8,128)(2,1)}), bf16[32,32,1024]{2,1,0:T(8,128)(2,1)}, u32[]{:S(2)}, u32[]{:S(2)}) async-start(bf16[32,32,1024]{2,1,0:T(8,128)(2,1)} %bitcast.53), calls=%async_computation.4 | async-start | bytes 4194304 | tf_op jit(solution)/shard_map/all_to_all | solution.py:353
  192.3 11.6 %collective-permute-start.12 = (bf16[6,32,1024]{2,1,0:T(8,128)(2,1)S(1)}, bf16[6,32,1024]{2,1,0:T(8,128)(2,1)S(1)}, u32[]{:S(2)}, u32[]{:S(2)}) collective-permute-start(bf16[6,32,1024]{2,1,0:T(8,128)(2,1)S(1)} %get-tuple-element.73.refs_0_), channel_id=1, source_target_pairs={{0,32},{32,64},{64,96},{96,0},{1,33},{33,65},{65,97},{97,1},{2,34}... | collective-permute-start | bytes 1179656 | tf_op jit(solution)/shard_map/ppermute | solution.py:383
  192.4 11.6 %collective-permute-start.15 = (bf16[6,32,1024]{2,1,0:T(8,128)(2,1)S(1)}, bf16[6,32,1024]{2,1,0:T(8,128)(2,1)S(1)}, u32[]{:S(2)}, u32[]{:S(2)}) collective-permute-start(bf16[6,32,1024]{2,1,0:T(8,128)(2,1)S(1)} %get-tuple-element.74.refs_1_), channel_id=1, source_target_pairs={{0,96},{32,0},{64,32},{96,64},{1,97},{33,1},{65,33},{97,65},{2,98}... | collective-permute-start | bytes 1179656 | tf_op jit(solution)/shard_map/ppermute | solution.py:384
  195.1 26.7 %collective-permute-start.13 = (bf16[6,32,1024]{2,1,0:T(8,128)(2,1)S(1)}, bf16[6,32,1024]{2,1,0:T(8,128)(2,1)S(1)}, u32[]{:S(2)}, u32[]{:S(2)}) collective-permute-start(bf16[6,32,1024]{2,1,0:T(8,128)(2,1)S(1)} %get-tuple-element.74.refs_1_), channel_id=1, source_target_pairs={{0,32},{32,64},{64,96},{96,0},{1,33},{33,65},{65,97},{97,1},{2,34}... | collective-permute-start | bytes 1179656 | tf_op jit(solution)/shard_map/ppermute | solution.py:385
  195.1 26.8 %collective-permute-start.14 = (bf16[6,32,1024]{2,1,0:T(8,128)(2,1)S(1)}, bf16[6,32,1024]{2,1,0:T(8,128)(2,1)}, u32[]{:S(2)}, u32[]{:S(2)}) collective-permute-start(bf16[6,32,1024]{2,1,0:T(8,128)(2,1)S(1)} %get-tuple-element.73.refs_0_), channel_id=1, source_target_pairs={{0,96},{32,0},{64,32},{96,64},{1,97},{33,1},{65,33},{97,65},{2,98}... | collective-permute-start | bytes 1179656 | tf_op jit(solution)/shard_map/ppermute | solution.py:386
  204.0 19.3 %collective-permute-start.16 = (bf16[6,32,1024]{2,1,0:T(8,128)(2,1)S(1)}, bf16[6,32,1024]{2,1,0:T(8,128)(2,1)}, u32[]{:S(2)}, u32[]{:S(2)}) collective-permute-start(bf16[6,32,1024]{2,1,0:T(8,128)(2,1)S(1)} %collective-permute-done.12.refs_2_.refs_1_), channel_id=1, source_target_pairs={{0,32},{32,64},{64,96},{96,0},{1,33},{33,65},{65,97},{97,1},{2,34}... | collective-permute-start | bytes 1179656 | tf_op jit(solution)/shard_map/ppermute | solution.py:387
  214.5 1.0 copy-start.2
  215.5 1.0 copy-start.4
  219.1 11.1 %collective-permute-start.18 = (bf16[6,32,1024]{2,1,0:T(8,128)(2,1)S(1)}, bf16[6,32,1024]{2,1,0:T(8,128)(2,1)S(1)}, u32[]{:S(2)}, u32[]{:S(2)}) collective-permute-start(bf16[6,32,1024]{2,1,0:T(8,128)(2,1)S(1)} %get-tuple-element.81.refs_0_), channel_id=1, source_target_pairs={{0,32},{32,64},{64,96},{96,0},{1,33},{33,65},{65,97},{97,1},{2,34}... | collective-permute-start | bytes 1179656 | tf_op jit(solution)/shard_map/ppermute | solution.py:383
  219.1 11.1 %collective-permute-start.21 = (bf16[6,32,1024]{2,1,0:T(8,128)(2,1)S(1)}, bf16[6,32,1024]{2,1,0:T(8,128)(2,1)S(1)}, u32[]{:S(2)}, u32[]{:S(2)}) collective-permute-start(bf16[6,32,1024]{2,1,0:T(8,128)(2,1)S(1)} %get-tuple-element.82.refs_1_), channel_id=1, source_target_pairs={{0,96},{32,0},{64,32},{96,64},{1,97},{33,1},{65,33},{97,65},{2,98}... | collective-permute-start | bytes 1179656 | tf_op jit(solution)/shard_map/ppermute | solution.py:384
  221.8 15.8 %collective-permute-start.17 = (bf16[6,32,1024]{2,1,0:T(8,128)(2,1)S(1)}, bf16[6,32,1024]{2,1,0:T(8,128)(2,1)S(1)}, u32[]{:S(2)}, u32[]{:S(2)}) collective-permute-start(bf16[6,32,1024]{2,1,0:T(8,128)(2,1)S(1)} %collective-permute-done.15.refs_5_.refs_2_), channel_id=1, source_target_pairs={{0,96},{32,0},{64,32},{96,64},{1,97},{33,1},{65,33},{97,65},{2,98}... | collective-permute-start | bytes 1179656 | tf_op jit(solution)/shard_map/ppermute | solution.py:388
  221.8 19.0 %collective-permute-start.19 = (bf16[6,32,1024]{2,1,0:T(8,128)(2,1)S(1)}, bf16[6,32,1024]{2,1,0:T(8,128)(2,1)S(1)}, u32[]{:S(2)}, u32[]{:S(2)}) collective-permute-start(bf16[6,32,1024]{2,1,0:T(8,128)(2,1)S(1)} %get-tuple-element.82.refs_1_), channel_id=1, source_target_pairs={{0,32},{32,64},{64,96},{96,0},{1,33},{33,65},{65,97},{97,1},{2,34}... | collective-permute-start | bytes 1179656 | tf_op jit(solution)/shard_map/ppermute | solution.py:385
  223.3 22.7 %collective-permute-start.20 = (bf16[6,32,1024]{2,1,0:T(8,128)(2,1)S(1)}, bf16[6,32,1024]{2,1,0:T(8,128)(2,1)S(1)}, u32[]{:S(2)}, u32[]{:S(2)}) collective-permute-start(bf16[6,32,1024]{2,1,0:T(8,128)(2,1)S(1)} %get-tuple-element.81.refs_0_), channel_id=1, source_target_pairs={{0,96},{32,0},{64,32},{96,64},{1,97},{33,1},{65,33},{97,65},{2,98}... | collective-permute-start | bytes 1179656 | tf_op jit(solution)/shard_map/ppermute | solution.py:386
  230.2 18.1 %collective-permute-start.22 = (bf16[6,32,1024]{2,1,0:T(8,128)(2,1)S(1)}, bf16[6,32,1024]{2,1,0:T(8,128)(2,1)S(1)}, u32[]{:S(2)}, u32[]{:S(2)}) collective-permute-start(bf16[6,32,1024]{2,1,0:T(8,128)(2,1)S(1)} %collective-permute-done.18.refs_2_), channel_id=1, source_target_pairs={{0,32},{32,64},{64,96},{96,0},{1,33},{33,65},{65,97},{97,1},{2,34}... | collective-permute-start | bytes 1179656 | tf_op jit(solution)/shard_map/ppermute | solution.py:387
  230.2 24.3 %collective-permute-start.23 = (bf16[6,32,1024]{2,1,0:T(8,128)(2,1)S(1)}, bf16[6,32,1024]{2,1,0:T(8,128)(2,1)S(1)}, u32[]{:S(2)}, u32[]{:S(2)}) collective-permute-start(bf16[6,32,1024]{2,1,0:T(8,128)(2,1)S(1)} %collective-permute-done.21.refs_5_), channel_id=1, source_target_pairs={{0,96},{32,0},{64,32},{96,64},{1,97},{33,1},{65,33},{97,65},{2,98}... | collective-permute-start | bytes 1179656 | tf_op jit(solution)/shard_map/ppermute | solution.py:388
  (2 other events, 1.5 us)

commit v7 on v6

--- a/solution.py
+++ b/solution.py
@@ -222,8 +222,7 @@
 
 
 def renew_kernel(first, slot, table, weights, back, *refs):
-    outs = refs[-2:]
-    made = refs[:-2]
+    made, outs, sems = refs[:-3], refs[-3:-1], refs[-1]
     half = outs[0].shape[0]
 
     def block(j):
@@ -232,15 +231,30 @@
         scale = lax.rsqrt(jnp.mean(stepped * stepped, axis=1, keepdims=True) + 1e-06)
         outs[j // half][j % half] = (stepped * scale).astype(jnp.bfloat16)
 
-    def keep(j):
-        outs[j // half][j % half] = made[j // half][j % half]
-
+    def kept(j):
+        return pltpu.make_async_copy(made[j // half].at[j % half], outs[j // half].at[j % half], sems.at[j])
+
+    if not made:
+        for j in range(2 * half):
+            block(j)
+        return
     for j in range(2 * half):
-        if not made:
-            block(j)
-            continue
+        pl.when(table[2 * half + j] != slot)(lambda: kept(j).start())
+    for j in range(2 * half):
         pl.when(table[2 * half + j] == slot)(functools.partial(block, j))
-        pl.when(table[2 * half + j] != slot)(functools.partial(keep, j))
+    for j in range(2 * half):
+        pl.when(table[2 * half + j] != slot)(lambda: kept(j).wait())
+
+
+def ahead_kernel(first, table, weights, back, out_a, out_b, some_a, some_b, sems):
+    renew_kernel(first, 0, table, weights, back, some_a, some_b, sems)
+    copies = [
+        pltpu.make_async_copy(x, out, sems.at[n]) for n, (x, out) in enumerate([(some_a, out_a), (some_b, out_b)])
+    ]
+    for c in copies:
+        c.start()
+    for c in copies:
+        c.wait()
 
 
 def renew(table, weights, back, first, slot, made=()):
@@ -249,10 +263,28 @@
     return pl.pallas_call(
         functools.partial(renew_kernel, first, slot),
         out_shape=(half, half),
-        in_specs=[SMEM] + [VMEM] * (2 + len(made)),
+        in_specs=[SMEM, VMEM, VMEM] + [ANY] * len(made),
         out_specs=(VMEM, VMEM),
-        compiler_params=SMALL,
-    )(table, in_vmem(weights), in_vmem(back), *[in_vmem(x) for x in made])
+        scratch_shapes=[pltpu.SemaphoreType.DMA((count,))],
+        compiler_params=SMALL,
+    )(table, in_vmem(weights), in_vmem(back), *[in_hbm(x) for x in made])
+
+
+def renew_ahead(table, weights, back, first):
+    count = table.shape[0] // 2
+    shape = (count // 2,) + weights.shape[1:]
+    return pl.pallas_call(
+        functools.partial(ahead_kernel, first),
+        out_shape=(pltpu.HBM(shape, jnp.bfloat16), pltpu.HBM(shape, jnp.bfloat16)),
+        in_specs=[SMEM, VMEM, VMEM],
+        out_specs=(ANY, ANY),
+        scratch_shapes=[
+            pltpu.VMEM(shape, jnp.bfloat16),
+            pltpu.VMEM(shape, jnp.bfloat16),
+            pltpu.SemaphoreType.DMA((2,)),
+        ],
+        compiler_params=SMALL,
+    )(table, in_vmem(weights), in_vmem(back))
 
 
 def pass_kernel(count, *refs):
@@ -407,7 +439,7 @@
     new = renew(tables[0], ordered, backs[0], 0, 0)
     pieces0 = to_all(new)
     late = pass_tables(tables[1:2], [pieces0[2], pieces0[5]])
-    made = renew(late[0], ordered, backs[0], half, 0)
+    made = renew_ahead(late[0], ordered, backs[0], half)
     new = renew(late[0], ordered, backs[1], half, 1, made)
     pieces1 = to_all(new)
     out = scatter_blocks(tables[2], pieces0, out_shape)

time: 259 us -> 257 us (level)
  local copies, waits for them, and re-layouts: 11.9 us -> 8.38 us
    unnamed x12 -> x4, local copies, waits for them, and re-layouts: 4.76 us -> 1.27 us
    pallas_call x0 -> x1, Pallas kernels: none -> 2.86 us  [renew_ahead(): pl.pallas_call(functools.partial(ahead_kernel, first), out_shape=(pltpu.H...]
    pallas_call x3 -> x2, Pallas kernels: 6.63 us -> 4.86 us  [renew(): pl.pallas_call(functools.partial(renew_kernel, first, slot), out_shape=(h...]
where the time goes in v7:
time: 257 us; the launch traced here: 254 us
  waiting for transfers between devices  103 us (40%)
  Pallas kernels  58.8 us (23%)
  starting transfers between devices  54.3 us (21%)
  blocking collectives  27.4 us (11%)
  local copies, waits for them, and re-layouts  8.38 us (3%)
    ppermute x12, waiting for transfers between devices, body(): lax.ppermute(p, 'groups', shift(n))  49.3 us
    all_to_all x1, blocking collectives, exchange(): return lax.all_to_all(x, 'shard', 0, 0, tiled=True)  27.4 us
    all_to_all x4, waiting for transfers between devices, exchange(): return lax.all_to_all(x, 'shard', 0, 0, tiled=True)  26.1 us
    pallas_call x2, Pallas kernels, owner_work(): pl.pallas_call(functools.partial(owner_kernel, slot), out_shape=pltpu.HBM...  24.9 us
    all_to_all x4, starting transfers between devices, exchange(): return lax.all_to_all(x, 'shard', 0, 0, tiled=True)  23.6 us
    ppermute x12, starting transfers between devices, body(): lax.ppermute(p, 'groups', shift(n))  17.2 us
    pallas_call x4, Pallas kernels, sum_replicas(): pl.pallas_call(functools.partial(sum_kernel, start, offset, before is Non...  14.8 us
    ppermute x2, waiting for transfers between devices, to_all(): prev_a = lax.ppermute(a, 'groups', shift(1))  12.8 us
  transfers between devices with their start and end apart: 28, of which 18 were waited for; matrix products, arithmetic and copies ran while one was open for 3% of the time, Pallas kernels for 21%

profile of v7, /device:TPU:1, one launch (start us, length us, event | category | flops | bytes accessed | tf_op | source)
XLA Modules:
  0.0 254.3 jit_solution(14029098448946719270)
XLA Ops:
  16.0 7.6 %collective-permute-done.5.three = bf16[24,8,1024]{2,1,0:T(8,128)(2,1)S(1)} collective-permute-done((bf16[24,8,1024]{2,1,0:T(8,128)(2,1)S(1)}, bf16[24,8,1024]{2,1,0:T(8,128)(2,1)S(1)}, u32[]{:S(2)}, u32[]{:S(2)}) %collective-permute-start.5) | collective-permute-done | bytes 393248 | tf_op jit(solution)/shard_map/ppermute | solution.py:361
  23.6 3.5 %shard_map.57 = (s16[32,2,16,1152]{3,2,1,0:T(8,128)(2,1)}, f32[24,1,128]{2,1,0:T(1,128)S(1)}) custom-call(s32[49]{0:T(128)S(1)} %pad_add_fusion.4.meta, bf16[1,96,32,1024]{3,2,1,0:T(8,128)(2,1)} %gradients.7, bf16[24,8,1024]{2,1,0:T(8,128)(2,1)S(1)} %collective-permute-done.3.one, bf16[24,8,1024]{2,1,0:T(8,128)(2,1)S(1)} %collective-permute-done.4.two, ...), custom_call_target="tpu_custom_call" | custom-call | tf_op jit(solution)/shard_map/pallas_call | solution.py:117
  27.1 3.6 %collective-permute-done.one = bf16[24,8,1024]{2,1,0:T(8,128)(2,1)S(1)} collective-permute-done((bf16[24,8,1024]{2,1,0:T(8,128)(2,1)}, bf16[24,8,1024]{2,1,0:T(8,128)(2,1)S(1)}, u32[]{:S(2)}, u32[]{:S(2)}) %collective-permute-start) | collective-permute-done | bytes 393248 | tf_op jit(solution)/shard_map/ppermute | solution.py:361
  30.9 9.5 %collective-permute-done.2.three = bf16[24,8,1024]{2,1,0:T(8,128)(2,1)S(1)} collective-permute-done((bf16[24,8,1024]{2,1,0:T(8,128)(2,1)S(1)}, bf16[24,8,1024]{2,1,0:T(8,128)(2,1)S(1)}, u32[]{:S(2)}, u32[]{:S(2)}) %collective-permute-start.2) | collective-permute-done | bytes 393248 | tf_op jit(solution)/shard_map/ppermute | solution.py:361
  40.4 3.5 %shard_map.58 = (s16[32,2,16,1152]{3,2,1,0:T(8,128)(2,1)}, f32[24,1,128]{2,1,0:T(1,128)S(1)}) custom-call(s32[49]{0:T(128)S(1)} %pad_add_fusion.4.meta, bf16[1,96,32,1024]{3,2,1,0:T(8,128)(2,1)} %gradients.7, bf16[24,8,1024]{2,1,0:T(8,128)(2,1)S(1)} %collective-permute-done.one, ...), custom_call_target="tpu_custom_call", output_to_operand_aliasing={{0}: (7, {})} | custom-call | tf_op jit(solution)/shard_map/pallas_call | solution.py:117
  44.0 9.6 %all-to-all-start = ((s16[32,2,16,1152]{3,2,1,0:T(8,128)(2,1)}), s16[32,2,16,1152]{3,2,1,0:T(8,128)(2,1)S(1)}, u32[]{:S(2)}, u32[]{:S(2)}) async-start(s16[32,2,16,1152]{3,2,1,0:T(8,128)(2,1)} %get-tuple-element.58), calls=%async_computation | async-start | bytes 4718592 | tf_op jit(solution)/shard_map/all_to_all | solution.py:385
  62.0 3.4 %collective-permute-done.10.two = bf16[24,8,1024]{2,1,0:T(8,128)(2,1)S(1)} collective-permute-done((bf16[24,8,1024]{2,1,0:T(8,128)(2,1)S(1)}, bf16[24,8,1024]{2,1,0:T(8,128)(2,1)S(1)}, u32[]{:S(2)}, u32[]{:S(2)}) %collective-permute-start.10) | collective-permute-done | bytes 393248 | tf_op jit(solution)/shard_map/ppermute | solution.py:361
  68.6 9.3 %collective-permute-done.9.one = bf16[24,8,1024]{2,1,0:T(8,128)(2,1)S(1)} collective-permute-done((bf16[24,8,1024]{2,1,0:T(8,128)(2,1)S(1)}, bf16[24,8,1024]{2,1,0:T(8,128)(2,1)S(1)}, u32[]{:S(2)}, u32[]{:S(2)}) %collective-permute-start.9) | collective-permute-done | bytes 393248 | tf_op jit(solution)/shard_map/ppermute | solution.py:361
  77.8 3.5 %shard_map.59 = (s16[32,16,1152]{2,1,0:T(8,128)(2,1)}, s16[32,16,1152]{2,1,0:T(8,128)(2,1)}, f32[24,1,128]{2,1,0:T(1,128)S(1)}) custom-call(s32[49]{0:T(128)S(1)} %pad_add_fusion.4.meta, bf16[1,96,32,1024]{3,2,1,0:T(8,128)(2,1)} %gradients.7, bf16[24,8,1024]{2,1,0:T(8,128)(2,1)S(1)} %collective-permute-done.9.one, ...), custom_call_target="tpu_custom_call" | custom-call | tf_op jit(solution)/shard_map/pallas_call | solution.py:117
  81.4 5.7 %collective-permute-done.6.one = bf16[24,8,1024]{2,1,0:T(8,128)(2,1)S(1)} collective-permute-done((bf16[24,8,1024]{2,1,0:T(8,128)(2,1)S(1)}, bf16[24,8,1024]{2,1,0:T(8,128)(2,1)S(1)}, u32[]{:S(2)}, u32[]{:S(2)}) %collective-permute-start.6) | collective-permute-done | bytes 393248 | tf_op jit(solution)/shard_map/ppermute | solution.py:361
  87.1 6.8 %collective-permute-done.8.three = bf16[24,8,1024]{2,1,0:T(8,128)(2,1)S(1)} collective-permute-done((bf16[24,8,1024]{2,1,0:T(8,128)(2,1)S(1)}, bf16[24,8,1024]{2,1,0:T(8,128)(2,1)S(1)}, u32[]{:S(2)}, u32[]{:S(2)}) %collective-permute-start.8) | collective-permute-done | bytes 393248 | tf_op jit(solution)/shard_map/ppermute | solution.py:361
  93.9 4.2 %shard_map.60 = (s16[32,16,1152]{2,1,0:T(8,128)(2,1)}, s16[32,16,1152]{2,1,0:T(8,128)(2,1)}) custom-call(s32[49]{0:T(128)S(1)} %pad_add_fusion.4.meta, bf16[1,96,32,1024]{3,2,1,0:T(8,128)(2,1)} %gradients.7, bf16[24,8,1024]{2,1,0:T(8,128)(2,1)S(1)} %collective-permute-done.6.one, ...), custom_call_target="tpu_custom_call", output_to_operand_aliasing={{0}: (7, {}), {1}: (8, {})} | custom-call | tf_op jit(solution)/shard_map/pallas_call | solution.py:117
  98.0 27.4 %all_to_all.25.refs_1_ = s16[32,16,1152]{2,1,0:T(8,128)(2,1)} all-to-all(s16[32,16,1152]{2,1,0:T(8,128)(2,1)} %get-tuple-element.72), channel_id=1, replica_groups=mesh['groups'=4,'shard'=32] {'shard'}, dimensions={0} | all-to-all | bytes 2359296 | tf_op jit(solution)/shard_map/all_to_all | solution.py:385
  125.4 4.0 %all-to-all-start.3 = ((s16[32,16,1152]{2,1,0:T(8,128)(2,1)}), s16[32,16,1152]{2,1,0:T(8,128)(2,1)S(1)}, u32[]{:S(2)}, u32[]{:S(2)}) async-start(s16[32,16,1152]{2,1,0:T(8,128)(2,1)} %get-tuple-element.77), calls=%async_computation.3 | async-start | bytes 2359296 | tf_op jit(solution)/shard_map/all_to_all | solution.py:385
  130.7 12.4 %shard_map.61 = bf16[1024,1024]{1,0:T(8,128)(2,1)} custom-call(bf16[1,1,2,2,1024,1024]{5,4,3,2,1,0:T(8,128)(2,1)} %all_roots.3, s16[32,2,16,1152]{3,2,1,0:T(8,128)(2,1)S(1)} %all-to-all-done.refs_0_, s16[32,16,1152]{2,1,0:T(8,128)(2,1)S(1)} %copy-done), custom_call_target="tpu_custom_call" | custom-call | tf_op jit(solution)/shard_map/pallas_call | solution.py:186
  143.1 4.8 %all-to-all-done.3.refs_1_ = s16[32,16,1152]{2,1,0:T(8,128)(2,1)S(1)} async-done(((s16[32,16,1152]{2,1,0:T(8,128)(2,1)}), s16[32,16,1152]{2,1,0:T(8,128)(2,1)S(1)}, u32[]{:S(2)}, u32[]{:S(2)}) %all-to-all-start.3) | async-done | bytes 1179680 | tf_op jit(solution)/shard_map/all_to_all | solution.py:385
  147.9 4.8 %all-to-all-start.2 = ((bf16[32,32,1024]{2,1,0:T(8,128)(2,1)}), bf16[32,32,1024]{2,1,0:T(8,128)(2,1)}, u32[]{:S(2)}, u32[]{:S(2)}) async-start(bf16[32,32,1024]{2,1,0:T(8,128)(2,1)} %bitcast.54), calls=%async_computation.2 | async-start | bytes 4194304 | tf_op jit(solution)/shard_map/all_to_all | solution.py:385
  153.4 12.5 %shard_map.65 = bf16[1024,1024]{1,0:T(8,128)(2,1)} custom-call(bf16[1,1,2,2,1024,1024]{5,4,3,2,1,0:T(8,128)(2,1)} %all_roots.3, s16[32,2,16,1152]{3,2,1,0:T(8,128)(2,1)S(1)} %all-to-all-done.refs_0_, s16[32,16,1152]{2,1,0:T(8,128)(2,1)S(1)} %all-to-all-done.3.refs_1_), custom_call_target="tpu_custom_call" | custom-call | tf_op jit(solution)/shard_map/pallas_call | solution.py:186
  165.8 15.0 %all-to-all-done.2.back = bf16[32,32,1024]{2,1,0:T(8,128)(2,1)} async-done(((bf16[32,32,1024]{2,1,0:T(8,128)(2,1)}), bf16[32,32,1024]{2,1,0:T(8,128)(2,1)}, u32[]{:S(2)}, u32[]{:S(2)}) %all-to-all-start.2) | async-done | bytes 2097184 | tf_op jit(solution)/shard_map/all_to_all | solution.py:385
  180.8 5.2 %all-to-all-start.4 = ((bf16[32,32,1024]{2,1,0:T(8,128)(2,1)}), bf16[32,32,1024]{2,1,0:T(8,128)(2,1)}, u32[]{:S(2)}, u32[]{:S(2)}) async-start(bf16[32,32,1024]{2,1,0:T(8,128)(2,1)} %bitcast.53), calls=%async_computation.4 | async-start | bytes 4194304 | tf_op jit(solution)/shard_map/all_to_all | solution.py:385
  192.5 2.7 %collective-permute-start.15 = (bf16[6,32,1024]{2,1,0:T(8,128)(2,1)S(1)}, bf16[6,32,1024]{2,1,0:T(8,128)(2,1)S(1)}, u32[]{:S(2)}, u32[]{:S(2)}) collective-permute-start(bf16[6,32,1024]{2,1,0:T(8,128)(2,1)S(1)} %get-tuple-element.74.refs_1_), channel_id=1, source_target_pairs={{0,96},{32,0},{64,32},{96,64},{1,97},{33,1},{65,33},{97,65},{2,98}... | collective-permute-start | bytes 1179656 | tf_op jit(solution)/shard_map/ppermute | solution.py:416
  195.2 2.7 %collective-permute-start.14 = (bf16[6,32,1024]{2,1,0:T(8,128)(2,1)S(1)}, bf16[6,32,1024]{2,1,0:T(8,128)(2,1)}, u32[]{:S(2)}, u32[]{:S(2)}) collective-permute-start(bf16[6,32,1024]{2,1,0:T(8,128)(2,1)S(1)} %get-tuple-element.73.refs_0_), channel_id=1, source_target_pairs={{0,96},{32,0},{64,32},{96,64},{1,97},{33,1},{65,33},{97,65},{2,98}... | collective-permute-start | bytes 1179656 | tf_op jit(solution)/shard_map/ppermute | solution.py:418
  197.9 6.2 %collective-permute-done.12.refs_2_.refs_1_ = bf16[6,32,1024]{2,1,0:T(8,128)(2,1)S(1)} collective-permute-done((bf16[6,32,1024]{2,1,0:T(8,128)(2,1)S(1)}, bf16[6,32,1024]{2,1,0:T(8,128)(2,1)S(1)}, u32[]{:S(2)}, u32[]{:S(2)}) %collective-permute-start.12) | collective-permute-done | bytes 393248 | tf_op jit(solution)/shard_map/ppermute | solution.py:415
  205.2 2.9 %shard_map.66 = (bf16[6,32,1024]{2,1,0:T(8,128)(2,1)}, bf16[6,32,1024]{2,1,0:T(8,128)(2,1)}) custom-call(s32[24]{0:T(128)S(1)} %shard_map.64.table, bf16[24,32,1024]{2,1,0:T(8,128)(2,1)S(1)} %shard_map.56.weights, bf16[32,32,1024]{2,1,0:T(8,128)(2,1)} %all-to-all-done.2.back), custom_call_target="tpu_custom_call" | custom-call | tf_op jit(solution)/shard_map/pallas_call | solution.py:276
  208.1 6.4 %all-to-all-done.4.back = bf16[32,32,1024]{2,1,0:T(8,128)(2,1)} async-done(((bf16[32,32,1024]{2,1,0:T(8,128)(2,1)}), bf16[32,32,1024]{2,1,0:T(8,128)(2,1)}, u32[]{:S(2)}, u32[]{:S(2)}) %all-to-all-start.4) | async-done | bytes 2097184 | tf_op jit(solution)/shard_map/all_to_all | solution.py:385
  214.5 2.7 %shard_map.67 = (bf16[6,32,1024]{2,1,0:T(8,128)(2,1)S(1)}, bf16[6,32,1024]{2,1,0:T(8,128)(2,1)S(1)}) custom-call(s32[24]{0:T(128)S(1)} %shard_map.64.table, bf16[24,32,1024]{2,1,0:T(8,128)(2,1)S(1)} %shard_map.56.weights, bf16[32,32,1024]{2,1,0:T(8,128)(2,1)} %all-to-all-done.4.back, bf16[6,32,1024]{2,1,0:T(8,128)(2,1)} %get-tuple-element.79.refs_0_, ...), custom_call_target="tpu_custom_call" | custom-call | tf_op jit(solution)/shard_map/pallas_call | solution.py:263
  222.7 6.6 %collective-permute-done.18.refs_2_ = bf16[6,32,1024]{2,1,0:T(8,128)(2,1)S(1)} collective-permute-done((bf16[6,32,1024]{2,1,0:T(8,128)(2,1)S(1)}, bf16[6,32,1024]{2,1,0:T(8,128)(2,1)S(1)}, u32[]{:S(2)}, u32[]{:S(2)}) %collective-permute-start.18) | collective-permute-done | bytes 393248 | tf_op jit(solution)/shard_map/ppermute | solution.py:415
  229.4 2.7 %collective-permute-start.23 = (bf16[6,32,1024]{2,1,0:T(8,128)(2,1)S(1)}, bf16[6,32,1024]{2,1,0:T(8,128)(2,1)S(1)}, u32[]{:S(2)}, u32[]{:S(2)}) collective-permute-start(bf16[6,32,1024]{2,1,0:T(8,128)(2,1)S(1)} %collective-permute-done.21.refs_5_), channel_id=1, source_target_pairs={{0,96},{32,0},{64,32},{96,64},{1,97},{33,1},{65,33},{97,65},{2,98}... | collective-permute-start | bytes 1179656 | tf_op jit(solution)/shard_map/ppermute | solution.py:420
  232.0 3.7 %collective-permute-done.17.refs_7_ = bf16[6,32,1024]{2,1,0:T(8,128)(2,1)S(1)} collective-permute-done((bf16[6,32,1024]{2,1,0:T(8,128)(2,1)S(1)}, bf16[6,32,1024]{2,1,0:T(8,128)(2,1)S(1)}, u32[]{:S(2)}, u32[]{:S(2)}) %collective-permute-start.17) | collective-permute-done | bytes 393248 | tf_op jit(solution)/shard_map/ppermute | solution.py:420
  235.8 3.2 %shard_map.63.base = bf16[96,32,1024]{2,1,0:T(8,128)(2,1)} custom-call(s32[48]{0:T(128)S(1)} %get-tuple-element.46.place, bf16[6,32,1024]{2,1,0:T(8,128)(2,1)S(1)} %get-tuple-element.73.refs_0_, bf16[6,32,1024]{2,1,0:T(8,128)(2,1)S(1)} %get-tuple-element.74.refs_1_, bf16[6,32,1024]{2,1,0:T(8,128)(2,1)S(1)} %collective-permute-done.12.refs_2_.refs_1_, ...), custom_call_target="tpu_custom_call" | custom-call | tf_op jit(solution)/shard_map/pallas_call | solution.py:328
  238.9 5.2 %collective-permute-done.20.refs_4_ = bf16[6,32,1024]{2,1,0:T(8,128)(2,1)S(1)} collective-permute-done((bf16[6,32,1024]{2,1,0:T(8,128)(2,1)S(1)}, bf16[6,32,1024]{2,1,0:T(8,128)(2,1)S(1)}, u32[]{:S(2)}, u32[]{:S(2)}) %collective-permute-start.20) | collective-permute-done | bytes 393248 | tf_op jit(solution)/shard_map/ppermute | solution.py:418
  246.4 6.2 %collective-permute-done.23.refs_1_ = bf16[6,32,1024]{2,1,0:T(8,128)(2,1)S(1)} collective-permute-done((bf16[6,32,1024]{2,1,0:T(8,128)(2,1)S(1)}, bf16[6,32,1024]{2,1,0:T(8,128)(2,1)S(1)}, u32[]{:S(2)}, u32[]{:S(2)}) %collective-permute-start.23) | collective-permute-done | bytes 393248 | tf_op jit(solution)/shard_map/ppermute | solution.py:420
  (68 shorter events, 46.6 us)
Async XLA Ops:
  0.0 15.7 %copy-start.1 = (s32[96]{0:T(128)S(1)}, s32[96]{0:T(128)}, u32[]{:S(2)}) copy-start(s32[96]{0:T(128)} %param.8) | copy-start | bytes 1156
  2.1 11.7 %collective-permute-start.3 = (bf16[24,8,1024]{2,1,0:T(8,128)(2,1)S(1)}, bf16[24,8,1024]{2,1,0:T(8,128)(2,1)S(1)}, u32[]{:S(2)}, u32[]{:S(2)}) collective-permute-start(bf16[24,8,1024]{2,1,0:T(8,128)(2,1)S(1)} %get-tuple-element.53), channel_id=1, source_target_pairs={{0,32},{32,64},{64,96},{96,0},{1,33},{33,65},{65,97},{97,1},{2,34}... | collective-permute-start | bytes 1179656 | tf_op jit(solution)/shard_map/ppermute | solution.py:361
  4.1 11.9 %collective-permute-start.4 = (bf16[24,8,1024]{2,1,0:T(8,128)(2,1)}, bf16[24,8,1024]{2,1,0:T(8,128)(2,1)S(1)}, u32[]{:S(2)}, u32[]{:S(2)}) collective-permute-start(bf16[24,8,1024]{2,1,0:T(8,128)(2,1)} %get-tuple-element.54), channel_id=1, source_target_pairs={{0,96},{32,0},{64,32},{96,64},{1,97},{33,1},{65,33},{97,65},{2,98}... | collective-permute-start | bytes 1179656 | tf_op jit(solution)/shard_map/ppermute | solution.py:361
  5.4 18.2 %collective-permute-start.5 = (bf16[24,8,1024]{2,1,0:T(8,128)(2,1)S(1)}, bf16[24,8,1024]{2,1,0:T(8,128)(2,1)S(1)}, u32[]{:S(2)}, u32[]{:S(2)}) collective-permute-start(bf16[24,8,1024]{2,1,0:T(8,128)(2,1)S(1)} %get-tuple-element.55), channel_id=1, source_target_pairs={{0,64},{32,96},{64,0},{96,32},{1,65},{33,97},{65,1},{97,33},{2,66}... | collective-permute-start | bytes 1179656 | tf_op jit(solution)/shard_map/ppermute | solution.py:361
  9.2 21.5 %collective-permute-start = (bf16[24,8,1024]{2,1,0:T(8,128)(2,1)}, bf16[24,8,1024]{2,1,0:T(8,128)(2,1)S(1)}, u32[]{:S(2)}, u32[]{:S(2)}) collective-permute-start(bf16[24,8,1024]{2,1,0:T(8,128)(2,1)} %get-tuple-element.50), channel_id=1, source_target_pairs={{0,32},{32,64},{64,96},{96,0},{1,33},{33,65},{65,97},{97,1},{2,34}... | collective-permute-start | bytes 1179656 | tf_op jit(solution)/shard_map/ppermute | solution.py:361
  9.5 21.5 %collective-permute-start.1 = (bf16[24,8,1024]{2,1,0:T(8,128)(2,1)S(1)}, bf16[24,8,1024]{2,1,0:T(8,128)(2,1)S(1)}, u32[]{:S(2)}, u32[]{:S(2)}) collective-permute-start(bf16[24,8,1024]{2,1,0:T(8,128)(2,1)S(1)} %get-tuple-element.51), channel_id=1, source_target_pairs={{0,96},{32,0},{64,32},{96,64},{1,97},{33,1},{65,33},{97,65},{2,98}... | collective-permute-start | bytes 1179656 | tf_op jit(solution)/shard_map/ppermute | solution.py:361
  13.8 26.6 %collective-permute-start.2 = (bf16[24,8,1024]{2,1,0:T(8,128)(2,1)S(1)}, bf16[24,8,1024]{2,1,0:T(8,128)(2,1)S(1)}, u32[]{:S(2)}, u32[]{:S(2)}) collective-permute-start(bf16[24,8,1024]{2,1,0:T(8,128)(2,1)S(1)} %get-tuple-element.52), channel_id=1, source_target_pairs={{0,64},{32,96},{64,0},{96,32},{1,65},{33,97},{65,1},{97,33},{2,66}... | collective-permute-start | bytes 1179656 | tf_op jit(solution)/shard_map/ppermute | solution.py:361
  44.0 54.1 %all-to-all-start = ((s16[32,2,16,1152]{3,2,1,0:T(8,128)(2,1)}), s16[32,2,16,1152]{3,2,1,0:T(8,128)(2,1)S(1)}, u32[]{:S(2)}, u32[]{:S(2)}) async-start(s16[32,2,16,1152]{3,2,1,0:T(8,128)(2,1)} %get-tuple-element.58), calls=%async_computation | async-start | bytes 4718592 | tf_op jit(solution)/shard_map/all_to_all | solution.py:385
  54.9 10.5 %collective-permute-start.10 = (bf16[24,8,1024]{2,1,0:T(8,128)(2,1)S(1)}, bf16[24,8,1024]{2,1,0:T(8,128)(2,1)S(1)}, u32[]{:S(2)}, u32[]{:S(2)}) collective-permute-start(bf16[24,8,1024]{2,1,0:T(8,128)(2,1)S(1)} %get-tuple-element.65), channel_id=1, source_target_pairs={{0,96},{32,0},{64,32},{96,64},{1,97},{33,1},{65,33},{97,65},{2,98}... | collective-permute-start | bytes 1179656 | tf_op jit(solution)/shard_map/ppermute | solution.py:361
  56.9 11.7 %collective-permute-start.11 = (bf16[24,8,1024]{2,1,0:T(8,128)(2,1)S(1)}, bf16[24,8,1024]{2,1,0:T(8,128)(2,1)S(1)}, u32[]{:S(2)}, u32[]{:S(2)}) collective-permute-start(bf16[24,8,1024]{2,1,0:T(8,128)(2,1)S(1)} %get-tuple-element.66), channel_id=1, source_target_pairs={{0,64},{32,96},{64,0},{96,32},{1,65},{33,97},{65,1},{97,33},{2,66}... | collective-permute-start | bytes 1179656 | tf_op jit(solution)/shard_map/ppermute | solution.py:361
  57.9 20.0 %collective-permute-start.9 = (bf16[24,8,1024]{2,1,0:T(8,128)(2,1)S(1)}, bf16[24,8,1024]{2,1,0:T(8,128)(2,1)S(1)}, u32[]{:S(2)}, u32[]{:S(2)}) collective-permute-start(bf16[24,8,1024]{2,1,0:T(8,128)(2,1)S(1)} %get-tuple-element.64), channel_id=1, source_target_pairs={{0,32},{32,64},{64,96},{96,0},{1,33},{33,65},{65,97},{97,1},{2,34}... | collective-permute-start | bytes 1179656 | tf_op jit(solution)/shard_map/ppermute | solution.py:361
  59.2 27.9 %collective-permute-start.6 = (bf16[24,8,1024]{2,1,0:T(8,128)(2,1)S(1)}, bf16[24,8,1024]{2,1,0:T(8,128)(2,1)S(1)}, u32[]{:S(2)}, u32[]{:S(2)}) collective-permute-start(bf16[24,8,1024]{2,1,0:T(8,128)(2,1)S(1)} %get-tuple-element.61), channel_id=1, source_target_pairs={{0,32},{32,64},{64,96},{96,0},{1,33},{33,65},{65,97},{97,1},{2,34}... | collective-permute-start | bytes 1179656 | tf_op jit(solution)/shard_map/ppermute | solution.py:361
  60.9 26.2 %collective-permute-start.7 = (bf16[24,8,1024]{2,1,0:T(8,128)(2,1)S(1)}, bf16[24,8,1024]{2,1,0:T(8,128)(2,1)S(1)}, u32[]{:S(2)}, u32[]{:S(2)}) collective-permute-start(bf16[24,8,1024]{2,1,0:T(8,128)(2,1)S(1)} %get-tuple-element.62), channel_id=1, source_target_pairs={{0,96},{32,0},{64,32},{96,64},{1,97},{33,1},{65,33},{97,65},{2,98}... | collective-permute-start | bytes 1179656 | tf_op jit(solution)/shard_map/ppermute | solution.py:361
  65.5 28.4 %collective-permute-start.8 = (bf16[24,8,1024]{2,1,0:T(8,128)(2,1)S(1)}, bf16[24,8,1024]{2,1,0:T(8,128)(2,1)S(1)}, u32[]{:S(2)}, u32[]{:S(2)}) collective-permute-start(bf16[24,8,1024]{2,1,0:T(8,128)(2,1)S(1)} %get-tuple-element.63), channel_id=1, source_target_pairs={{0,64},{32,96},{64,0},{96,32},{1,65},{33,97},{65,1},{97,33},{2,66}... | collective-permute-start | bytes 1179656 | tf_op jit(solution)/shard_map/ppermute | solution.py:361
  125.4 22.4 %all-to-all-start.3 = ((s16[32,16,1152]{2,1,0:T(8,128)(2,1)}), s16[32,16,1152]{2,1,0:T(8,128)(2,1)S(1)}, u32[]{:S(2)}, u32[]{:S(2)}) async-start(s16[32,16,1152]{2,1,0:T(8,128)(2,1)} %get-tuple-element.77), calls=%async_computation.3 | async-start | bytes 2359296 | tf_op jit(solution)/shard_map/all_to_all | solution.py:385
  129.4 1.3 copy-start
  147.9 32.9 %all-to-all-start.2 = ((bf16[32,32,1024]{2,1,0:T(8,128)(2,1)}), bf16[32,32,1024]{2,1,0:T(8,128)(2,1)}, u32[]{:S(2)}, u32[]{:S(2)}) async-start(bf16[32,32,1024]{2,1,0:T(8,128)(2,1)} %bitcast.54), calls=%async_computation.2 | async-start | bytes 4194304 | tf_op jit(solution)/shard_map/all_to_all | solution.py:385
  180.8 33.6 %all-to-all-start.4 = ((bf16[32,32,1024]{2,1,0:T(8,128)(2,1)}), bf16[32,32,1024]{2,1,0:T(8,128)(2,1)}, u32[]{:S(2)}, u32[]{:S(2)}) async-start(bf16[32,32,1024]{2,1,0:T(8,128)(2,1)} %bitcast.53), calls=%async_computation.4 | async-start | bytes 4194304 | tf_op jit(solution)/shard_map/all_to_all | solution.py:385
  192.4 11.6 %collective-permute-start.12 = (bf16[6,32,1024]{2,1,0:T(8,128)(2,1)S(1)}, bf16[6,32,1024]{2,1,0:T(8,128)(2,1)S(1)}, u32[]{:S(2)}, u32[]{:S(2)}) collective-permute-start(bf16[6,32,1024]{2,1,0:T(8,128)(2,1)S(1)} %get-tuple-element.73.refs_0_), channel_id=1, source_target_pairs={{0,32},{32,64},{64,96},{96,0},{1,33},{33,65},{65,97},{97,1},{2,34}... | collective-permute-start | bytes 1179656 | tf_op jit(solution)/shard_map/ppermute | solution.py:415
  192.5 11.6 %collective-permute-start.15 = (bf16[6,32,1024]{2,1,0:T(8,128)(2,1)S(1)}, bf16[6,32,1024]{2,1,0:T(8,128)(2,1)S(1)}, u32[]{:S(2)}, u32[]{:S(2)}) collective-permute-start(bf16[6,32,1024]{2,1,0:T(8,128)(2,1)S(1)} %get-tuple-element.74.refs_1_), channel_id=1, source_target_pairs={{0,96},{32,0},{64,32},{96,64},{1,97},{33,1},{65,33},{97,65},{2,98}... | collective-permute-start | bytes 1179656 | tf_op jit(solution)/shard_map/ppermute | solution.py:416
  195.2 24.8 %collective-permute-start.13 = (bf16[6,32,1024]{2,1,0:T(8,128)(2,1)S(1)}, bf16[6,32,1024]{2,1,0:T(8,128)(2,1)S(1)}, u32[]{:S(2)}, u32[]{:S(2)}) collective-permute-start(bf16[6,32,1024]{2,1,0:T(8,128)(2,1)S(1)} %get-tuple-element.74.refs_1_), channel_id=1, source_target_pairs={{0,32},{32,64},{64,96},{96,0},{1,33},{33,65},{65,97},{97,1},{2,34}... | collective-permute-start | bytes 1179656 | tf_op jit(solution)/shard_map/ppermute | solution.py:417
  195.2 24.8 %collective-permute-start.14 = (bf16[6,32,1024]{2,1,0:T(8,128)(2,1)S(1)}, bf16[6,32,1024]{2,1,0:T(8,128)(2,1)}, u32[]{:S(2)}, u32[]{:S(2)}) collective-permute-start(bf16[6,32,1024]{2,1,0:T(8,128)(2,1)S(1)} %get-tuple-element.73.refs_0_), channel_id=1, source_target_pairs={{0,96},{32,0},{64,32},{96,64},{1,97},{33,1},{65,33},{97,65},{2,98}... | collective-permute-start | bytes 1179656 | tf_op jit(solution)/shard_map/ppermute | solution.py:418
  204.1 17.4 %collective-permute-start.16 = (bf16[6,32,1024]{2,1,0:T(8,128)(2,1)S(1)}, bf16[6,32,1024]{2,1,0:T(8,128)(2,1)}, u32[]{:S(2)}, u32[]{:S(2)}) collective-permute-start(bf16[6,32,1024]{2,1,0:T(8,128)(2,1)S(1)} %collective-permute-done.12.refs_2_.refs_1_), channel_id=1, source_target_pairs={{0,32},{32,64},{64,96},{96,0},{1,33},{33,65},{65,97},{97,1},{2,34}... | collective-permute-start | bytes 1179656 | tf_op jit(solution)/shard_map/ppermute | solution.py:419
  217.2 12.1 %collective-permute-start.18 = (bf16[6,32,1024]{2,1,0:T(8,128)(2,1)S(1)}, bf16[6,32,1024]{2,1,0:T(8,128)(2,1)S(1)}, u32[]{:S(2)}, u32[]{:S(2)}) collective-permute-start(bf16[6,32,1024]{2,1,0:T(8,128)(2,1)S(1)} %get-tuple-element.81.refs_0_), channel_id=1, source_target_pairs={{0,32},{32,64},{64,96},{96,0},{1,33},{33,65},{65,97},{97,1},{2,34}... | collective-permute-start | bytes 1179656 | tf_op jit(solution)/shard_map/ppermute | solution.py:415
  217.3 12.1 %collective-permute-start.21 = (bf16[6,32,1024]{2,1,0:T(8,128)(2,1)S(1)}, bf16[6,32,1024]{2,1,0:T(8,128)(2,1)S(1)}, u32[]{:S(2)}, u32[]{:S(2)}) collective-permute-start(bf16[6,32,1024]{2,1,0:T(8,128)(2,1)S(1)} %get-tuple-element.82.refs_1_), channel_id=1, source_target_pairs={{0,96},{32,0},{64,32},{96,64},{1,97},{33,1},{65,33},{97,65},{2,98}... | collective-permute-start | bytes 1179656 | tf_op jit(solution)/shard_map/ppermute | solution.py:416
  220.0 15.8 %collective-permute-start.17 = (bf16[6,32,1024]{2,1,0:T(8,128)(2,1)S(1)}, bf16[6,32,1024]{2,1,0:T(8,128)(2,1)S(1)}, u32[]{:S(2)}, u32[]{:S(2)}) collective-permute-start(bf16[6,32,1024]{2,1,0:T(8,128)(2,1)S(1)} %collective-permute-done.15.refs_5_.refs_2_), channel_id=1, source_target_pairs={{0,96},{32,0},{64,32},{96,64},{1,97},{33,1},{65,33},{97,65},{2,98}... | collective-permute-start | bytes 1179656 | tf_op jit(solution)/shard_map/ppermute | solution.py:420
  220.0 19.0 %collective-permute-start.19 = (bf16[6,32,1024]{2,1,0:T(8,128)(2,1)S(1)}, bf16[6,32,1024]{2,1,0:T(8,128)(2,1)S(1)}, u32[]{:S(2)}, u32[]{:S(2)}) collective-permute-start(bf16[6,32,1024]{2,1,0:T(8,128)(2,1)S(1)} %get-tuple-element.82.refs_1_), channel_id=1, source_target_pairs={{0,32},{32,64},{64,96},{96,0},{1,33},{33,65},{65,97},{97,1},{2,34}... | collective-permute-start | bytes 1179656 | tf_op jit(solution)/shard_map/ppermute | solution.py:417
  221.4 22.7 %collective-permute-start.20 = (bf16[6,32,1024]{2,1,0:T(8,128)(2,1)S(1)}, bf16[6,32,1024]{2,1,0:T(8,128)(2,1)S(1)}, u32[]{:S(2)}, u32[]{:S(2)}) collective-permute-start(bf16[6,32,1024]{2,1,0:T(8,128)(2,1)S(1)} %get-tuple-element.81.refs_0_), channel_id=1, source_target_pairs={{0,96},{32,0},{64,32},{96,64},{1,97},{33,1},{65,33},{97,65},{2,98}... | collective-permute-start | bytes 1179656 | tf_op jit(solution)/shard_map/ppermute | solution.py:418
  229.3 17.1 %collective-permute-start.22 = (bf16[6,32,1024]{2,1,0:T(8,128)(2,1)S(1)}, bf16[6,32,1024]{2,1,0:T(8,128)(2,1)S(1)}, u32[]{:S(2)}, u32[]{:S(2)}) collective-permute-start(bf16[6,32,1024]{2,1,0:T(8,128)(2,1)S(1)} %collective-permute-done.18.refs_2_), channel_id=1, source_target_pairs={{0,32},{32,64},{64,96},{96,0},{1,33},{33,65},{65,97},{97,1},{2,34}... | collective-permute-start | bytes 1179656 | tf_op jit(solution)/shard_map/ppermute | solution.py:419
  229.4 23.2 %collective-permute-start.23 = (bf16[6,32,1024]{2,1,0:T(8,128)(2,1)S(1)}, bf16[6,32,1024]{2,1,0:T(8,128)(2,1)S(1)}, u32[]{:S(2)}, u32[]{:S(2)}) collective-permute-start(bf16[6,32,1024]{2,1,0:T(8,128)(2,1)S(1)} %collective-permute-done.21.refs_5_), channel_id=1, source_target_pairs={{0,96},{32,0},{64,32},{96,64},{1,97},{33,1},{65,33},{97,65},{2,98}... | collective-permute-start | bytes 1179656 | tf_op jit(solution)/shard_map/ppermute | solution.py:420
